TPU v7x, 256 devices: a whole 4x4x8 slice. The times are simulated.
256 devices in a mesh: sub: 64 (over z, y, x_hi), crow: 4 (over x_lo, core).
Axes of the slice: x: 4 (x_hi: 2, x_lo: 2; x = x_hi * 2 + x_lo), y: 4, z: 8, core: 2. Of those that a mesh axis runs over, the one named last changes fastest.
Arguments:
- test_vectors: float32 [64, 48, 3, 512], P('sub', None, None, 'crow'), may hold values from -6 to 6
- ell_values: float32 [64, 9, 27, 512], P('sub', None, None, 'crow'), may hold values from -0.6 to 0.6
- ell_cols: int32 [64, 27, 512], P('sub', None, 'crow'), may hold values from 0 to 511
- ell_count: int32 [64, 512], P('sub', 'crow'), may hold values from 1 to 27
- pivot: float32 [64, 3, 512], P('sub', None, 'crow'), may hold values from 2.5 to 4
- send_rows: int32 [64, 6, 128], P('sub', None, 'crow'), may hold values from 0 to 127
- recv_rows: int32 [64, 6, 128], P('sub', None, 'crow'), may hold values from 0 to 127
- ov_count: int32 [64, 6, 4], P('sub', None, 'crow'), may hold values from 1 to 32, 64 in all within a row
Outputs:
- basis: float32 [64, 48, 3, 512], P('sub', None, None, 'crow')
- coarse: float32 [64, 7, 48, 48], P('sub', None, 'crow')
Inputs may be any that keep to these rules, and one draw needn't show every extreme that they name: `ov_count`: in each pair the live margin rows of the 4 blocks add up to 64; some block of some pair holds exactly 32.
All inputs are finite; a program needn't handle non-finite values.
Results may differ from a plain program's by a relative error of at most 0.0003.
Values sent between devices are 32-bit elements; how exact they have to be, the bound alone decides.
No kernel may reach another device: no remote copies, remote signals or barrier semaphores. Data moves between devices by JAX's collectives and lax.ppermute only.
A program may use at most 64 MiB of HBM per device.

v0:
```python
import jax
import jax.numpy as jnp
from jax import lax
from jax.experimental import pallas as pl
from jax.experimental.pallas import tpu as pltpu
from jax.sharding import PartitionSpec as P

RADIUS = 3
SLOTS = 2 * RADIUS
V = 48
LANES = 128
NB = 27
NC = 4
OVD = 32
SCALE = float(LANES * NC // OVD)
TILES = V // 8

X0 = 0
VAL0 = 3 * V
COL0 = VAL0 + 9 * NB
PIV0 = COL0 + NB
SEND0 = PIV0 + 3
RECV0 = SEND0 + SLOTS
LIVE0 = RECV0 + SLOTS
PACKED = LIVE0 + SLOTS

OFFSETS = [o - RADIUS if o < RADIUS else o - RADIUS + 1 for o in range(SLOTS)]
HIGH = lax.Precision.HIGHEST
F32 = jnp.float32


def vmem():
    return pl.BlockSpec(memory_space=pltpu.VMEM)


def smem():
    return pl.BlockSpec(memory_space=pltpu.SMEM)


def pack_kernel(c_ref, ov_ref, x_ref, val_ref, col_ref, cnt_ref, piv_ref, send_ref, recv_ref, out_ref):
    out_ref[X0 : X0 + 3 * V, :] = x_ref[...]
    count = cnt_ref[...]
    for k in range(NB):
        live = k < count
        for ab in range(9):
            out_ref[VAL0 + ab * NB + k : VAL0 + ab * NB + k + 1, :] = jnp.where(live, val_ref[ab * NB + k], 0.0)
        out_ref[COL0 + k : COL0 + k + 1, :] = col_ref[k].astype(F32)
    for a in range(3):
        out_ref[PIV0 + a : PIV0 + a + 1, :] = piv_ref[a]
    lane = lax.broadcasted_iota(jnp.int32, (1, LANES), 1)
    c = c_ref[0]
    here = (lane // OVD) == c
    for o in range(SLOTS):
        for ref, base in ((send_ref, SEND0), (recv_ref, RECV0)):
            piece = ref[o].astype(F32)
            row = jnp.concatenate([piece] * NC, axis=1)
            out_ref[base + o : base + o + 1, :] = jnp.where(here, row, 0.0)
        alive = here & ((lane % OVD) < ov_ref[o])
        out_ref[LIVE0 + o : LIVE0 + o + 1, :] = jnp.where(alive, 1.0, 0.0).astype(F32)


def wide(row):
    return jnp.broadcast_to(row, (8, LANES))


def lanes_of(block, index):
    return jnp.take_along_axis(block, index, axis=1)


def start_op(pay_ref, src_ref, dst_ref):
    for q in range(NC):
        for a in range(3):
            piv = wide(pay_ref[q, PIV0 + a : PIV0 + a + 1, :])
            for t in range(TILES):
                rows = slice(a * V + 8 * t, a * V + 8 * t + 8)
                dst_ref[q, rows, :] = piv * src_ref[q, rows, :]


def op_piece(pay_ref, src_ref, dst_ref, rc, first, width):
    total = [[dst_ref[rc, a * V + 8 * t : a * V + 8 * t + 8, :] for t in range(TILES)] for a in range(3)]
    for u in range(width):
        k = first + u
        col = wide(pay_ref[rc, pl.ds(COL0 + k, 1), :]).astype(jnp.int32)
        index = col & (LANES - 1)
        which = col >> 7
        is_q = [which == q for q in range(NC - 1)]
        val = [[wide(pay_ref[rc, pl.ds(VAL0 + (3 * a + b) * NB + k, 1), :]) for b in range(3)] for a in range(3)]
        for b in range(3):
            for t in range(TILES):
                got = [lanes_of(src_ref[q, b * V + 8 * t : b * V + 8 * t + 8, :], index) for q in range(NC)]
                pick = got[NC - 1]
                for q in range(NC - 1):
                    pick = jnp.where(is_q[q], got[q], pick)
                for a in range(3):
                    total[a][t] = total[a][t] + val[a][b] * pick
    for a in range(3):
        for t in range(TILES):
            dst_ref[rc, a * V + 8 * t : a * V + 8 * t + 8, :] = total[a][t]


def flat(ref):
    return jnp.concatenate([ref[q, a * V : a * V + V, :] for a in range(3) for q in range(NC)], axis=1)


def gram_to(m_ref, block):
    gram = lax.dot_general(block, block, (((1,), (1,)), ((), ())), precision=HIGH, preferred_element_type=F32)
    row = lax.broadcasted_iota(jnp.int32, (V, 64), 0)
    lane = lax.broadcasted_iota(jnp.int32, (V, 64), 1)
    eye = jnp.where(row == lane, 1.0, 0.0).astype(F32)
    m_ref[...] = jnp.concatenate([eye, gram, jnp.zeros((V, LANES - 64 - V), F32)], axis=1)


CHOL = 4


def factor_piece(m_ref, col_ref, j):
    sub = lax.broadcasted_iota(jnp.int32, (8, LANES), 0)
    m = [m_ref[8 * t : 8 * t + 8, :] for t in range(TILES)]
    cols = []
    for s in range(CHOL):
        index = jnp.full((8, LANES), 64 + s, jnp.int32) + j
        cols.append([lanes_of(m[t], index) for t in range(TILES)])
        for t in range(TILES):
            col_ref[s, 8 * t : 8 * t + 8, :] = cols[s][t]
    for s in range(CHOL):
        row = wide(m_ref[pl.ds(j + s, 1), :])
        head = {n: wide(col_ref[n, pl.ds(j + s, 1), :]) for n in range(s, CHOL)}
        inverse = 1.0 / head[s]
        for t in range(TILES):
            factor = jnp.where(sub + 8 * t > j + s, cols[s][t] * inverse, 0.0)
            m[t] = m[t] - factor * row
            m_ref[8 * t : 8 * t + 8, :] = m[t]
            for n in range(s + 1, CHOL):
                cols[n][t] = cols[n][t] - factor * head[n]
                col_ref[n, 8 * t : 8 * t + 8, :] = cols[n][t]


def inverse_of(m_ref):
    m = m_ref[...]
    row = lax.broadcasted_iota(jnp.int32, (V, LANES), 0)
    lane = lax.broadcasted_iota(jnp.int32, (V, LANES), 1)
    diag = jnp.sum(jnp.where(lane == row + 64, m, 0.0), axis=1, keepdims=True)
    return m[:, :V] / jnp.sqrt(diag)


def solve_to(dst_ref, linv, src_ref):
    out = jnp.dot(linv, flat(src_ref), precision=HIGH, preferred_element_type=F32)
    for a in range(3):
        for q in range(NC):
            at = (a * NC + q) * LANES
            dst_ref[q, a * V : a * V + V, :] = out[:, at : at + LANES]


def rows_of(src_ref, index, tiles):
    lane = lax.broadcasted_iota(jnp.int32, (8, LANES), 1) // OVD
    out = []
    for at in tiles:
        pick = lanes_of(src_ref[NC - 1, at, :], index)
        for q in range(NC - 1):
            pick = jnp.where(lane == q, lanes_of(src_ref[q, at, :], index), pick)
        out.append(pick)
    return out


def index_row(pay_ref, row):
    total = pay_ref[0, pl.ds(row, 1), :]
    for q in range(1, NC):
        total = total + pay_ref[q, pl.ds(row, 1), :]
    return wide(total)


PARTS = 12
WIDTH = NC * NB // PARTS


def main_kernel(c_ref, pay_ref, y2_ref, w_ref, linv_ref, s1_ref, s2_ref, y_ref, z_ref, m_ref, col_ref, g_ref):
    c = c_ref[0]

    def loop(src_ref, dst_ref, chol):
        start_op(pay_ref, src_ref, dst_ref)

        def step(it, carry):
            op_piece(pay_ref, src_ref, dst_ref, it // 3, (it % 3) * WIDTH, WIDTH)
            if chol:
                factor_piece(m_ref, col_ref, it * CHOL)
            return carry

        lax.fori_loop(0, PARTS, step, 0)

    loop(pay_ref, y_ref, False)
    gram_to(m_ref, flat(y_ref))
    loop(y_ref, z_ref, True)
    solve_to(y2_ref, inverse_of(m_ref), z_ref)
    gram_to(m_ref, flat(y2_ref))
    loop(y2_ref, w_ref, True)
    linv = inverse_of(m_ref)
    linv_ref[...] = linv
    first = index_row(pay_ref, SEND0 + c).astype(jnp.int32)
    second = index_row(pay_ref, SEND0 + NC + c // 2).astype(jnp.int32)
    half = (c % 2) * (V // 2)
    tiles = [slice(8 * t, 8 * t + 8) for t in range(3 * TILES)]
    for n, index in enumerate((first, second)):
        for at, piece in zip(tiles, rows_of(w_ref, index, tiles)):
            g_ref[n, at, :] = piece
    both = jnp.concatenate([g_ref[n, a * V : a * V + V, :] for n in range(2) for a in range(3)], axis=1)
    image = jnp.dot(linv, both, precision=HIGH, preferred_element_type=F32)
    for a in range(3):
        s1_ref[a * V : a * V + V, :] = image[:, a * LANES : a * LANES + LANES]
        g_ref[1, a * V : a * V + V, :] = image[:, (3 + a) * LANES : (4 + a) * LANES]
        s2_ref[a * (V // 2) : (a + 1) * (V // 2), :] = g_ref[1, pl.ds(pl.multiple_of(a * V + half, 8), V // 2), :]


def middle_kernel(c_ref, pay_ref, y2_ref, w_ref, linv_ref, basis_ref, mine1_ref, mine2_ref, center_ref, q_ref):
    c = c_ref[0]
    linv = linv_ref[...]
    solve_to(q_ref, linv, y2_ref)
    basis_ref[...] = q_ref[c]
    tiles = [slice(8 * t, 8 * t + 8) for t in range(3 * TILES)]
    for out_ref, slot in ((mine1_ref, c), (mine2_ref, NC + c // 2)):
        index = index_row(pay_ref, RECV0 + slot).astype(jnp.int32)
        live = index_row(pay_ref, LIVE0 + slot)
        for at, piece in zip(tiles, rows_of(q_ref, index, tiles)):
            out_ref[at, :] = piece * live
    image = jnp.dot(linv, flat(w_ref), precision=HIGH, preferred_element_type=F32)
    center_ref[...] = lax.dot_general(
        flat(q_ref), image, (((1,), (1,)), ((), ())), precision=HIGH, preferred_element_type=F32
    )


def coarse_kernel(c_ref, mine1_ref, mine2_ref, got1_ref, got2_ref, own_ref, a_ref, b_ref, d_ref, r_ref):
    c = c_ref[0]

    def side(ref, count):
        return jnp.concatenate([ref[a * count : a * count + count, :] for a in range(3)], axis=1)

    nt = (((1,), (1,)), ((), ()))
    one = lax.dot_general(side(mine1_ref, V), side(got1_ref, V), nt, precision=HIGH, preferred_element_type=F32) * SCALE
    two = lax.dot_general(side(mine2_ref, V), side(got2_ref, V // 2), nt, precision=HIGH, preferred_element_type=F32) * SCALE
    part = V // NC
    for d in range(NC):
        r_ref[d, 0:part, 0:V] = one[d * part : d * part + part, :]
        r_ref[d, 16 : 16 + part, 0 : V // 2] = two[d * part : d * part + part, :]
    own_ref[...] = r_ref[c]
    a_ref[...] = r_ref[c ^ 1]
    b_ref[...] = r_ref[c ^ 2]
    d_ref[...] = r_ref[c ^ 3]


def join_kernel(c_ref, center_ref, own_ref, a_ref, b_ref, d_ref, out_ref, r_ref):
    c = c_ref[0]
    part = V // NC
    for m, ref in enumerate((own_ref, a_ref, b_ref, d_ref)):
        r_ref[m] = ref[...]
    for slot in range(NC):
        out_ref[slot if slot < RADIUS else slot + 1] = r_ref[c ^ slot, 0:part, 0:V]
    for slot in range(NC, SLOTS):
        even = 2 * (slot - NC)
        low = r_ref[c ^ even, 16 : 16 + part, 0 : V // 2]
        high = r_ref[c ^ (even + 1), 16 : 16 + part, 0 : V // 2]
        out_ref[slot + 1] = jnp.concatenate([low, high], axis=1)
    for d in range(NC):
        @pl.when(c == d)
        def _():
            out_ref[RADIUS] = center_ref[d * part : d * part + part, :]


def shards(test_vectors, ell_values, ell_cols, ell_count, pivot, send_rows, recv_rows, ov_count):
    shape = jax.ShapeDtypeStruct
    c = lax.axis_index("crow").astype(jnp.int32).reshape(1)
    x = jnp.transpose(test_vectors[0], (1, 0, 2)).reshape(3 * V, LANES)
    packed = pl.pallas_call(
        pack_kernel,
        out_shape=shape((PACKED, LANES), F32),
        in_specs=[smem(), smem()] + [vmem()] * 7,
        out_specs=vmem(),
    )(
        c,
        ov_count.reshape(SLOTS),
        x,
        ell_values.reshape(9 * NB, 1, LANES),
        ell_cols.reshape(NB, 1, LANES),
        ell_count.reshape(1, LANES),
        pivot.reshape(3, 1, LANES),
        send_rows.reshape(SLOTS, 1, OVD),
        recv_rows.reshape(SLOTS, 1, OVD),
    )
    pay = lax.all_gather(packed, "crow", axis=0)
    block = (NC, 3 * V, LANES)
    y2, w, linv, s1, s2 = pl.pallas_call(
        main_kernel,
        out_shape=(
            shape(block, F32),
            shape(block, F32),
            shape((V, V), F32),
            shape((3 * V, LANES), F32),
            shape((3 * V // 2, LANES), F32),
        ),
        in_specs=[smem(), vmem()],
        out_specs=(vmem(),) * 5,
        scratch_shapes=[
            pltpu.VMEM(block, F32),
            pltpu.VMEM(block, F32),
            pltpu.VMEM((V, LANES), F32),
            pltpu.VMEM((CHOL, V, LANES), F32),
            pltpu.VMEM((2, 3 * V, LANES), F32),
        ],
    )(c, pay)

    size = lax.axis_size("sub")

    def across(piece, slot_of):
        pairs = []
        for j in range(size):
            for n in range(NC):
                i = (j - OFFSETS[slot_of(n)]) % size
                pairs.append((j * NC + n, i * NC + n))
        return lax.ppermute(piece, ("sub", "crow"), pairs)

    got1 = across(s1, lambda n: n)
    got2 = across(s2, lambda n: NC + n // 2)
    basis, mine1, mine2, center = pl.pallas_call(
        middle_kernel,
        out_shape=(
            shape((3 * V, LANES), F32),
            shape((3 * V, LANES), F32),
            shape((3 * V, LANES), F32),
            shape((V, V), F32),
        ),
        in_specs=[smem()] + [vmem()] * 4,
        out_specs=(vmem(),) * 4,
        scratch_shapes=[pltpu.VMEM(block, F32)],
    )(c, pay, y2, w, linv)
    slab = shape((32, LANES), F32)
    own, to1, to2, to3 = pl.pallas_call(
        coarse_kernel,
        out_shape=(slab,) * 4,
        in_specs=[smem()] + [vmem()] * 4,
        out_specs=(vmem(),) * 4,
        scratch_shapes=[pltpu.VMEM((NC, 32, LANES), F32)],
    )(c, mine1, mine2, got1, got2)
    got = [lax.ppermute(t, "crow", [(n, n ^ m) for n in range(NC)]) for m, t in ((1, to1), (2, to2), (3, to3))]
    coarse = pl.pallas_call(
        join_kernel,
        out_shape=shape((2 * RADIUS + 1, V // NC, V), F32),
        in_specs=[smem()] + [vmem()] * 5,
        out_specs=vmem(),
        scratch_shapes=[pltpu.VMEM((NC, 32, LANES), F32)],
    )(c, center, own, *got)
    basis = jnp.transpose(basis.reshape(3, V, LANES), (1, 0, 2))
    return basis[None], coarse[None]


def solution(mesh):
    placed = (
        P("sub", None, None, "crow"),
        P("sub", None, None, "crow"),
        P("sub", None, "crow"),
        P("sub", "crow"),
        P("sub", None, "crow"),
        P("sub", None, "crow"),
        P("sub", None, "crow"),
        P("sub", None, "crow"),
    )
    return jax.shard_map(
        shards,
        mesh=mesh,
        in_specs=placed,
        out_specs=(P("sub", None, None, "crow"), P("sub", None, "crow", None)),
        check_vma=False,
    )
```

profile of v0, /device:TPU:1, one launch (start us, length us, event | category | flops | bytes accessed | tf_op | source)
XLA Modules:
  0.0 76.5 jit_solution(11431592656157867773)
XLA Ops:
  0.6 1.8 %shard_map.95 = f32[435,128]{1,0:T(8,128)} custom-call(s32[1]{0:T(128)} %bitcast.c_ref, s32[6]{0:T(128)} %bitcast.27, f32[144,128]{1,0:T(8,128)} %bitcast.22, f32[243,1,128]{2,1,0:T(1,128)} %bitcast.21, s32[27,1,128]{2,1,0:T(1,128)} %bitcast.23, s32[1,128]{1,0:T(1,128)} %cnt_ref.1, f32[3,1,128]{2,1,0:T(1,128)} %bitcast.26, s32[6,1,32]{2,1,0:T(1,128)} %bitcast.24, ...), custom_call_target="tpu_custom_call" | custom-call | tf_op jit(solution)/shard_map/pallas_call | solution.py:271
  2.5 13.4 %all-gather.1.pay_ref = f32[4,435,128]{2,1,0:T(8,128)} all-gather(f32[1,435,128]{2,1,0:T(8,128)} %bitcast.19), channel_id=2, replica_groups=mesh['sub'=64,'crow'=4] {'crow'}, dimensions={0}, use_global_device_ids=true | all-gather | bytes 1113600 | tf_op jit(solution)/shard_map/all_gather | solution.py:287
  15.9 35.2 %shard_map.96 = (f32[4,144,128]{2,1,0:T(8,128)}, f32[4,144,128]{2,1,0:T(8,128)}, f32[48,48]{1,0:T(8,128)}, f32[144,128]{1,0:T(8,128)}, f32[72,128]{1,0:T(8,128)}) custom-call(s32[1]{0:T(128)} %bitcast.c_ref, f32[4,435,128]{2,1,0:T(8,128)} %all-gather.1.pay_ref), custom_call_target="tpu_custom_call" | custom-call | tf_op jit(solution)/shard_map/pallas_call | solution.py:289
  51.0 1.3 %collective-permute-start = (f32[144,128]{1,0:T(8,128)}, f32[144,128]{1,0:T(8,128)S(1)}, u32[]{:S(2)}, u32[]{:S(2)}) collective-permute-start(f32[144,128]{1,0:T(8,128)} %get-tuple-element.22), channel_id=1, source_target_pairs={{0,12},{1,9},{2,6},{3,255},{4,16},{5,13},{6,10},{7,3},{8,20},{9,17... | collective-permute-start | bytes 221192 | tf_op jit(solution)/shard_map/ppermute | solution.py:317
  52.3 6.7 %collective-permute-start.1 = (f32[72,128]{1,0:T(8,128)}, f32[72,128]{1,0:T(8,128)S(1)}, u32[]{:S(2)}, u32[]{:S(2)}) collective-permute-start(f32[72,128]{1,0:T(8,128)} %get-tuple-element.23), channel_id=1, source_target_pairs={{0,248},{1,249},{2,246},{3,247},{4,252},{5,253},{6,250},{7,251},{8... | collective-permute-start | bytes 110600 | tf_op jit(solution)/shard_map/ppermute | solution.py:317
  59.1 3.1 %shard_map.97 = (f32[144,128]{1,0:T(8,128)}, f32[144,128]{1,0:T(8,128)}, f32[144,128]{1,0:T(8,128)}, f32[48,48]{1,0:T(8,128)}) custom-call(s32[1]{0:T(128)} %bitcast.c_ref, f32[4,435,128]{2,1,0:T(8,128)} %all-gather.1.pay_ref, f32[4,144,128]{2,1,0:T(8,128)} %get-tuple-element.15.y2_ref, f32[4,144,128]{2,1,0:T(8,128)} %get-tuple-element.16.w_ref, ...), custom_call_target="tpu_custom_call" | custom-call | tf_op jit(solution)/shard_map/pallas_call | solution.py:321
  62.2 0.0 collective-permute-done.1.got2_ref
  62.2 0.0 copy-start.1
  62.2 0.0 collective-permute-done.got1_ref
  62.2 0.0 copy-start
  62.2 0.6 copy-done.1
  62.8 0.0 copy-done
  62.9 1.9 %shard_map.98 = (f32[32,128]{1,0:T(8,128)}, f32[32,128]{1,0:T(8,128)}, f32[32,128]{1,0:T(8,128)}, f32[32,128]{1,0:T(8,128)}) custom-call(s32[1]{0:T(128)} %bitcast.c_ref, f32[144,128]{1,0:T(8,128)} %get-tuple-element.20.mine1_ref, f32[144,128]{1,0:T(8,128)} %get-tuple-element.21.mine2_ref, f32[144,128]{1,0:T(8,128)} %copy-done, f32[72,128]{1,0:T(8,128)} %copy-done.1), custom_call_target="tpu_custom_call" | custom-call | tf_op jit(solution)/shard_map/pallas_call | solution.py:334
  64.7 2.2 %collective-permute-start.2 = (f32[32,128]{1,0:T(8,128)}, f32[32,128]{1,0:T(8,128)S(1)}, u32[]{:S(2)}, u32[]{:S(2)}) collective-permute-start(f32[32,128]{1,0:T(8,128)} %get-tuple-element.25), channel_id=1, source_target_pairs={{0,1},{1,0},{2,3},{3,2},{4,5},{5,4},{6,7},{7,6},{8,9},{9,8},{10,11... | collective-permute-start | bytes 49160 | tf_op jit(solution)/shard_map/ppermute | solution.py:341
  66.9 2.4 %collective-permute-start.3 = (f32[32,128]{1,0:T(8,128)}, f32[32,128]{1,0:T(8,128)S(1)}, u32[]{:S(2)}, u32[]{:S(2)}) collective-permute-start(f32[32,128]{1,0:T(8,128)} %get-tuple-element.26), channel_id=1, source_target_pairs={{0,2},{1,3},{2,0},{3,1},{4,6},{5,7},{6,4},{7,5},{8,10},{9,11},{10,... | collective-permute-start | bytes 49160 | tf_op jit(solution)/shard_map/ppermute | solution.py:341
  69.3 0.2 collective-permute-start.4
  69.5 0.0 collective-permute-done.2.a_ref
  69.5 0.0 copy-start.2
  69.5 1.1 %collective-permute-done.3.b_ref = f32[32,128]{1,0:T(8,128)S(1)} collective-permute-done((f32[32,128]{1,0:T(8,128)}, f32[32,128]{1,0:T(8,128)S(1)}, u32[]{:S(2)}, u32[]{:S(2)}) %collective-permute-start.3) | collective-permute-done | bytes 16416 | tf_op jit(solution)/shard_map/ppermute | solution.py:341
  70.6 0.0 copy-start.3
  70.6 2.3 %collective-permute-done.4.d_ref = f32[32,128]{1,0:T(8,128)S(1)} collective-permute-done((f32[32,128]{1,0:T(8,128)}, f32[32,128]{1,0:T(8,128)S(1)}, u32[]{:S(2)}, u32[]{:S(2)}) %collective-permute-start.4) | collective-permute-done | bytes 16416 | tf_op jit(solution)/shard_map/ppermute | solution.py:341
  72.9 0.0 copy-start.4
  73.0 0.0 copy-done.2
  73.0 0.0 copy-done.3
  73.0 0.6 copy-done.4
  73.5 1.5 %shard_map.99 = f32[7,12,48]{2,1,0:T(8,128)} custom-call(s32[1]{0:T(128)} %bitcast.c_ref, f32[48,48]{1,0:T(8,128)} %get-tuple-element.19.center_ref, f32[32,128]{1,0:T(8,128)} %get-tuple-element.24.own_ref, f32[32,128]{1,0:T(8,128)} %copy-done.2, f32[32,128]{1,0:T(8,128)} %copy-done.3, f32[32,128]{1,0:T(8,128)} %copy-done.4), custom_call_target="tpu_custom_call" | custom-call | tf_op jit(solution)/shard_map/pallas_call | solution.py:342
  75.0 1.5 %copy.11 = f32[1,7,12,48]{3,0,2,1:T(1,128)} copy(f32[1,7,12,48]{3,2,1,0:T(8,128)} %bitcast.20) | data formatting | bytes 32256
Async XLA Ops:
  51.0 11.2 %collective-permute-start = (f32[144,128]{1,0:T(8,128)}, f32[144,128]{1,0:T(8,128)S(1)}, u32[]{:S(2)}, u32[]{:S(2)}) collective-permute-start(f32[144,128]{1,0:T(8,128)} %get-tuple-element.22), channel_id=1, source_target_pairs={{0,12},{1,9},{2,6},{3,255},{4,16},{5,13},{6,10},{7,3},{8,20},{9,17... | collective-permute-start | bytes 221192 | tf_op jit(solution)/shard_map/ppermute | solution.py:317
  52.3 9.9 %collective-permute-start.1 = (f32[72,128]{1,0:T(8,128)}, f32[72,128]{1,0:T(8,128)S(1)}, u32[]{:S(2)}, u32[]{:S(2)}) collective-permute-start(f32[72,128]{1,0:T(8,128)} %get-tuple-element.23), channel_id=1, source_target_pairs={{0,248},{1,249},{2,246},{3,247},{4,252},{5,253},{6,250},{7,251},{8... | collective-permute-start | bytes 110600 | tf_op jit(solution)/shard_map/ppermute | solution.py:317
  62.2 0.6 copy-start.1
  62.2 0.6 copy-start
  64.7 4.8 %collective-permute-start.2 = (f32[32,128]{1,0:T(8,128)}, f32[32,128]{1,0:T(8,128)S(1)}, u32[]{:S(2)}, u32[]{:S(2)}) collective-permute-start(f32[32,128]{1,0:T(8,128)} %get-tuple-element.25), channel_id=1, source_target_pairs={{0,1},{1,0},{2,3},{3,2},{4,5},{5,4},{6,7},{7,6},{8,9},{9,8},{10,11... | collective-permute-start | bytes 49160 | tf_op jit(solution)/shard_map/ppermute | solution.py:341
  66.9 3.7 %collective-permute-start.3 = (f32[32,128]{1,0:T(8,128)}, f32[32,128]{1,0:T(8,128)S(1)}, u32[]{:S(2)}, u32[]{:S(2)}) collective-permute-start(f32[32,128]{1,0:T(8,128)} %get-tuple-element.26), channel_id=1, source_target_pairs={{0,2},{1,3},{2,0},{3,1},{4,6},{5,7},{6,4},{7,5},{8,10},{9,11},{10,... | collective-permute-start | bytes 49160 | tf_op jit(solution)/shard_map/ppermute | solution.py:341
  69.3 3.7 %collective-permute-start.4 = (f32[32,128]{1,0:T(8,128)}, f32[32,128]{1,0:T(8,128)S(1)}, u32[]{:S(2)}, u32[]{:S(2)}) collective-permute-start(f32[32,128]{1,0:T(8,128)} %get-tuple-element.27), channel_id=1, source_target_pairs={{0,3},{1,2},{2,1},{3,0},{4,7},{5,6},{6,5},{7,4},{8,11},{9,10},{10,... | collective-permute-start | bytes 49160 | tf_op jit(solution)/shard_map/ppermute | solution.py:341
  69.5 3.5 %copy-start.2 = (f32[32,128]{1,0:T(8,128)}, f32[32,128]{1,0:T(8,128)S(1)}, u32[]{:S(2)}) copy-start(f32[32,128]{1,0:T(8,128)S(1)} %collective-permute-done.2.a_ref) | copy-start | bytes 49156
  70.6 2.4 %copy-start.3 = (f32[32,128]{1,0:T(8,128)}, f32[32,128]{1,0:T(8,128)S(1)}, u32[]{:S(2)}) copy-start(f32[32,128]{1,0:T(8,128)S(1)} %collective-permute-done.3.b_ref) | copy-start | bytes 49156
  72.9 0.6 copy-start.4
where the time goes:
time: 77 us; the launch traced here: 76.5 us
  Pallas kernels  43.5 us (56%)
  blocking collectives  13.4 us (17%)
  starting transfers between devices  12.8 us (17%)
  waiting for transfers between devices  3.46 us (4%)
  local copies, waits for them, and re-layouts  2.71 us (4%)
    pallas_call x1, Pallas kernels, shards(): pl.pallas_call(main_kernel, out_shape=(shape(block, F32), shape(block, F3...  35.2 us
    all_gather x1, blocking collectives, shards(): pay = lax.all_gather(packed, 'crow', axis=0)  13.4 us
    ppermute x2, starting transfers between devices, across(): return lax.ppermute(piece, ('sub', 'crow'), pairs)  8.03 us
    ppermute x3, starting transfers between devices, shards(): lax.ppermute(t, 'crow', [(n, n ^ m) for n in range(NC)])  4.76 us
    ppermute x3, waiting for transfers between devices, shards(): lax.ppermute(t, 'crow', [(n, n ^ m) for n in range(NC)])  3.46 us
    pallas_call x1, Pallas kernels, shards(): pl.pallas_call(middle_kernel, out_shape=(shape((3 * V, LANES), F32), shap...  3.15 us
    unnamed x11, local copies, waits for them, and re-layouts  2.71 us
    pallas_call x1, Pallas kernels, shards(): pl.pallas_call(coarse_kernel, out_shape=(slab,) * 4, in_specs=[smem()] +...  1.85 us
  transfers between devices with their start and end apart: 5, of which 2 were waited for; matrix products, arithmetic and copies ran while one was open for 0% of the time, Pallas kernels for 4%

commit v1 on v0

--- a/solution.py
+++ b/solution.py
@@ -76,26 +76,74 @@
                 dst_ref[q, rows, :] = piv * src_ref[q, rows, :]
 
 
-def op_piece(pay_ref, src_ref, dst_ref, rc, first, width):
-    total = [[dst_ref[rc, a * V + 8 * t : a * V + 8 * t + 8, :] for t in range(TILES)] for a in range(3)]
-    for u in range(width):
-        k = first + u
-        col = wide(pay_ref[rc, pl.ds(COL0 + k, 1), :]).astype(jnp.int32)
-        index = col & (LANES - 1)
-        which = col >> 7
-        is_q = [which == q for q in range(NC - 1)]
-        val = [[wide(pay_ref[rc, pl.ds(VAL0 + (3 * a + b) * NB + k, 1), :]) for b in range(3)] for a in range(3)]
-        for b in range(3):
-            for t in range(TILES):
-                got = [lanes_of(src_ref[q, b * V + 8 * t : b * V + 8 * t + 8, :], index) for q in range(NC)]
-                pick = got[NC - 1]
-                for q in range(NC - 1):
-                    pick = jnp.where(is_q[q], got[q], pick)
-                for a in range(3):
-                    total[a][t] = total[a][t] + val[a][b] * pick
-    for a in range(3):
-        for t in range(TILES):
-            dst_ref[rc, a * V + 8 * t : a * V + 8 * t + 8, :] = total[a][t]
+ONE = 18
+BF16 = jnp.bfloat16
+
+
+def value_row(pay_ref, rc, ab, k):
+    return wide(pay_ref[rc, pl.ds(VAL0 + ab * NB + k, 1), :])
+
+
+def add_block(pay_ref, dst_ref, rc, k, pick_of):
+    val = [[value_row(pay_ref, rc, 3 * a + b, k) for b in range(3)] for a in range(3)]
+    for t in range(TILES):
+        pick = [pick_of(b, t) for b in range(3)]
+        for a in range(3):
+            at = slice(a * V + 8 * t, a * V + 8 * t + 8)
+            dst_ref[rc, at, :] = dst_ref[rc, at, :] + (
+                val[a][0] * pick[0] + val[a][1] * pick[1] + val[a][2] * pick[2]
+            )
+
+
+def lane_block(pay_ref, src_ref, dst_ref, rc, k):
+    col = wide(pay_ref[rc, pl.ds(COL0 + k, 1), :]).astype(jnp.int32)
+    index = col & (LANES - 1)
+    odd = (col & LANES) != 0
+    top = col >= 2 * LANES
+
+    def pick_of(b, t):
+        got = [lanes_of(src_ref[q, b * V + 8 * t : b * V + 8 * t + 8, :], index) for q in range(NC)]
+        return jnp.where(top, jnp.where(odd, got[3], got[2]), jnp.where(odd, got[1], got[0]))
+
+    add_block(pay_ref, dst_ref, rc, k, pick_of)
+
+
+def one_hot(pay_ref, oh_ref, k):
+    half = 2 * LANES
+    place = lax.broadcasted_iota(jnp.int32, (half, half), 0).astype(F32).astype(BF16)
+    for m in range(2):
+        col = jnp.concatenate([pay_ref[2 * m + n, pl.ds(COL0 + k, 1), :] for n in range(2)], axis=1)
+        for h in range(2):
+            local = col - float(h * half)
+            local = jnp.where((local >= 0.0) & (local < float(half)), local, -1.0)
+            target = jnp.concatenate([jnp.broadcast_to(local, (16, half)).astype(BF16)] * (half // 16), axis=0)
+            oh_ref[m, k, h * half : h * half + half, :] = jnp.where(
+                place == target, jnp.ones((), BF16), jnp.zeros((), BF16)
+            )
+
+
+def split_to(x_ref, src_ref):
+    for q in range(NC):
+        at = slice(q * LANES, q * LANES + LANES)
+        value = src_ref[q, 0 : 3 * V, :]
+        high = value.astype(BF16)
+        x_ref[0 : 3 * V, at] = high
+        x_ref[3 * V :, at] = (value - high.astype(F32)).astype(BF16)
+
+
+def issue(x_ref, oh_ref, t_ref, k, parity):
+    for m in range(2):
+        got = jnp.dot(x_ref[...], oh_ref[m, k], preferred_element_type=F32)
+        t_ref[parity, m] = got[: 3 * V, :] + got[3 * V :, :]
+
+
+def take(pay_ref, dst_ref, t_ref, k, parity):
+    for m in range(2):
+        for n in range(2):
+            at = slice(n * LANES, n * LANES + LANES)
+            add_block(
+                pay_ref, dst_ref, 2 * m + n, k, lambda b, t: t_ref[parity, m, b * V + 8 * t : b * V + 8 * t + 8, at]
+            )
 
 
 def flat(ref):
@@ -107,10 +155,11 @@
     row = lax.broadcasted_iota(jnp.int32, (V, 64), 0)
     lane = lax.broadcasted_iota(jnp.int32, (V, 64), 1)
     eye = jnp.where(row == lane, 1.0, 0.0).astype(F32)
-    m_ref[...] = jnp.concatenate([eye, gram, jnp.zeros((V, LANES - 64 - V), F32)], axis=1)
-
-
-CHOL = 4
+    m_ref[:V, :] = jnp.concatenate([eye, gram, jnp.zeros((V, LANES - 64 - V), F32)], axis=1)
+
+
+CHOL = 3
+UN = 6
 
 
 def factor_piece(m_ref, col_ref, j):
@@ -136,7 +185,7 @@
 
 
 def inverse_of(m_ref):
-    m = m_ref[...]
+    m = m_ref[:V, :]
     row = lax.broadcasted_iota(jnp.int32, (V, LANES), 0)
     lane = lax.broadcasted_iota(jnp.int32, (V, LANES), 1)
     diag = jnp.sum(jnp.where(lane == row + 64, m, 0.0), axis=1, keepdims=True)
@@ -169,30 +218,41 @@
     return wide(total)
 
 
-PARTS = 12
-WIDTH = NC * NB // PARTS
-
-
-def main_kernel(c_ref, pay_ref, y2_ref, w_ref, linv_ref, s1_ref, s2_ref, y_ref, z_ref, m_ref, col_ref, g_ref):
+def main_kernel(
+    c_ref, pay_ref, y2_ref, w_ref, linv_ref, s1_ref, s2_ref, y_ref, z_ref, m_ref, col_ref, g_ref, x_ref, oh_ref, t_ref
+):
     c = c_ref[0]
-
-    def loop(src_ref, dst_ref, chol):
+    m_ref[V:, :] = jnp.zeros((8, LANES), F32)
+
+    def loop(src_ref, dst_ref, first):
         start_op(pay_ref, src_ref, dst_ref)
+        split_to(x_ref, src_ref)
+        if first:
+            one_hot(pay_ref, oh_ref, 0)
+            one_hot(pay_ref, oh_ref, 1)
+        issue(x_ref, oh_ref, t_ref, 0, 0)
 
         def step(it, carry):
-            op_piece(pay_ref, src_ref, dst_ref, it // 3, (it % 3) * WIDTH, WIDTH)
-            if chol:
-                factor_piece(m_ref, col_ref, it * CHOL)
+            for u in range(UN):
+                k = UN * it + u
+                issue(x_ref, oh_ref, t_ref, jnp.minimum(k + 1, ONE - 1), (u + 1) % 2)
+                for rc in (2 * (u % 2), 2 * (u % 2) + 1):
+                    lane_block(pay_ref, src_ref, dst_ref, rc, ONE + (UN // 2) * it + u // 2)
+                if first:
+                    one_hot(pay_ref, oh_ref, jnp.minimum(k + 2, ONE - 1))
+                else:
+                    factor_piece(m_ref, col_ref, k * CHOL)
+                take(pay_ref, dst_ref, t_ref, k, u % 2)
             return carry
 
-        lax.fori_loop(0, PARTS, step, 0)
-
-    loop(pay_ref, y_ref, False)
+        lax.fori_loop(0, ONE // UN, step, 0)
+
+    loop(pay_ref, y_ref, True)
     gram_to(m_ref, flat(y_ref))
-    loop(y_ref, z_ref, True)
+    loop(y_ref, z_ref, False)
     solve_to(y2_ref, inverse_of(m_ref), z_ref)
     gram_to(m_ref, flat(y2_ref))
-    loop(y2_ref, w_ref, True)
+    loop(y2_ref, w_ref, False)
     linv = inverse_of(m_ref)
     linv_ref[...] = linv
     first = index_row(pay_ref, SEND0 + c).astype(jnp.int32)
@@ -300,9 +360,12 @@
         scratch_shapes=[
             pltpu.VMEM(block, F32),
             pltpu.VMEM(block, F32),
-            pltpu.VMEM((V, LANES), F32),
-            pltpu.VMEM((CHOL, V, LANES), F32),
+            pltpu.VMEM((V + 8, LANES), F32),
+            pltpu.VMEM((CHOL, V + 8, LANES), F32),
             pltpu.VMEM((2, 3 * V, LANES), F32),
+            pltpu.VMEM((6 * V, NC * LANES), BF16),
+            pltpu.VMEM((2, ONE, NC * LANES, 2 * LANES), BF16),
+            pltpu.VMEM((2, 2, 3 * V, 2 * LANES), F32),
         ],
     )(c, pay)
 

time: 77 us -> 59.9 us (0.78)
  Pallas kernels: 43.5 us -> 26.4 us
    pallas_call x1, Pallas kernels: 35.2 us -> 18 us  [shards(): pl.pallas_call(main_kernel, out_shape=(shape(block, F32), shape(block, F3...]
  transfers between devices with their start and end apart: 5 -> 5, of which waited for: 2 -> 2; matrix products, arithmetic and copies ran while one was open for 0% -> 0% of each run, Pallas kernels for 4% -> 5%
where the time goes in v1:
time: 59.9 us; the launch traced here: 59.4 us
  Pallas kernels  26.4 us (44%)
  blocking collectives  13.4 us (22%)
  starting transfers between devices  12.8 us (21%)
  waiting for transfers between devices  3.47 us (6%)
  local copies, waits for them, and re-layouts  2.71 us (5%)
  between operations  0.66 us (1%)
    pallas_call x1, Pallas kernels, shards(): pl.pallas_call(main_kernel, out_shape=(shape(block, F32), shape(block, F3...  18 us
    all_gather x1, blocking collectives, shards(): pay = lax.all_gather(packed, 'crow', axis=0)  13.4 us
    ppermute x2, starting transfers between devices, across(): return lax.ppermute(piece, ('sub', 'crow'), pairs)  8.03 us
    ppermute x3, starting transfers between devices, shards(): lax.ppermute(t, 'crow', [(n, n ^ m) for n in range(NC)])  4.76 us
    ppermute x3, waiting for transfers between devices, shards(): lax.ppermute(t, 'crow', [(n, n ^ m) for n in range(NC)])  3.47 us
    pallas_call x1, Pallas kernels, shards(): pl.pallas_call(middle_kernel, out_shape=(shape((3 * V, LANES), F32), shap...  3.15 us
    unnamed x11, local copies, waits for them, and re-layouts  2.71 us
    pallas_call x1, Pallas kernels, shards(): pl.pallas_call(coarse_kernel, out_shape=(slab,) * 4, in_specs=[smem()] +...  1.85 us
  transfers between devices with their start and end apart: 5, of which 2 were waited for; matrix products, arithmetic and copies ran while one was open for 0% of the time, Pallas kernels for 5%

profile of v1, /device:TPU:1, one launch (start us, length us, event | category | flops | bytes accessed | tf_op | source)
XLA Modules:
  0.0 59.4 jit_solution(16762032579629583961)
XLA Ops:
  0.6 1.8 %shard_map.95 = f32[435,128]{1,0:T(8,128)} custom-call(s32[1]{0:T(128)} %bitcast.c_ref, s32[6]{0:T(128)} %bitcast.27, f32[144,128]{1,0:T(8,128)} %bitcast.22, f32[243,1,128]{2,1,0:T(1,128)} %bitcast.21, s32[27,1,128]{2,1,0:T(1,128)} %bitcast.23, s32[1,128]{1,0:T(1,128)} %cnt_ref.1, f32[3,1,128]{2,1,0:T(1,128)} %bitcast.26, s32[6,1,32]{2,1,0:T(1,128)} %bitcast.24, ...), custom_call_target="tpu_custom_call" | custom-call | tf_op jit(solution)/shard_map/pallas_call | solution.py:331
  2.5 13.4 %all-gather.1.pay_ref = f32[4,435,128]{2,1,0:T(8,128)} all-gather(f32[1,435,128]{2,1,0:T(8,128)} %bitcast.19), channel_id=2, replica_groups=mesh['sub'=64,'crow'=4] {'crow'}, dimensions={0}, use_global_device_ids=true | all-gather | bytes 1113600 | tf_op jit(solution)/shard_map/all_gather | solution.py:347
  15.9 18.0 %shard_map.96 = (f32[4,144,128]{2,1,0:T(8,128)}, f32[4,144,128]{2,1,0:T(8,128)}, f32[48,48]{1,0:T(8,128)}, f32[144,128]{1,0:T(8,128)}, f32[72,128]{1,0:T(8,128)}) custom-call(s32[1]{0:T(128)} %bitcast.c_ref, f32[4,435,128]{2,1,0:T(8,128)} %all-gather.1.pay_ref), custom_call_target="tpu_custom_call" | custom-call | tf_op jit(solution)/shard_map/pallas_call | solution.py:349
  33.9 1.3 %collective-permute-start = (f32[144,128]{1,0:T(8,128)}, f32[144,128]{1,0:T(8,128)S(1)}, u32[]{:S(2)}, u32[]{:S(2)}) collective-permute-start(f32[144,128]{1,0:T(8,128)} %get-tuple-element.22), channel_id=1, source_target_pairs={{0,12},{1,9},{2,6},{3,255},{4,16},{5,13},{6,10},{7,3},{8,20},{9,17... | collective-permute-start | bytes 221192 | tf_op jit(solution)/shard_map/ppermute | solution.py:380
  35.2 6.7 %collective-permute-start.1 = (f32[72,128]{1,0:T(8,128)}, f32[72,128]{1,0:T(8,128)S(1)}, u32[]{:S(2)}, u32[]{:S(2)}) collective-permute-start(f32[72,128]{1,0:T(8,128)} %get-tuple-element.23), channel_id=1, source_target_pairs={{0,248},{1,249},{2,246},{3,247},{4,252},{5,253},{6,250},{7,251},{8... | collective-permute-start | bytes 110600 | tf_op jit(solution)/shard_map/ppermute | solution.py:380
  41.9 3.1 %shard_map.97 = (f32[144,128]{1,0:T(8,128)}, f32[144,128]{1,0:T(8,128)}, f32[144,128]{1,0:T(8,128)}, f32[48,48]{1,0:T(8,128)}) custom-call(s32[1]{0:T(128)} %bitcast.c_ref, f32[4,435,128]{2,1,0:T(8,128)} %all-gather.1.pay_ref, f32[4,144,128]{2,1,0:T(8,128)} %get-tuple-element.15.y2_ref, f32[4,144,128]{2,1,0:T(8,128)} %get-tuple-element.16.w_ref, ...), custom_call_target="tpu_custom_call" | custom-call | tf_op jit(solution)/shard_map/pallas_call | solution.py:384
  45.1 0.0 collective-permute-done.1.got2_ref
  45.1 0.0 copy-start.1
  45.1 0.0 collective-permute-done.got1_ref
  45.1 0.0 copy-start
  45.1 0.6 %copy-done.1 = f32[72,128]{1,0:T(8,128)} copy-done((f32[72,128]{1,0:T(8,128)}, f32[72,128]{1,0:T(8,128)S(1)}, u32[]{:S(2)}) %copy-start.1) | copy-done | bytes 36888
  45.7 0.0 copy-done
  45.7 1.9 %shard_map.98 = (f32[32,128]{1,0:T(8,128)}, f32[32,128]{1,0:T(8,128)}, f32[32,128]{1,0:T(8,128)}, f32[32,128]{1,0:T(8,128)}) custom-call(s32[1]{0:T(128)} %bitcast.c_ref, f32[144,128]{1,0:T(8,128)} %get-tuple-element.20.mine1_ref, f32[144,128]{1,0:T(8,128)} %get-tuple-element.21.mine2_ref, f32[144,128]{1,0:T(8,128)} %copy-done, f32[72,128]{1,0:T(8,128)} %copy-done.1), custom_call_target="tpu_custom_call" | custom-call | tf_op jit(solution)/shard_map/pallas_call | solution.py:397
  47.6 2.2 %collective-permute-start.2 = (f32[32,128]{1,0:T(8,128)}, f32[32,128]{1,0:T(8,128)S(1)}, u32[]{:S(2)}, u32[]{:S(2)}) collective-permute-start(f32[32,128]{1,0:T(8,128)} %get-tuple-element.25), channel_id=1, source_target_pairs={{0,1},{1,0},{2,3},{3,2},{4,5},{5,4},{6,7},{7,6},{8,9},{9,8},{10,11... | collective-permute-start | bytes 49160 | tf_op jit(solution)/shard_map/ppermute | solution.py:404
  49.7 2.4 %collective-permute-start.3 = (f32[32,128]{1,0:T(8,128)}, f32[32,128]{1,0:T(8,128)S(1)}, u32[]{:S(2)}, u32[]{:S(2)}) collective-permute-start(f32[32,128]{1,0:T(8,128)} %get-tuple-element.26), channel_id=1, source_target_pairs={{0,2},{1,3},{2,0},{3,1},{4,6},{5,7},{6,4},{7,5},{8,10},{9,11},{10,... | collective-permute-start | bytes 49160 | tf_op jit(solution)/shard_map/ppermute | solution.py:404
  52.1 0.2 collective-permute-start.4
  52.3 0.0 collective-permute-done.2.a_ref
  52.3 0.0 copy-start.2
  52.3 1.1 %collective-permute-done.3.b_ref = f32[32,128]{1,0:T(8,128)S(1)} collective-permute-done((f32[32,128]{1,0:T(8,128)}, f32[32,128]{1,0:T(8,128)S(1)}, u32[]{:S(2)}, u32[]{:S(2)}) %collective-permute-start.3) | collective-permute-done | bytes 16416 | tf_op jit(solution)/shard_map/ppermute | solution.py:404
  53.5 0.0 copy-start.3
  53.5 2.4 %collective-permute-done.4.d_ref = f32[32,128]{1,0:T(8,128)S(1)} collective-permute-done((f32[32,128]{1,0:T(8,128)}, f32[32,128]{1,0:T(8,128)S(1)}, u32[]{:S(2)}, u32[]{:S(2)}) %collective-permute-start.4) | collective-permute-done | bytes 16416 | tf_op jit(solution)/shard_map/ppermute | solution.py:404
  55.8 0.0 copy-start.4
  55.8 0.0 copy-done.2
  55.8 0.0 copy-done.3
  55.8 0.6 copy-done.4
  56.4 1.5 %shard_map.99 = f32[7,12,48]{2,1,0:T(8,128)} custom-call(s32[1]{0:T(128)} %bitcast.c_ref, f32[48,48]{1,0:T(8,128)} %get-tuple-element.19.center_ref, f32[32,128]{1,0:T(8,128)} %get-tuple-element.24.own_ref, f32[32,128]{1,0:T(8,128)} %copy-done.2, f32[32,128]{1,0:T(8,128)} %copy-done.3, f32[32,128]{1,0:T(8,128)} %copy-done.4), custom_call_target="tpu_custom_call" | custom-call | tf_op jit(solution)/shard_map/pallas_call | solution.py:405
  57.9 1.5 %copy.11 = f32[1,7,12,48]{3,0,2,1:T(1,128)} copy(f32[1,7,12,48]{3,2,1,0:T(8,128)} %bitcast.20) | data formatting | bytes 32256
Async XLA Ops:
  33.9 11.2 %collective-permute-start = (f32[144,128]{1,0:T(8,128)}, f32[144,128]{1,0:T(8,128)S(1)}, u32[]{:S(2)}, u32[]{:S(2)}) collective-permute-start(f32[144,128]{1,0:T(8,128)} %get-tuple-element.22), channel_id=1, source_target_pairs={{0,12},{1,9},{2,6},{3,255},{4,16},{5,13},{6,10},{7,3},{8,20},{9,17... | collective-permute-start | bytes 221192 | tf_op jit(solution)/shard_map/ppermute | solution.py:380
  35.2 9.9 %collective-permute-start.1 = (f32[72,128]{1,0:T(8,128)}, f32[72,128]{1,0:T(8,128)S(1)}, u32[]{:S(2)}, u32[]{:S(2)}) collective-permute-start(f32[72,128]{1,0:T(8,128)} %get-tuple-element.23), channel_id=1, source_target_pairs={{0,248},{1,249},{2,246},{3,247},{4,252},{5,253},{6,250},{7,251},{8... | collective-permute-start | bytes 110600 | tf_op jit(solution)/shard_map/ppermute | solution.py:380
  45.1 0.6 %copy-start.1 = (f32[72,128]{1,0:T(8,128)}, f32[72,128]{1,0:T(8,128)S(1)}, u32[]{:S(2)}) copy-start(f32[72,128]{1,0:T(8,128)S(1)} %collective-permute-done.1.got2_ref) | copy-start | bytes 110596
  45.1 0.6 %copy-start = (f32[144,128]{1,0:T(8,128)}, f32[144,128]{1,0:T(8,128)S(1)}, u32[]{:S(2)}) copy-start(f32[144,128]{1,0:T(8,128)S(1)} %collective-permute-done.got1_ref) | copy-start | bytes 221188
  47.6 4.8 %collective-permute-start.2 = (f32[32,128]{1,0:T(8,128)}, f32[32,128]{1,0:T(8,128)S(1)}, u32[]{:S(2)}, u32[]{:S(2)}) collective-permute-start(f32[32,128]{1,0:T(8,128)} %get-tuple-element.25), channel_id=1, source_target_pairs={{0,1},{1,0},{2,3},{3,2},{4,5},{5,4},{6,7},{7,6},{8,9},{9,8},{10,11... | collective-permute-start | bytes 49160 | tf_op jit(solution)/shard_map/ppermute | solution.py:404
  49.7 3.7 %collective-permute-start.3 = (f32[32,128]{1,0:T(8,128)}, f32[32,128]{1,0:T(8,128)S(1)}, u32[]{:S(2)}, u32[]{:S(2)}) collective-permute-start(f32[32,128]{1,0:T(8,128)} %get-tuple-element.26), channel_id=1, source_target_pairs={{0,2},{1,3},{2,0},{3,1},{4,6},{5,7},{6,4},{7,5},{8,10},{9,11},{10,... | collective-permute-start | bytes 49160 | tf_op jit(solution)/shard_map/ppermute | solution.py:404
  52.1 3.7 %collective-permute-start.4 = (f32[32,128]{1,0:T(8,128)}, f32[32,128]{1,0:T(8,128)S(1)}, u32[]{:S(2)}, u32[]{:S(2)}) collective-permute-start(f32[32,128]{1,0:T(8,128)} %get-tuple-element.27), channel_id=1, source_target_pairs={{0,3},{1,2},{2,1},{3,0},{4,7},{5,6},{6,5},{7,4},{8,11},{9,10},{10,... | collective-permute-start | bytes 49160 | tf_op jit(solution)/shard_map/ppermute | solution.py:404
  52.3 3.5 %copy-start.2 = (f32[32,128]{1,0:T(8,128)}, f32[32,128]{1,0:T(8,128)S(1)}, u32[]{:S(2)}) copy-start(f32[32,128]{1,0:T(8,128)S(1)} %collective-permute-done.2.a_ref) | copy-start | bytes 49156
  53.5 2.4 %copy-start.3 = (f32[32,128]{1,0:T(8,128)}, f32[32,128]{1,0:T(8,128)S(1)}, u32[]{:S(2)}) copy-start(f32[32,128]{1,0:T(8,128)S(1)} %collective-permute-done.3.b_ref) | copy-start | bytes 49156
  55.8 0.6 %copy-start.4 = (f32[32,128]{1,0:T(8,128)}, f32[32,128]{1,0:T(8,128)S(1)}, u32[]{:S(2)}) copy-start(f32[32,128]{1,0:T(8,128)S(1)} %collective-permute-done.4.d_ref) | copy-start | bytes 49156

commit v2 on v1

v2 whole, which is shorter than its diff:
```python
import jax
import jax.numpy as jnp
from jax import lax
from jax.experimental import pallas as pl
from jax.experimental.pallas import tpu as pltpu
from jax.sharding import PartitionSpec as P

RADIUS = 3
SLOTS = 2 * RADIUS
V = 48
LANES = 128
NB = 27
NC = 4
OVD = 32
SCALE = float(LANES * NC // OVD)
TILES = V // 8

COL0 = 0
PIV0 = COL0 + NB
SEND0 = PIV0 + 3
RECV0 = SEND0 + SLOTS
LIVE0 = RECV0 + SLOTS
PACKED = LIVE0 + SLOTS

OFFSETS = [o - RADIUS if o < RADIUS else o - RADIUS + 1 for o in range(SLOTS)]
SENT = [0, 2, 5, 3]
GOT = [SENT[c ^ 2] for c in range(NC)]
SPLIT = [1, 4, 1, 4]
HIGH = lax.Precision.HIGHEST
F32 = jnp.float32


def vmem():
    return pl.BlockSpec(memory_space=pltpu.VMEM)


def smem():
    return pl.BlockSpec(memory_space=pltpu.SMEM)


def whole():
    return pl.BlockSpec(memory_space=pl.ANY)


def pack_kernel(c_ref, ov_ref, col_ref, cnt_ref, piv_ref, send_ref, recv_ref, out_ref):
    count = cnt_ref[...]
    for k in range(NB):
        out_ref[COL0 + k : COL0 + k + 1, :] = jnp.where(k < count, col_ref[k].astype(F32), -1.0)
    for a in range(3):
        out_ref[PIV0 + a : PIV0 + a + 1, :] = piv_ref[a]
    lane = lax.broadcasted_iota(jnp.int32, (1, LANES), 1)
    c = c_ref[0]
    here = (lane // OVD) == c
    for o in range(SLOTS):
        for ref, base in ((send_ref, SEND0), (recv_ref, RECV0)):
            piece = ref[o].astype(F32)
            row = jnp.concatenate([piece] * NC, axis=1)
            out_ref[base + o : base + o + 1, :] = jnp.where(here, row, 0.0)
        alive = here & ((lane % OVD) < ov_ref[o])
        out_ref[LIVE0 + o : LIVE0 + o + 1, :] = jnp.where(alive, 1.0, 0.0).astype(F32)


def fetch(pairs, sem):
    copies = [pltpu.make_async_copy(src, dst, sem.at[n]) for n, (src, dst) in enumerate(pairs)]
    for copy in copies:
        copy.start()
    for copy in copies:
        copy.wait()


def entry(table, c):
    value = jnp.int32(table[0])
    for n in range(1, NC):
        value = jnp.where(c == n, table[n], value)
    return value


def wide(row):
    return jnp.broadcast_to(row, (8, LANES))


def lanes_of(block, index):
    return jnp.take_along_axis(block, index, axis=1)


def start_op(small_ref, src_ref, dst_ref):
    for q in range(NC):
        for a in range(3):
            piv = wide(small_ref[q, PIV0 + a : PIV0 + a + 1, :])
            for t in range(TILES):
                rows = slice(a * V + 8 * t, a * V + 8 * t + 8)
                dst_ref[q, rows, :] = piv * src_ref[q, rows, :]


ONE = 18
BF16 = jnp.bfloat16


def value_row(val_ref, rc, ab, k):
    return wide(val_ref[rc, ab * NB + k])


def add_block(val, dst_ref, rc, pick_of):
    for t in range(TILES):
        pick = [pick_of(b, t) for b in range(3)]
        for a in range(3):
            at = slice(a * V + 8 * t, a * V + 8 * t + 8)
            dst_ref[rc, at, :] = dst_ref[rc, at, :] + (
                val[3 * a] * pick[0] + val[3 * a + 1] * pick[1] + val[3 * a + 2] * pick[2]
            )


def lane_block(val_ref, small_ref, src_ref, dst_ref, rc, k):
    col = wide(small_ref[rc, pl.ds(COL0 + k, 1), :]).astype(jnp.int32)
    val = [jnp.where(col >= 0, value_row(val_ref, rc, ab, k), 0.0) for ab in range(9)]
    index = col & (LANES - 1)
    odd = (col & LANES) != 0
    top = col >= 2 * LANES

    def pick_of(b, t):
        got = [lanes_of(src_ref[q, b * V + 8 * t : b * V + 8 * t + 8, :], index) for q in range(NC)]
        return jnp.where(top, jnp.where(odd, got[3], got[2]), jnp.where(odd, got[1], got[0]))

    add_block(val, dst_ref, rc, pick_of)


def one_hot(small_ref, oh_ref, k):
    half = 2 * LANES
    place = lax.broadcasted_iota(jnp.int32, (half, half), 0).astype(F32).astype(BF16)
    for m in range(2):
        col = jnp.concatenate([small_ref[2 * m + n, pl.ds(COL0 + k, 1), :] for n in range(2)], axis=1)
        for h in range(2):
            local = col - float(h * half)
            local = jnp.where((local >= 0.0) & (local < float(half)), local, -1.0)
            target = jnp.concatenate([jnp.broadcast_to(local, (16, half)).astype(BF16)] * (half // 16), axis=0)
            oh_ref[m, k, h * half : h * half + half, :] = jnp.where(
                place == target, jnp.ones((), BF16), jnp.zeros((), BF16)
            )


def split_to(x_ref, src_ref):
    for q in range(NC):
        at = slice(q * LANES, q * LANES + LANES)
        value = src_ref[q, 0 : 3 * V, :]
        high = value.astype(BF16)
        x_ref[0 : 3 * V, at] = high
        x_ref[3 * V :, at] = (value - high.astype(F32)).astype(BF16)


def issue(x_ref, oh_ref, t_ref, k, parity):
    for m in range(2):
        got = jnp.dot(x_ref[...], oh_ref[m, k], preferred_element_type=F32)
        t_ref[parity, m] = got[: 3 * V, :] + got[3 * V :, :]


def take(val_ref, dst_ref, t_ref, k, parity):
    for m in range(2):
        for n in range(2):
            at = slice(n * LANES, n * LANES + LANES)
            rc = 2 * m + n
            val = [value_row(val_ref, rc, ab, k) for ab in range(9)]
            add_block(val, dst_ref, rc, lambda b, t: t_ref[parity, m, b * V + 8 * t : b * V + 8 * t + 8, at])


def flat(ref):
    return jnp.concatenate([ref[q, a * V : a * V + V, :] for a in range(3) for q in range(NC)], axis=1)


def gram_to(m_ref, block):
    gram = lax.dot_general(block, block, (((1,), (1,)), ((), ())), precision=HIGH, preferred_element_type=F32)
    row = lax.broadcasted_iota(jnp.int32, (V, 64), 0)
    lane = lax.broadcasted_iota(jnp.int32, (V, 64), 1)
    eye = jnp.where(row == lane, 1.0, 0.0).astype(F32)
    m_ref[:V, :] = jnp.concatenate([eye, gram, jnp.zeros((V, LANES - 64 - V), F32)], axis=1)


CHOL = 3
UN = 6


def factor_piece(m_ref, col_ref, j):
    sub = lax.broadcasted_iota(jnp.int32, (8, LANES), 0)
    m = [m_ref[8 * t : 8 * t + 8, :] for t in range(TILES)]
    cols = []
    for s in range(CHOL):
        index = jnp.full((8, LANES), 64 + s, jnp.int32) + j
        cols.append([lanes_of(m[t], index) for t in range(TILES)])
        for t in range(TILES):
            col_ref[s, 8 * t : 8 * t + 8, :] = cols[s][t]
    for s in range(CHOL):
        row = wide(m_ref[pl.ds(j + s, 1), :])
        head = {n: wide(col_ref[n, pl.ds(j + s, 1), :]) for n in range(s, CHOL)}
        inverse = 1.0 / head[s]
        for t in range(TILES):
            factor = jnp.where(sub + 8 * t > j + s, cols[s][t] * inverse, 0.0)
            m[t] = m[t] - factor * row
            m_ref[8 * t : 8 * t + 8, :] = m[t]
            for n in range(s + 1, CHOL):
                cols[n][t] = cols[n][t] - factor * head[n]
                col_ref[n, 8 * t : 8 * t + 8, :] = cols[n][t]


def inverse_of(m_ref):
    m = m_ref[:V, :]
    row = lax.broadcasted_iota(jnp.int32, (V, LANES), 0)
    lane = lax.broadcasted_iota(jnp.int32, (V, LANES), 1)
    diag = jnp.sum(jnp.where(lane == row + 64, m, 0.0), axis=1, keepdims=True)
    return m[:, :V] / jnp.sqrt(diag)


def solve_to(dst_ref, linv, src_ref):
    out = jnp.dot(linv, flat(src_ref), precision=HIGH, preferred_element_type=F32)
    for a in range(3):
        for q in range(NC):
            at = (a * NC + q) * LANES
            dst_ref[q, a * V : a * V + V, :] = out[:, at : at + LANES]


def rows_of(src_ref, index, tiles, c):
    block = (lax.broadcasted_iota(jnp.int32, (8, LANES), 1) // OVD) ^ c
    out = []
    for at in tiles:
        pick = lanes_of(src_ref[NC - 1, at, :], index)
        for q in range(NC - 1):
            pick = jnp.where(block == q, lanes_of(src_ref[q, at, :], index), pick)
        out.append(pick)
    return out


def index_row(small_ref, row):
    total = small_ref[0, pl.ds(row, 1), :]
    for q in range(1, NC):
        total = total + small_ref[q, pl.ds(row, 1), :]
    return total


def main_kernel(
    c_ref, x0, x1, x2, x3, v0, v1, v2, v3, p0, p1, p2, p3,
    y2_ref, w_ref, linv_ref, s1_ref, s2_ref, row_ref,
    in_ref, val_ref, small_ref, sem, y_ref, z_ref, m_ref, col_ref, g_ref, x_ref, oh_ref, t_ref,
):
    c = c_ref[0]
    fetch(
        [(ref, dst.at[m]) for refs, dst in (((x0, x1, x2, x3), in_ref), ((v0, v1, v2, v3), val_ref), ((p0, p1, p2, p3), small_ref)) for m, ref in enumerate(refs)],
        sem,
    )
    for m in range(NC):
        col = small_ref[m, COL0 : COL0 + NB, :]
        local = (col.astype(jnp.int32) ^ (c * LANES)).astype(F32)
        small_ref[m, COL0 : COL0 + NB, :] = jnp.where(col < 0.0, -1.0, local)
    m_ref[V:, :] = jnp.zeros((8, LANES), F32)

    def loop(src_ref, dst_ref, first):
        start_op(small_ref, src_ref, dst_ref)
        split_to(x_ref, src_ref)
        if first:
            one_hot(small_ref, oh_ref, 0)
            one_hot(small_ref, oh_ref, 1)
        issue(x_ref, oh_ref, t_ref, 0, 0)

        def step(it, carry):
            for u in range(UN):
                k = UN * it + u
                issue(x_ref, oh_ref, t_ref, jnp.minimum(k + 1, ONE - 1), (u + 1) % 2)
                for rc in (2 * (u % 2), 2 * (u % 2) + 1):
                    lane_block(val_ref, small_ref, src_ref, dst_ref, rc, ONE + (UN // 2) * it + u // 2)
                if first:
                    one_hot(small_ref, oh_ref, jnp.minimum(k + 2, ONE - 1))
                else:
                    factor_piece(m_ref, col_ref, k * CHOL)
                take(val_ref, dst_ref, t_ref, k, u % 2)
            return carry

        lax.fori_loop(0, ONE // UN, step, 0)

    loop(in_ref, y_ref, True)
    gram_to(m_ref, flat(y_ref))
    loop(y_ref, z_ref, False)
    solve_to(y2_ref, inverse_of(m_ref), z_ref)
    gram_to(m_ref, flat(y2_ref))
    loop(y2_ref, w_ref, False)
    linv = inverse_of(m_ref)
    linv_ref[...] = linv
    first = wide(index_row(small_ref, SEND0 + entry(SENT, c))).astype(jnp.int32)
    second = wide(index_row(small_ref, SEND0 + entry(SPLIT, c))).astype(jnp.int32)
    half = (c // 2) * (V // 2)
    for n, slot in enumerate((entry(GOT, c), entry(SPLIT, c))):
        row_ref[2 * n : 2 * n + 1, :] = index_row(small_ref, RECV0 + slot)
        row_ref[2 * n + 1 : 2 * n + 2, :] = index_row(small_ref, LIVE0 + slot)
    tiles = [slice(8 * t, 8 * t + 8) for t in range(3 * TILES)]
    for n, index in enumerate((first, second)):
        for at, piece in zip(tiles, rows_of(w_ref, index, tiles, c)):
            g_ref[n, at, :] = piece
    both = jnp.concatenate([g_ref[n, a * V : a * V + V, :] for n in range(2) for a in range(3)], axis=1)
    image = jnp.dot(linv, both, precision=HIGH, preferred_element_type=F32)
    for a in range(3):
        s1_ref[a * V : a * V + V, :] = image[:, a * LANES : a * LANES + LANES]
        g_ref[1, a * V : a * V + V, :] = image[:, (3 + a) * LANES : (4 + a) * LANES]
        s2_ref[a * (V // 2) : (a + 1) * (V // 2), :] = g_ref[1, pl.ds(pl.multiple_of(a * V + half, 8), V // 2), :]


def middle_kernel(c_ref, row_ref, y2_ref, w_ref, linv_ref, basis_ref, mine1_ref, mine2_ref, center_ref, q_ref):
    c = c_ref[0]
    linv = linv_ref[...]
    solve_to(q_ref, linv, y2_ref)
    basis_ref[...] = q_ref[0]
    tiles = [slice(8 * t, 8 * t + 8) for t in range(3 * TILES)]
    for n, out_ref in enumerate((mine1_ref, mine2_ref)):
        index = wide(row_ref[2 * n : 2 * n + 1, :]).astype(jnp.int32)
        live = wide(row_ref[2 * n + 1 : 2 * n + 2, :])
        for at, piece in zip(tiles, rows_of(q_ref, index, tiles, c)):
            out_ref[at, :] = piece * live
    image = jnp.dot(linv, flat(w_ref), precision=HIGH, preferred_element_type=F32)
    center_ref[...] = lax.dot_general(
        flat(q_ref), image, (((1,), (1,)), ((), ())), precision=HIGH, preferred_element_type=F32
    )


def coarse_kernel(c_ref, mine1_ref, mine2_ref, in1_ref, in2_ref, own_ref, a_ref, b_ref, d_ref, r_ref, got1_ref, got2_ref, sem):
    c = c_ref[0]
    fetch([(in1_ref, got1_ref), (in2_ref, got2_ref)], sem)

    def side(ref, count):
        return jnp.concatenate([ref[a * count : a * count + count, :] for a in range(3)], axis=1)

    nt = (((1,), (1,)), ((), ()))
    one = lax.dot_general(side(mine1_ref, V), side(got1_ref, V), nt, precision=HIGH, preferred_element_type=F32) * SCALE
    two = lax.dot_general(side(mine2_ref, V), side(got2_ref, V // 2), nt, precision=HIGH, preferred_element_type=F32) * SCALE
    part = V // NC
    for d in range(NC):
        r_ref[d, 0:part, 0:V] = one[d * part : d * part + part, :]
        r_ref[d, 16 : 16 + part, 0 : V // 2] = two[d * part : d * part + part, :]
    own_ref[...] = r_ref[c]
    a_ref[...] = r_ref[c ^ 1]
    b_ref[...] = r_ref[c ^ 2]
    d_ref[...] = r_ref[c ^ 3]


def join_kernel(c_ref, center_ref, own_ref, a_ref, b_ref, d_ref, out_ref, r_ref, sem):
    c = c_ref[0]
    part = V // NC
    fetch([(ref, r_ref.at[m]) for m, ref in enumerate((own_ref, a_ref, b_ref, d_ref))], sem)

    def put(place, value):
        for v in range(part):
            out_ref[place * part + v] = value[v : v + 1, :]

    for d in range(NC):
        slot = GOT[d]
        put(slot if slot < RADIUS else slot + 1, r_ref[c ^ d, 0:part, 0:V])
    for d in range(2):
        slot = SPLIT[d]
        sides = [r_ref[c ^ (d + 2 * h), 16 : 16 + part, 0 : V // 2] for h in range(2)]
        put(slot if slot < RADIUS else slot + 1, jnp.concatenate(sides, axis=1))
    for d in range(NC):

        @pl.when(c == d)
        def _():
            put(RADIUS, center_ref[d * part : d * part + part, :])


def shards(test_vectors, ell_values, ell_cols, ell_count, pivot, send_rows, recv_rows, ov_count):
    shape = jax.ShapeDtypeStruct
    c = lax.axis_index("crow").astype(jnp.int32).reshape(1)
    x = jnp.transpose(test_vectors[0], (1, 0, 2)).reshape(3 * V, LANES)
    values = ell_values.reshape(9 * NB, 1, LANES)

    def pass_on(piece, m):
        return lax.ppermute(piece, "crow", [(n, n ^ m) for n in range(NC)])

    far_x = pass_on(x, 2)
    far_v = pass_on(values, 2)
    small = pl.pallas_call(
        pack_kernel,
        out_shape=shape((PACKED, LANES), F32),
        in_specs=[smem(), smem()] + [vmem()] * 5,
        out_specs=vmem(),
    )(
        c,
        ov_count.reshape(SLOTS),
        ell_cols.reshape(NB, 1, LANES),
        ell_count.reshape(1, LANES),
        pivot.reshape(3, 1, LANES),
        send_rows.reshape(SLOTS, 1, OVD),
        recv_rows.reshape(SLOTS, 1, OVD),
    )
    far_s = pass_on(small, 2)
    blocks = []
    for own, far in ((x, far_x), (values, far_v), (small, far_s)):
        blocks += [own, pass_on(own, 1), far, pass_on(far, 1)]
    block = (NC, 3 * V, LANES)
    y2, w, linv, s1, s2, row = pl.pallas_call(
        main_kernel,
        out_shape=(
            shape(block, F32),
            shape(block, F32),
            shape((V, V), F32),
            shape((3 * V, LANES), F32),
            shape((3 * V // 2, LANES), F32),
            shape((8, LANES), F32),
        ),
        in_specs=[smem()] + [whole()] * 12,
        out_specs=(vmem(),) * 6,
        scratch_shapes=[
            pltpu.VMEM(block, F32),
            pltpu.VMEM((NC, 9 * NB, 1, LANES), F32),
            pltpu.VMEM((NC, PACKED, LANES), F32),
            pltpu.SemaphoreType.DMA((12,)),
            pltpu.VMEM(block, F32),
            pltpu.VMEM(block, F32),
            pltpu.VMEM((V + 8, LANES), F32),
            pltpu.VMEM((CHOL, V + 8, LANES), F32),
            pltpu.VMEM((2, 3 * V, LANES), F32),
            pltpu.VMEM((6 * V, NC * LANES), BF16),
            pltpu.VMEM((2, ONE, NC * LANES, 2 * LANES), BF16),
            pltpu.VMEM((2, 2, 3 * V, 2 * LANES), F32),
        ],
    )(c, *blocks)

    size = lax.axis_size("sub")

    def across(piece, slots, turn):
        pairs = []
        for j in range(size):
            for n in range(NC):
                i = (j - OFFSETS[slots[n]]) % size
                pairs.append((j * NC + n, i * NC + (n ^ turn)))
        return lax.ppermute(piece, ("sub", "crow"), pairs)

    got1 = across(s1, SENT, 2)
    got2 = across(s2, SPLIT, 0)
    basis, mine1, mine2, center = pl.pallas_call(
        middle_kernel,
        out_shape=(
            shape((3 * V, LANES), F32),
            shape((3 * V, LANES), F32),
            shape((3 * V, LANES), F32),
            shape((V, V), F32),
        ),
        in_specs=[smem()] + [vmem()] * 4,
        out_specs=(vmem(),) * 4,
        scratch_shapes=[pltpu.VMEM(block, F32)],
    )(c, row, y2, w, linv)
    slab = shape((32, LANES), F32)
    own, to1, to2, to3 = pl.pallas_call(
        coarse_kernel,
        out_shape=(slab,) * 4,
        in_specs=[smem()] + [vmem()] * 2 + [whole()] * 2,
        out_specs=(vmem(),) * 4,
        scratch_shapes=[
            pltpu.VMEM((NC, 32, LANES), F32),
            pltpu.VMEM((3 * V, LANES), F32),
            pltpu.VMEM((3 * V // 2, LANES), F32),
            pltpu.SemaphoreType.DMA((2,)),
        ],
    )(c, mine1, mine2, got1, got2)
    got = [pass_on(t, m) for m, t in ((1, to1), (2, to2), (3, to3))]
    coarse = pl.pallas_call(
        join_kernel,
        out_shape=shape(((2 * RADIUS + 1) * (V // NC), 1, V), F32),
        in_specs=[smem(), vmem()] + [whole()] * 4,
        out_specs=vmem(),
        scratch_shapes=[pltpu.VMEM((NC, 32, LANES), F32), pltpu.SemaphoreType.DMA((4,))],
    )(c, center, own, *got)
    coarse = coarse.reshape(2 * RADIUS + 1, V // NC, V)
    basis = jnp.transpose(basis.reshape(3, V, LANES), (1, 0, 2))
    return basis[None], coarse[None]


def solution(mesh):
    placed = (
        P("sub", None, None, "crow"),
        P("sub", None, None, "crow"),
        P("sub", None, "crow"),
        P("sub", "crow"),
        P("sub", None, "crow"),
        P("sub", None, "crow"),
        P("sub", None, "crow"),
        P("sub", None, "crow"),
    )
    return jax.shard_map(
        shards,
        mesh=mesh,
        in_specs=placed,
        out_specs=(P("sub", None, None, "crow"), P("sub", None, "crow", None)),
        check_vma=False,
    )
```

time: 59.9 us -> 65.8 us (1.098)
  blocking collectives: 13.4 us -> 0 us
  starting transfers between devices: 12.8 us -> 26 us
  waiting for transfers between devices: 3.47 us -> 7.09 us
  Pallas kernels: 26.4 us -> 28.9 us
    all_gather x1 -> x0, blocking collectives: 13.4 us -> none  [shards(): pay = lax.all_gather(packed, 'crow', axis=0)]
    ppermute x3 -> x12, starting transfers between devices: 4.76 us -> 16.1 us  [pass_on(): return lax.ppermute(piece, 'crow', [(n, n ^ m) for n in range(NC)])]
    ppermute x3 -> x12, waiting for transfers between devices: 3.47 us -> 7.09 us  [pass_on(): return lax.ppermute(piece, 'crow', [(n, n ^ m) for n in range(NC)])]
    ppermute x2, starting transfers between devices: 8.03 us -> 9.88 us  [across(): return lax.ppermute(piece, ('sub', 'crow'), pairs)]
    pallas_call x1, Pallas kernels: 18 us -> 19.5 us  [shards(): pl.pallas_call(main_kernel, out_shape=(shape(block, F32), shape(block, F3...]
    pallas_call x1, Pallas kernels: 1.85 us -> 2.72 us  [shards(): pl.pallas_call(coarse_kernel, out_shape=(slab,) * 4, in_specs=[smem()] +...]
    pallas_call x1, Pallas kernels: 1.48 us -> 2.24 us  [shards(): pl.pallas_call(join_kernel, out_shape=shape(((2 * RADIUS + 1) * (V // NC)...]
    unnamed x11 -> x28, local copies, waits for them, and re-layouts: 2.71 us -> 2.52 us
  transfers between devices with their start and end apart: 5 -> 14, of which waited for: 2 -> 5; matrix products, arithmetic and copies ran while one was open for 0% -> 0% of each run, Pallas kernels for 5% -> 7%
where the time goes in v2:
time: 65.8 us; the launch traced here: 65.4 us
  Pallas kernels  28.9 us (44%)
  starting transfers between devices  26 us (40%)
  waiting for transfers between devices  7.09 us (11%)
  local copies, waits for them, and re-layouts  2.52 us (4%)
  between operations  0.92 us (1%)
    pallas_call x1, Pallas kernels, shards(): pl.pallas_call(main_kernel, out_shape=(shape(block, F32), shape(block, F3...  19.5 us
    ppermute x12, starting transfers between devices, pass_on(): return lax.ppermute(piece, 'crow', [(n, n ^ m) for n in range(NC)])  16.1 us
    ppermute x2, starting transfers between devices, across(): return lax.ppermute(piece, ('sub', 'crow'), pairs)  9.88 us
    ppermute x12, waiting for transfers between devices, pass_on(): return lax.ppermute(piece, 'crow', [(n, n ^ m) for n in range(NC)])  7.09 us
    pallas_call x1, Pallas kernels, shards(): pl.pallas_call(middle_kernel, out_shape=(shape((3 * V, LANES), F32), shap...  2.88 us
    pallas_call x1, Pallas kernels, shards(): pl.pallas_call(coarse_kernel, out_shape=(slab,) * 4, in_specs=[smem()] +...  2.72 us
    unnamed x28, local copies, waits for them, and re-layouts  2.52 us
    pallas_call x1, Pallas kernels, shards(): pl.pallas_call(join_kernel, out_shape=shape(((2 * RADIUS + 1) * (V // NC)...  2.24 us
  transfers between devices with their start and end apart: 14, of which 5 were waited for; matrix products, arithmetic and copies ran while one was open for 0% of the time, Pallas kernels for 7%

profile of v2, /device:TPU:1, one launch (start us, length us, event | category | flops | bytes accessed | tf_op | source)
XLA Modules:
  0.0 65.4 jit_solution(15143383058665417734)
XLA Ops:
  0.6 2.1 %collective-permute-start.4 = (f32[243,1,128]{2,1,0:T(1,128)}, f32[243,1,128]{2,1,0:T(1,128)S(1)}, u32[]{:S(2)}, u32[]{:S(2)}) collective-permute-start(f32[243,1,128]{2,1,0:T(1,128)} %bitcast.18), channel_id=1, source_target_pairs={{0,2},{1,3},{2,0},{3,1},{4,6},{5,7},{6,4},{7,5},{8,10},{9,11},{10,... | collective-permute-start | bytes 373256 | tf_op jit(solution)/shard_map/ppermute | solution.py:369
  2.7 0.1 collective-permute-start.1
  2.9 3.1 %collective-permute-start.3 = (f32[243,1,128]{2,1,0:T(1,128)}, f32[243,1,128]{2,1,0:T(1,128)S(1)}, u32[]{:S(2)}, u32[]{:S(2)}) collective-permute-start(f32[243,1,128]{2,1,0:T(1,128)} %bitcast.19), channel_id=1, source_target_pairs={{0,1},{1,0},{2,3},{3,2},{4,5},{5,4},{6,7},{7,6},{8,9},{9,8},{10,11... | collective-permute-start | bytes 373256 | tf_op jit(solution)/shard_map/ppermute | solution.py:369
  5.9 0.0 collective-permute-done.4.v2
  6.0 3.1 %collective-permute-start.5 = (f32[243,1,128]{2,1,0:T(1,128)S(1)}, f32[243,1,128]{2,1,0:T(1,128)S(1)}, u32[]{:S(2)}, u32[]{:S(2)}) collective-permute-start(f32[243,1,128]{2,1,0:T(1,128)S(1)} %collective-permute-done.4.v2), channel_id=1, source_target_pairs={{0,1},{1,0},{2,3},{3,2},{4,5},{5,4},{6,7},{7,6},{8,9},{9,8},{10,11... | collective-permute-start | bytes 373256 | tf_op jit(solution)/shard_map/ppermute | solution.py:369
  9.0 1.5 %shard_map.95.p0 = f32[48,128]{1,0:T(8,128)} custom-call(s32[1]{0:T(128)} %bitcast.c_ref, s32[6]{0:T(128)} %bitcast.29, s32[27,1,128]{2,1,0:T(1,128)} %bitcast.25, s32[1,128]{1,0:T(1,128)} %cnt_ref.1, f32[3,1,128]{2,1,0:T(1,128)} %bitcast.28, s32[6,1,32]{2,1,0:T(1,128)} %bitcast.26, s32[6,1,32]{2,1,0:T(1,128)} %bitcast.27), custom_call_target="tpu_custom_call" | custom-call | tf_op jit(solution)/shard_map/pallas_call | solution.py:373
  10.5 0.5 collective-permute-start.7
  11.0 0.3 collective-permute-start
  11.3 0.0 collective-permute-done.1.x2
  11.3 0.2 collective-permute-start.2
  11.5 1.9 %collective-permute-done.7.p2 = f32[48,128]{1,0:T(8,128)S(1)} collective-permute-done((f32[48,128]{1,0:T(8,128)}, f32[48,128]{1,0:T(8,128)S(1)}, u32[]{:S(2)}, u32[]{:S(2)}) %collective-permute-start.7) | collective-permute-done | bytes 24608 | tf_op jit(solution)/shard_map/ppermute | solution.py:369
  13.4 1.2 %collective-permute-start.6 = (f32[48,128]{1,0:T(8,128)}, f32[48,128]{1,0:T(8,128)S(1)}, u32[]{:S(2)}, u32[]{:S(2)}) collective-permute-start(f32[48,128]{1,0:T(8,128)} %shard_map.95.p0), channel_id=1, source_target_pairs={{0,1},{1,0},{2,3},{3,2},{4,5},{5,4},{6,7},{7,6},{8,9},{9,8},{10,11... | collective-permute-start | bytes 73736 | tf_op jit(solution)/shard_map/ppermute | solution.py:369
  14.6 1.1 %collective-permute-done.6.p1 = f32[48,128]{1,0:T(8,128)S(1)} collective-permute-done((f32[48,128]{1,0:T(8,128)}, f32[48,128]{1,0:T(8,128)S(1)}, u32[]{:S(2)}, u32[]{:S(2)}) %collective-permute-start.6) | collective-permute-done | bytes 24608 | tf_op jit(solution)/shard_map/ppermute | solution.py:369
  15.6 0.3 collective-permute-start.8
  16.0 0.8 %collective-permute-done.8.p3 = f32[48,128]{1,0:T(8,128)S(1)} collective-permute-done((f32[48,128]{1,0:T(8,128)S(1)}, f32[48,128]{1,0:T(8,128)S(1)}, u32[]{:S(2)}, u32[]{:S(2)}) %collective-permute-start.8) | collective-permute-done | bytes 24608 | tf_op jit(solution)/shard_map/ppermute | solution.py:369
  16.8 0.0 collective-permute-done.x1
  16.8 0.0 collective-permute-done.3.v1
  16.9 0.0 copy-start.1
  16.9 0.0 collective-permute-done.2.x3
  16.9 0.0 copy-start.5
  16.9 0.0 collective-permute-done.5.v3
  16.9 0.0 copy-done
  16.9 0.0 copy-done.3
  16.9 0.0 copy-done.8
  16.9 0.0 copy-done.9
  16.9 0.5 copy-done.10
  17.4 0.0 copy-done.4
  17.5 0.0 copy-done.1
  17.5 0.0 copy-done.5
  17.5 0.7 %copy-done.2 = f32[243,1,128]{2,1,0:T(1,128)} copy-done((f32[243,1,128]{2,1,0:T(1,128)}, f32[243,1,128]{2,1,0:T(1,128)S(1)}, u32[]{:S(2)}) %copy-start.2) | copy-done | bytes 124440
  18.2 19.5 %shard_map.96 = (f32[4,144,128]{2,1,0:T(8,128)}, f32[4,144,128]{2,1,0:T(8,128)}, f32[48,48]{1,0:T(8,128)}, f32[144,128]{1,0:T(8,128)}, f32[72,128]{1,0:T(8,128)}, /*index=5*/f32[8,128]{1,0:T(8,128)}) custom-call(s32[1]{0:T(128)} %bitcast.c_ref, f32[144,128]{1,0:T(8,128)} %bitcast.23, f32[144,128]{1,0:T(8,128)} %copy-done.4, f32[144,128]{1,0:T(8,128)} %copy-done.3, ...), custom_call_target="tpu_custom_call" | custom-call | tf_op jit(solution)/shard_map/pallas_call | solution.py:392
  37.8 1.9 %collective-permute-start.9 = (f32[144,128]{1,0:T(8,128)}, f32[144,128]{1,0:T(8,128)S(1)}, u32[]{:S(2)}, u32[]{:S(2)}) collective-permute-start(f32[144,128]{1,0:T(8,128)} %get-tuple-element.24), channel_id=1, source_target_pairs={{0,14},{1,7},{2,244},{3,253},{4,18},{5,11},{6,248},{7,1},{8,22},{9... | collective-permute-start | bytes 221192 | tf_op jit(solution)/shard_map/ppermute | solution.py:428
  39.6 8.0 %collective-permute-start.10 = (f32[72,128]{1,0:T(8,128)}, f32[72,128]{1,0:T(8,128)S(1)}, u32[]{:S(2)}, u32[]{:S(2)}) collective-permute-start(f32[72,128]{1,0:T(8,128)} %get-tuple-element.25), channel_id=1, source_target_pairs={{0,8},{1,249},{2,10},{3,251},{4,12},{5,253},{6,14},{7,255},{8,16},... | collective-permute-start | bytes 110600 | tf_op jit(solution)/shard_map/ppermute | solution.py:428
  47.6 2.9 %shard_map.97 = (f32[144,128]{1,0:T(8,128)}, f32[144,128]{1,0:T(8,128)}, f32[144,128]{1,0:T(8,128)}, f32[48,48]{1,0:T(8,128)}) custom-call(s32[1]{0:T(128)} %bitcast.c_ref, f32[8,128]{1,0:T(8,128)} %get-tuple-element.16.row_ref, f32[4,144,128]{2,1,0:T(8,128)} %get-tuple-element.17.y2_ref, f32[4,144,128]{2,1,0:T(8,128)} %get-tuple-element.18.w_ref, ...), custom_call_target="tpu_custom_call" | custom-call | tf_op jit(solution)/shard_map/pallas_call | solution.py:432
  50.5 0.0 collective-permute-done.10.in2_ref
  50.5 0.0 collective-permute-done.9.in1_ref
  50.5 0.0 copy-start.6
  50.5 0.6 copy-done.7
  51.1 0.0 copy-done.6
  51.2 2.7 %shard_map.98 = (f32[32,128]{1,0:T(8,128)}, f32[32,128]{1,0:T(8,128)}, f32[32,128]{1,0:T(8,128)}, f32[32,128]{1,0:T(8,128)}) custom-call(s32[1]{0:T(128)} %bitcast.c_ref, f32[144,128]{1,0:T(8,128)} %get-tuple-element.22.mine1_ref, f32[144,128]{1,0:T(8,128)} %get-tuple-element.23.mine2_ref, f32[144,128]{1,0:T(8,128)} %copy-done.6, f32[72,128]{1,0:T(8,128)} %copy-done.7), custom_call_target="tpu_custom_call" | custom-call | tf_op jit(solution)/shard_map/pallas_call | solution.py:445
  53.9 0.1 collective-permute-start.11
  54.0 5.1 %collective-permute-start.12 = (f32[32,128]{1,0:T(8,128)}, f32[32,128]{1,0:T(8,128)S(1)}, u32[]{:S(2)}, u32[]{:S(2)}) collective-permute-start(f32[32,128]{1,0:T(8,128)} %get-tuple-element.28), channel_id=1, source_target_pairs={{0,2},{1,3},{2,0},{3,1},{4,6},{5,7},{6,4},{7,5},{8,10},{9,11},{10,... | collective-permute-start | bytes 49160 | tf_op jit(solution)/shard_map/ppermute | solution.py:369
  59.0 0.1 collective-permute-start.13
  59.1 0.0 collective-permute-done.11.a_ref
  59.1 1.2 %collective-permute-done.12.b_ref = f32[32,128]{1,0:T(8,128)S(1)} collective-permute-done((f32[32,128]{1,0:T(8,128)}, f32[32,128]{1,0:T(8,128)S(1)}, u32[]{:S(2)}, u32[]{:S(2)}) %collective-permute-start.12) | collective-permute-done | bytes 16416 | tf_op jit(solution)/shard_map/ppermute | solution.py:369
  60.4 2.0 %collective-permute-done.13.d_ref = f32[32,128]{1,0:T(8,128)S(1)} collective-permute-done((f32[32,128]{1,0:T(8,128)}, f32[32,128]{1,0:T(8,128)S(1)}, u32[]{:S(2)}, u32[]{:S(2)}) %collective-permute-start.13) | collective-permute-done | bytes 16416 | tf_op jit(solution)/shard_map/ppermute | solution.py:369
  62.4 0.6 copy-done.13
  63.0 2.2 %shard_map.99 = f32[84,1,48]{2,1,0:T(1,128)} custom-call(s32[1]{0:T(128)} %bitcast.c_ref, f32[48,48]{1,0:T(8,128)} %get-tuple-element.21.center_ref, f32[32,128]{1,0:T(8,128)} %get-tuple-element.26.own_ref, f32[32,128]{1,0:T(8,128)} %copy-done.11, f32[32,128]{1,0:T(8,128)} %copy-done.12, f32[32,128]{1,0:T(8,128)} %copy-done.13), custom_call_target="tpu_custom_call" | custom-call | tf_op jit(solution)/shard_map/pallas_call | solution.py:458
  (13 shorter events, 0.0 us)
Async XLA Ops:
  0.6 5.3 %collective-permute-start.4 = (f32[243,1,128]{2,1,0:T(1,128)}, f32[243,1,128]{2,1,0:T(1,128)S(1)}, u32[]{:S(2)}, u32[]{:S(2)}) collective-permute-start(f32[243,1,128]{2,1,0:T(1,128)} %bitcast.18), channel_id=1, source_target_pairs={{0,2},{1,3},{2,0},{3,1},{4,6},{5,7},{6,4},{7,5},{8,10},{9,11},{10,... | collective-permute-start | bytes 373256 | tf_op jit(solution)/shard_map/ppermute | solution.py:369
  2.7 8.6 %collective-permute-start.1 = (f32[144,128]{1,0:T(8,128)}, f32[144,128]{1,0:T(8,128)S(1)}, u32[]{:S(2)}, u32[]{:S(2)}) collective-permute-start(f32[144,128]{1,0:T(8,128)} %bitcast.21), channel_id=1, source_target_pairs={{0,2},{1,3},{2,0},{3,1},{4,6},{5,7},{6,4},{7,5},{8,10},{9,11},{10,... | collective-permute-start | bytes 221192 | tf_op jit(solution)/shard_map/ppermute | solution.py:369
  2.9 14.0 %collective-permute-start.3 = (f32[243,1,128]{2,1,0:T(1,128)}, f32[243,1,128]{2,1,0:T(1,128)S(1)}, u32[]{:S(2)}, u32[]{:S(2)}) collective-permute-start(f32[243,1,128]{2,1,0:T(1,128)} %bitcast.19), channel_id=1, source_target_pairs={{0,1},{1,0},{2,3},{3,2},{4,5},{5,4},{6,7},{7,6},{8,9},{9,8},{10,11... | collective-permute-start | bytes 373256 | tf_op jit(solution)/shard_map/ppermute | solution.py:369
  5.9 10.9 %copy-start = (f32[243,1,128]{2,1,0:T(1,128)}, f32[243,1,128]{2,1,0:T(1,128)S(1)}, u32[]{:S(2)}) copy-start(f32[243,1,128]{2,1,0:T(1,128)S(1)} %collective-permute-done.4.v2) | copy-start | bytes 373252
  6.0 10.9 %collective-permute-start.5 = (f32[243,1,128]{2,1,0:T(1,128)S(1)}, f32[243,1,128]{2,1,0:T(1,128)S(1)}, u32[]{:S(2)}, u32[]{:S(2)}) collective-permute-start(f32[243,1,128]{2,1,0:T(1,128)S(1)} %collective-permute-done.4.v2), channel_id=1, source_target_pairs={{0,1},{1,0},{2,3},{3,2},{4,5},{5,4},{6,7},{7,6},{8,9},{9,8},{10,11... | collective-permute-start | bytes 373256 | tf_op jit(solution)/shard_map/ppermute | solution.py:369
  10.5 2.9 %collective-permute-start.7 = (f32[48,128]{1,0:T(8,128)}, f32[48,128]{1,0:T(8,128)S(1)}, u32[]{:S(2)}, u32[]{:S(2)}) collective-permute-start(f32[48,128]{1,0:T(8,128)} %shard_map.95.p0), channel_id=1, source_target_pairs={{0,2},{1,3},{2,0},{3,1},{4,6},{5,7},{6,4},{7,5},{8,10},{9,11},{10,... | collective-permute-start | bytes 73736 | tf_op jit(solution)/shard_map/ppermute | solution.py:369
  11.0 5.8 %collective-permute-start = (f32[144,128]{1,0:T(8,128)}, f32[144,128]{1,0:T(8,128)S(1)}, u32[]{:S(2)}, u32[]{:S(2)}) collective-permute-start(f32[144,128]{1,0:T(8,128)} %bitcast.22), channel_id=1, source_target_pairs={{0,1},{1,0},{2,3},{3,2},{4,5},{5,4},{6,7},{7,6},{8,9},{9,8},{10,11... | collective-permute-start | bytes 221192 | tf_op jit(solution)/shard_map/ppermute | solution.py:369
  11.3 5.6 %copy-start.3 = (f32[144,128]{1,0:T(8,128)}, f32[144,128]{1,0:T(8,128)S(1)}, u32[]{:S(2)}) copy-start(f32[144,128]{1,0:T(8,128)S(1)} %collective-permute-done.1.x2) | copy-start | bytes 221188
  11.3 5.5 %collective-permute-start.2 = (f32[144,128]{1,0:T(8,128)S(1)}, f32[144,128]{1,0:T(8,128)S(1)}, u32[]{:S(2)}, u32[]{:S(2)}) collective-permute-start(f32[144,128]{1,0:T(8,128)S(1)} %collective-permute-done.1.x2), channel_id=1, source_target_pairs={{0,1},{1,0},{2,3},{3,2},{4,5},{5,4},{6,7},{7,6},{8,9},{9,8},{10,11... | collective-permute-start | bytes 221192 | tf_op jit(solution)/shard_map/ppermute | solution.py:369
  13.4 3.5 %copy-start.8 = (f32[48,128]{1,0:T(8,128)}, f32[48,128]{1,0:T(8,128)S(1)}, u32[]{:S(2)}) copy-start(f32[48,128]{1,0:T(8,128)S(1)} %collective-permute-done.7.p2) | copy-start | bytes 73732
  13.4 2.2 %collective-permute-start.6 = (f32[48,128]{1,0:T(8,128)}, f32[48,128]{1,0:T(8,128)S(1)}, u32[]{:S(2)}, u32[]{:S(2)}) collective-permute-start(f32[48,128]{1,0:T(8,128)} %shard_map.95.p0), channel_id=1, source_target_pairs={{0,1},{1,0},{2,3},{3,2},{4,5},{5,4},{6,7},{7,6},{8,9},{9,8},{10,11... | collective-permute-start | bytes 73736 | tf_op jit(solution)/shard_map/ppermute | solution.py:369
  15.6 1.3 %copy-start.9 = (f32[48,128]{1,0:T(8,128)}, f32[48,128]{1,0:T(8,128)S(1)}, u32[]{:S(2)}) copy-start(f32[48,128]{1,0:T(8,128)S(1)} %collective-permute-done.6.p1) | copy-start | bytes 73732
  15.6 1.2 %collective-permute-start.8 = (f32[48,128]{1,0:T(8,128)S(1)}, f32[48,128]{1,0:T(8,128)S(1)}, u32[]{:S(2)}, u32[]{:S(2)}) collective-permute-start(f32[48,128]{1,0:T(8,128)S(1)} %collective-permute-done.7.p2), channel_id=1, source_target_pairs={{0,1},{1,0},{2,3},{3,2},{4,5},{5,4},{6,7},{7,6},{8,9},{9,8},{10,11... | collective-permute-start | bytes 73736 | tf_op jit(solution)/shard_map/ppermute | solution.py:369
  16.8 0.6 copy-start.10
  16.8 0.6 copy-start.4
  16.9 0.7 %copy-start.1 = (f32[243,1,128]{2,1,0:T(1,128)}, f32[243,1,128]{2,1,0:T(1,128)S(1)}, u32[]{:S(2)}) copy-start(f32[243,1,128]{2,1,0:T(1,128)S(1)} %collective-permute-done.3.v1) | copy-start | bytes 373252
  16.9 0.7 %copy-start.5 = (f32[144,128]{1,0:T(8,128)}, f32[144,128]{1,0:T(8,128)S(1)}, u32[]{:S(2)}) copy-start(f32[144,128]{1,0:T(8,128)S(1)} %collective-permute-done.2.x3) | copy-start | bytes 221188
  17.5 0.7 %copy-start.2 = (f32[243,1,128]{2,1,0:T(1,128)}, f32[243,1,128]{2,1,0:T(1,128)S(1)}, u32[]{:S(2)}) copy-start(f32[243,1,128]{2,1,0:T(1,128)S(1)} %collective-permute-done.5.v3) | copy-start | bytes 373252
  37.8 12.8 %collective-permute-start.9 = (f32[144,128]{1,0:T(8,128)}, f32[144,128]{1,0:T(8,128)S(1)}, u32[]{:S(2)}, u32[]{:S(2)}) collective-permute-start(f32[144,128]{1,0:T(8,128)} %get-tuple-element.24), channel_id=1, source_target_pairs={{0,14},{1,7},{2,244},{3,253},{4,18},{5,11},{6,248},{7,1},{8,22},{9... | collective-permute-start | bytes 221192 | tf_op jit(solution)/shard_map/ppermute | solution.py:428
  39.6 10.9 %collective-permute-start.10 = (f32[72,128]{1,0:T(8,128)}, f32[72,128]{1,0:T(8,128)S(1)}, u32[]{:S(2)}, u32[]{:S(2)}) collective-permute-start(f32[72,128]{1,0:T(8,128)} %get-tuple-element.25), channel_id=1, source_target_pairs={{0,8},{1,249},{2,10},{3,251},{4,12},{5,253},{6,14},{7,255},{8,16},... | collective-permute-start | bytes 110600 | tf_op jit(solution)/shard_map/ppermute | solution.py:428
  50.5 0.6 copy-start.7
  50.5 0.6 copy-start.6
  53.9 5.2 %collective-permute-start.11 = (f32[32,128]{1,0:T(8,128)}, f32[32,128]{1,0:T(8,128)S(1)}, u32[]{:S(2)}, u32[]{:S(2)}) collective-permute-start(f32[32,128]{1,0:T(8,128)} %get-tuple-element.27), channel_id=1, source_target_pairs={{0,1},{1,0},{2,3},{3,2},{4,5},{5,4},{6,7},{7,6},{8,9},{9,8},{10,11... | collective-permute-start | bytes 49160 | tf_op jit(solution)/shard_map/ppermute | solution.py:369
  54.0 6.4 %collective-permute-start.12 = (f32[32,128]{1,0:T(8,128)}, f32[32,128]{1,0:T(8,128)S(1)}, u32[]{:S(2)}, u32[]{:S(2)}) collective-permute-start(f32[32,128]{1,0:T(8,128)} %get-tuple-element.28), channel_id=1, source_target_pairs={{0,2},{1,3},{2,0},{3,1},{4,6},{5,7},{6,4},{7,5},{8,10},{9,11},{10,... | collective-permute-start | bytes 49160 | tf_op jit(solution)/shard_map/ppermute | solution.py:369
  59.0 3.4 %collective-permute-start.13 = (f32[32,128]{1,0:T(8,128)}, f32[32,128]{1,0:T(8,128)S(1)}, u32[]{:S(2)}, u32[]{:S(2)}) collective-permute-start(f32[32,128]{1,0:T(8,128)} %get-tuple-element.29), channel_id=1, source_target_pairs={{0,3},{1,2},{2,1},{3,0},{4,7},{5,6},{6,5},{7,4},{8,11},{9,10},{10,... | collective-permute-start | bytes 49160 | tf_op jit(solution)/shard_map/ppermute | solution.py:369
  59.1 3.3 %copy-start.11 = (f32[32,128]{1,0:T(8,128)}, f32[32,128]{1,0:T(8,128)S(1)}, u32[]{:S(2)}) copy-start(f32[32,128]{1,0:T(8,128)S(1)} %collective-permute-done.11.a_ref) | copy-start | bytes 49156
  60.4 2.0 %copy-start.12 = (f32[32,128]{1,0:T(8,128)}, f32[32,128]{1,0:T(8,128)S(1)}, u32[]{:S(2)}) copy-start(f32[32,128]{1,0:T(8,128)S(1)} %collective-permute-done.12.b_ref) | copy-start | bytes 49156
  62.4 0.6 copy-start.13

commit v3 on v2

--- a/solution.py
+++ b/solution.py
@@ -15,7 +15,7 @@
 SCALE = float(LANES * NC // OVD)
 TILES = V // 8
 
-COL0 = 0
+COL0 = 3 * V
 PIV0 = COL0 + NB
 SEND0 = PIV0 + 3
 RECV0 = SEND0 + SLOTS
@@ -38,11 +38,23 @@
     return pl.BlockSpec(memory_space=pltpu.SMEM)
 
 
-def whole():
-    return pl.BlockSpec(memory_space=pl.ANY)
-
-
-def pack_kernel(c_ref, ov_ref, col_ref, cnt_ref, piv_ref, send_ref, recv_ref, out_ref):
+LIMIT = pltpu.CompilerParams(vmem_limit_bytes=40 * 2**20)
+
+
+def near(array):
+    return pltpu.with_memory_space_constraint(array, pltpu.VMEM)
+
+
+class Blocks:
+    def __init__(self, refs):
+        self.refs = refs
+
+    def __getitem__(self, at):
+        return self.refs[at[0]][at[1:]]
+
+
+def pack_kernel(c_ref, ov_ref, x_ref, col_ref, cnt_ref, piv_ref, send_ref, recv_ref, out_ref):
+    out_ref[0 : 3 * V, :] = x_ref[...]
     count = cnt_ref[...]
     for k in range(NB):
         out_ref[COL0 + k : COL0 + k + 1, :] = jnp.where(k < count, col_ref[k].astype(F32), -1.0)
@@ -60,14 +72,6 @@
         out_ref[LIVE0 + o : LIVE0 + o + 1, :] = jnp.where(alive, 1.0, 0.0).astype(F32)
 
 
-def fetch(pairs, sem):
-    copies = [pltpu.make_async_copy(src, dst, sem.at[n]) for n, (src, dst) in enumerate(pairs)]
-    for copy in copies:
-        copy.start()
-    for copy in copies:
-        copy.wait()
-
-
 def entry(table, c):
     value = jnp.int32(table[0])
     for n in range(1, NC):
@@ -97,7 +101,7 @@
 
 
 def value_row(val_ref, rc, ab, k):
-    return wide(val_ref[rc, ab * NB + k])
+    return wide(val_ref[rc, ab * NB + k, :, :])
 
 
 def add_block(val, dst_ref, rc, pick_of):
@@ -110,8 +114,8 @@
             )
 
 
-def lane_block(val_ref, small_ref, src_ref, dst_ref, rc, k):
-    col = wide(small_ref[rc, pl.ds(COL0 + k, 1), :]).astype(jnp.int32)
+def lane_block(val_ref, cols_ref, src_ref, dst_ref, rc, k):
+    col = wide(cols_ref[rc, pl.ds(k, 1), :]).astype(jnp.int32)
     val = [jnp.where(col >= 0, value_row(val_ref, rc, ab, k), 0.0) for ab in range(9)]
     index = col & (LANES - 1)
     odd = (col & LANES) != 0
@@ -124,11 +128,11 @@
     add_block(val, dst_ref, rc, pick_of)
 
 
-def one_hot(small_ref, oh_ref, k):
+def one_hot(cols_ref, oh_ref, k):
     half = 2 * LANES
     place = lax.broadcasted_iota(jnp.int32, (half, half), 0).astype(F32).astype(BF16)
     for m in range(2):
-        col = jnp.concatenate([small_ref[2 * m + n, pl.ds(COL0 + k, 1), :] for n in range(2)], axis=1)
+        col = jnp.concatenate([cols_ref[2 * m + n, pl.ds(k, 1), :] for n in range(2)], axis=1)
         for h in range(2):
             local = col - float(h * half)
             local = jnp.where((local >= 0.0) & (local < float(half)), local, -1.0)
@@ -142,9 +146,7 @@
     for q in range(NC):
         at = slice(q * LANES, q * LANES + LANES)
         value = src_ref[q, 0 : 3 * V, :]
-        high = value.astype(BF16)
-        x_ref[0 : 3 * V, at] = high
-        x_ref[3 * V :, at] = (value - high.astype(F32)).astype(BF16)
+        x_ref[0 : 3 * V, at], x_ref[3 * V :, at] = halves(value)
 
 
 def issue(x_ref, oh_ref, t_ref, k, parity):
@@ -166,12 +168,36 @@
     return jnp.concatenate([ref[q, a * V : a * V + V, :] for a in range(3) for q in range(NC)], axis=1)
 
 
-def gram_to(m_ref, block):
-    gram = lax.dot_general(block, block, (((1,), (1,)), ((), ())), precision=HIGH, preferred_element_type=F32)
+NT = (((1,), (1,)), ((), ()))
+
+
+def gram_to(m_ref, x_ref):
+    total = jnp.zeros((2 * V, V), F32)
+    for b in range(3):
+        high = x_ref[b * V : b * V + V, :]
+        both = jnp.concatenate([high, x_ref[(3 + b) * V : (4 + b) * V, :]], axis=0)
+        total = total + lax.dot_general(both, high, NT, preferred_element_type=F32)
+    low = total[V:, :]
+    gram = total[:V, :] + low + low.T
     row = lax.broadcasted_iota(jnp.int32, (V, 64), 0)
     lane = lax.broadcasted_iota(jnp.int32, (V, 64), 1)
     eye = jnp.where(row == lane, 1.0, 0.0).astype(F32)
     m_ref[:V, :] = jnp.concatenate([eye, gram, jnp.zeros((V, LANES - 64 - V), F32)], axis=1)
+
+
+def halves(value):
+    high = value.astype(BF16)
+    return high, (value - high.astype(F32)).astype(BF16)
+
+
+def mix(linv, value):
+    left, left_low = halves(linv)
+    right, right_low = halves(value)
+    return jnp.dot(
+        jnp.concatenate([left, left, left_low], axis=1),
+        jnp.concatenate([right, right_low, right], axis=0),
+        preferred_element_type=F32,
+    )
 
 
 CHOL = 3
@@ -209,7 +235,7 @@
 
 
 def solve_to(dst_ref, linv, src_ref):
-    out = jnp.dot(linv, flat(src_ref), precision=HIGH, preferred_element_type=F32)
+    out = mix(linv, flat(src_ref))
     for a in range(3):
         for q in range(NC):
             at = (a * NC + q) * LANES
@@ -235,27 +261,27 @@
 
 
 def main_kernel(
-    c_ref, x0, x1, x2, x3, v0, v1, v2, v3, p0, p1, p2, p3,
+    c_ref, p0, p1, p2, p3, v0, v1, v2, v3,
     y2_ref, w_ref, linv_ref, s1_ref, s2_ref, row_ref,
-    in_ref, val_ref, small_ref, sem, y_ref, z_ref, m_ref, col_ref, g_ref, x_ref, oh_ref, t_ref,
+    y_ref, z_ref, m_ref, col_ref, g_ref, x_ref, oh_ref, t_ref, cols_ref,
 ):
     c = c_ref[0]
-    fetch(
-        [(ref, dst.at[m]) for refs, dst in (((x0, x1, x2, x3), in_ref), ((v0, v1, v2, v3), val_ref), ((p0, p1, p2, p3), small_ref)) for m, ref in enumerate(refs)],
-        sem,
-    )
+    small_ref = Blocks((p0, p1, p2, p3))
+    val_ref = Blocks((v0, v1, v2, v3))
     for m in range(NC):
         col = small_ref[m, COL0 : COL0 + NB, :]
         local = (col.astype(jnp.int32) ^ (c * LANES)).astype(F32)
-        small_ref[m, COL0 : COL0 + NB, :] = jnp.where(col < 0.0, -1.0, local)
+        cols_ref[m, 0:NB, :] = jnp.where(col < 0.0, -1.0, local)
     m_ref[V:, :] = jnp.zeros((8, LANES), F32)
 
     def loop(src_ref, dst_ref, first):
-        start_op(small_ref, src_ref, dst_ref)
         split_to(x_ref, src_ref)
         if first:
-            one_hot(small_ref, oh_ref, 0)
-            one_hot(small_ref, oh_ref, 1)
+            one_hot(cols_ref, oh_ref, 0)
+            one_hot(cols_ref, oh_ref, 1)
+        else:
+            gram_to(m_ref, x_ref)
+        start_op(small_ref, src_ref, dst_ref)
         issue(x_ref, oh_ref, t_ref, 0, 0)
 
         def step(it, carry):
@@ -263,9 +289,9 @@
                 k = UN * it + u
                 issue(x_ref, oh_ref, t_ref, jnp.minimum(k + 1, ONE - 1), (u + 1) % 2)
                 for rc in (2 * (u % 2), 2 * (u % 2) + 1):
-                    lane_block(val_ref, small_ref, src_ref, dst_ref, rc, ONE + (UN // 2) * it + u // 2)
+                    lane_block(val_ref, cols_ref, src_ref, dst_ref, rc, ONE + (UN // 2) * it + u // 2)
                 if first:
-                    one_hot(small_ref, oh_ref, jnp.minimum(k + 2, ONE - 1))
+                    one_hot(cols_ref, oh_ref, jnp.minimum(k + 2, ONE - 1))
                 else:
                     factor_piece(m_ref, col_ref, k * CHOL)
                 take(val_ref, dst_ref, t_ref, k, u % 2)
@@ -273,11 +299,9 @@
 
         lax.fori_loop(0, ONE // UN, step, 0)
 
-    loop(in_ref, y_ref, True)
-    gram_to(m_ref, flat(y_ref))
+    loop(small_ref, y_ref, True)
     loop(y_ref, z_ref, False)
     solve_to(y2_ref, inverse_of(m_ref), z_ref)
-    gram_to(m_ref, flat(y2_ref))
     loop(y2_ref, w_ref, False)
     linv = inverse_of(m_ref)
     linv_ref[...] = linv
@@ -292,7 +316,7 @@
         for at, piece in zip(tiles, rows_of(w_ref, index, tiles, c)):
             g_ref[n, at, :] = piece
     both = jnp.concatenate([g_ref[n, a * V : a * V + V, :] for n in range(2) for a in range(3)], axis=1)
-    image = jnp.dot(linv, both, precision=HIGH, preferred_element_type=F32)
+    image = mix(linv, both)
     for a in range(3):
         s1_ref[a * V : a * V + V, :] = image[:, a * LANES : a * LANES + LANES]
         g_ref[1, a * V : a * V + V, :] = image[:, (3 + a) * LANES : (4 + a) * LANES]
@@ -310,22 +334,20 @@
         live = wide(row_ref[2 * n + 1 : 2 * n + 2, :])
         for at, piece in zip(tiles, rows_of(q_ref, index, tiles, c)):
             out_ref[at, :] = piece * live
-    image = jnp.dot(linv, flat(w_ref), precision=HIGH, preferred_element_type=F32)
+    image = mix(linv, flat(w_ref))
     center_ref[...] = lax.dot_general(
-        flat(q_ref), image, (((1,), (1,)), ((), ())), precision=HIGH, preferred_element_type=F32
+        flat(q_ref), image, NT, precision=HIGH, preferred_element_type=F32
     )
 
 
-def coarse_kernel(c_ref, mine1_ref, mine2_ref, in1_ref, in2_ref, own_ref, a_ref, b_ref, d_ref, r_ref, got1_ref, got2_ref, sem):
+def coarse_kernel(c_ref, mine1_ref, mine2_ref, got1_ref, got2_ref, own_ref, a_ref, b_ref, d_ref, r_ref):
     c = c_ref[0]
-    fetch([(in1_ref, got1_ref), (in2_ref, got2_ref)], sem)
 
     def side(ref, count):
         return jnp.concatenate([ref[a * count : a * count + count, :] for a in range(3)], axis=1)
 
-    nt = (((1,), (1,)), ((), ()))
-    one = lax.dot_general(side(mine1_ref, V), side(got1_ref, V), nt, precision=HIGH, preferred_element_type=F32) * SCALE
-    two = lax.dot_general(side(mine2_ref, V), side(got2_ref, V // 2), nt, precision=HIGH, preferred_element_type=F32) * SCALE
+    one = lax.dot_general(side(mine1_ref, V), side(got1_ref, V), NT, precision=HIGH, preferred_element_type=F32) * SCALE
+    two = lax.dot_general(side(mine2_ref, V), side(got2_ref, V // 2), NT, precision=HIGH, preferred_element_type=F32) * SCALE
     part = V // NC
     for d in range(NC):
         r_ref[d, 0:part, 0:V] = one[d * part : d * part + part, :]
@@ -336,10 +358,11 @@
     d_ref[...] = r_ref[c ^ 3]
 
 
-def join_kernel(c_ref, center_ref, own_ref, a_ref, b_ref, d_ref, out_ref, r_ref, sem):
+def join_kernel(c_ref, center_ref, own_ref, a_ref, b_ref, d_ref, out_ref, r_ref):
     c = c_ref[0]
     part = V // NC
-    fetch([(ref, r_ref.at[m]) for m, ref in enumerate((own_ref, a_ref, b_ref, d_ref))], sem)
+    for m, ref in enumerate((own_ref, a_ref, b_ref, d_ref)):
+        r_ref[m] = ref[...]
 
     def put(place, value):
         for v in range(part):
@@ -360,7 +383,7 @@
 
 
 def shards(test_vectors, ell_values, ell_cols, ell_count, pivot, send_rows, recv_rows, ov_count):
-    shape = jax.ShapeDtypeStruct
+    shape = pltpu.VMEM
     c = lax.axis_index("crow").astype(jnp.int32).reshape(1)
     x = jnp.transpose(test_vectors[0], (1, 0, 2)).reshape(3 * V, LANES)
     values = ell_values.reshape(9 * NB, 1, LANES)
@@ -368,25 +391,26 @@
     def pass_on(piece, m):
         return lax.ppermute(piece, "crow", [(n, n ^ m) for n in range(NC)])
 
-    far_x = pass_on(x, 2)
     far_v = pass_on(values, 2)
-    small = pl.pallas_call(
+    packed = pl.pallas_call(
         pack_kernel,
         out_shape=shape((PACKED, LANES), F32),
-        in_specs=[smem(), smem()] + [vmem()] * 5,
+        in_specs=[smem(), smem()] + [vmem()] * 6,
         out_specs=vmem(),
+        compiler_params=LIMIT,
     )(
         c,
         ov_count.reshape(SLOTS),
+        x,
         ell_cols.reshape(NB, 1, LANES),
         ell_count.reshape(1, LANES),
         pivot.reshape(3, 1, LANES),
         send_rows.reshape(SLOTS, 1, OVD),
         recv_rows.reshape(SLOTS, 1, OVD),
     )
-    far_s = pass_on(small, 2)
+    far_p = pass_on(packed, 2)
     blocks = []
-    for own, far in ((x, far_x), (values, far_v), (small, far_s)):
+    for own, far in ((packed, far_p), (values, far_v)):
         blocks += [own, pass_on(own, 1), far, pass_on(far, 1)]
     block = (NC, 3 * V, LANES)
     y2, w, linv, s1, s2, row = pl.pallas_call(
@@ -399,13 +423,9 @@
             shape((3 * V // 2, LANES), F32),
             shape((8, LANES), F32),
         ),
-        in_specs=[smem()] + [whole()] * 12,
+        in_specs=[smem()] + [vmem()] * 8,
         out_specs=(vmem(),) * 6,
         scratch_shapes=[
-            pltpu.VMEM(block, F32),
-            pltpu.VMEM((NC, 9 * NB, 1, LANES), F32),
-            pltpu.VMEM((NC, PACKED, LANES), F32),
-            pltpu.SemaphoreType.DMA((12,)),
             pltpu.VMEM(block, F32),
             pltpu.VMEM(block, F32),
             pltpu.VMEM((V + 8, LANES), F32),
@@ -414,8 +434,10 @@
             pltpu.VMEM((6 * V, NC * LANES), BF16),
             pltpu.VMEM((2, ONE, NC * LANES, 2 * LANES), BF16),
             pltpu.VMEM((2, 2, 3 * V, 2 * LANES), F32),
+            pltpu.VMEM((NC, 32, LANES), F32),
         ],
-    )(c, *blocks)
+        compiler_params=LIMIT,
+    )(c, *map(near, blocks))
 
     size = lax.axis_size("sub")
 
@@ -432,7 +454,7 @@
     basis, mine1, mine2, center = pl.pallas_call(
         middle_kernel,
         out_shape=(
-            shape((3 * V, LANES), F32),
+            jax.ShapeDtypeStruct((3 * V, LANES), F32),
             shape((3 * V, LANES), F32),
             shape((3 * V, LANES), F32),
             shape((V, V), F32),
@@ -440,28 +462,26 @@
         in_specs=[smem()] + [vmem()] * 4,
         out_specs=(vmem(),) * 4,
         scratch_shapes=[pltpu.VMEM(block, F32)],
-    )(c, row, y2, w, linv)
+        compiler_params=LIMIT,
+    )(c, *map(near, (row, y2, w, linv)))
     slab = shape((32, LANES), F32)
     own, to1, to2, to3 = pl.pallas_call(
         coarse_kernel,
         out_shape=(slab,) * 4,
-        in_specs=[smem()] + [vmem()] * 2 + [whole()] * 2,
+        in_specs=[smem()] + [vmem()] * 4,
         out_specs=(vmem(),) * 4,
-        scratch_shapes=[
-            pltpu.VMEM((NC, 32, LANES), F32),
-            pltpu.VMEM((3 * V, LANES), F32),
-            pltpu.VMEM((3 * V // 2, LANES), F32),
-            pltpu.SemaphoreType.DMA((2,)),
-        ],
-    )(c, mine1, mine2, got1, got2)
+        scratch_shapes=[pltpu.VMEM((NC, 32, LANES), F32)],
+        compiler_params=LIMIT,
+    )(c, *map(near, (mine1, mine2, got1, got2)))
     got = [pass_on(t, m) for m, t in ((1, to1), (2, to2), (3, to3))]
     coarse = pl.pallas_call(
         join_kernel,
-        out_shape=shape(((2 * RADIUS + 1) * (V // NC), 1, V), F32),
-        in_specs=[smem(), vmem()] + [whole()] * 4,
+        out_shape=jax.ShapeDtypeStruct(((2 * RADIUS + 1) * (V // NC), 1, V), F32),
+        in_specs=[smem()] + [vmem()] * 5,
         out_specs=vmem(),
-        scratch_shapes=[pltpu.VMEM((NC, 32, LANES), F32), pltpu.SemaphoreType.DMA((4,))],
-    )(c, center, own, *got)
+        scratch_shapes=[pltpu.VMEM((NC, 32, LANES), F32)],
+        compiler_params=LIMIT,
+    )(c, *map(near, (center, own, *got)))
     coarse = coarse.reshape(2 * RADIUS + 1, V // NC, V)
     basis = jnp.transpose(basis.reshape(3, V, LANES), (1, 0, 2))
     return basis[None], coarse[None]

time: 65.8 us -> 54.4 us (0.83)
  Pallas kernels: 28.9 us -> 19.6 us
  waiting for transfers between devices: 7.09 us -> 4.03 us
  local copies, waits for them, and re-layouts: 2.52 us -> 4.96 us
  starting transfers between devices: 26 us -> 24.8 us
    pallas_call x2, Pallas kernels: 5.12 us -> 1.9 us  [the longest x1 1.18 us: shards(): pl.pallas_call(middle_kernel, out_shape=(jax.ShapeDtypeStruct((3 * V, LAN...]
    ppermute x12 -> x9, waiting for transfers between devices: 7.09 us -> 4.03 us  [pass_on(): return lax.ppermute(piece, 'crow', [(n, n ^ m) for n in range(NC)])]
    pallas_call x1, Pallas kernels: 19.5 us -> 16.8 us  [shards(): pl.pallas_call(main_kernel, out_shape=(shape(block, F32), shape(block, F3...]
    pallas_call x1, Pallas kernels: 2.72 us -> 0.28 us  [shards(): pl.pallas_call(coarse_kernel, out_shape=(slab,) * 4, in_specs=[smem()] +...]
    unnamed x28 -> x16, local copies, waits for them, and re-layouts: 2.52 us -> 4.96 us
    ppermute x12 -> x9, starting transfers between devices: 16.1 us -> 15.1 us  [pass_on(): return lax.ppermute(piece, 'crow', [(n, n ^ m) for n in range(NC)])]
    pallas_call x1, Pallas kernels: 1.51 us -> 0.64 us  [shards(): pl.pallas_call(pack_kernel, out_shape=shape((PACKED, LANES), F32), in_spe...]
  transfers between devices with their start and end apart: 14 -> 11, of which waited for: 5 -> 3; matrix products, arithmetic and copies ran while one was open for 0% -> 0% of each run, Pallas kernels for 7% -> 3%
where the time goes in v3:
time: 54.4 us; the launch traced here: 54.1 us
  starting transfers between devices  24.8 us (46%)
  Pallas kernels  19.6 us (36%)
  local copies, waits for them, and re-layouts  4.96 us (9%)
  waiting for transfers between devices  4.03 us (7%)
  between operations  0.68 us (1%)
    pallas_call x1, Pallas kernels, shards(): pl.pallas_call(main_kernel, out_shape=(shape(block, F32), shape(block, F3...  16.8 us
    ppermute x9, starting transfers between devices, pass_on(): return lax.ppermute(piece, 'crow', [(n, n ^ m) for n in range(NC)])  15.1 us
    ppermute x2, starting transfers between devices, across(): return lax.ppermute(piece, ('sub', 'crow'), pairs)  9.7 us
    unnamed x16, local copies, waits for them, and re-layouts  4.96 us
    ppermute x9, waiting for transfers between devices, pass_on(): return lax.ppermute(piece, 'crow', [(n, n ^ m) for n in range(NC)])  4.03 us
    pallas_call x1, Pallas kernels, shards(): pl.pallas_call(middle_kernel, out_shape=(jax.ShapeDtypeStruct((3 * V, LAN...  1.18 us
  transfers between devices with their start and end apart: 11, of which 3 were waited for; matrix products, arithmetic and copies ran while one was open for 0% of the time, Pallas kernels for 3%

profile of v3, /device:TPU:1, one launch (start us, length us, event | category | flops | bytes accessed | tf_op | source)
XLA Modules:
  0.0 54.1 jit_solution(15064128861080118460)
XLA Ops:
  0.6 0.0 copy-start
  0.6 2.1 %collective-permute-start.4 = (f32[243,1,128]{2,1,0:T(1,128)}, f32[243,1,128]{2,1,0:T(1,128)S(1)}, u32[]{:S(2)}, u32[]{:S(2)}) collective-permute-start(f32[243,1,128]{2,1,0:T(1,128)} %bitcast.18), channel_id=1, source_target_pairs={{0,2},{1,3},{2,0},{3,1},{4,6},{5,7},{6,4},{7,5},{8,10},{9,11},{10,... | collective-permute-start | bytes 373256 | tf_op jit(solution)/shard_map/ppermute | solution.py:392
  2.8 0.0 copy-start.1
  2.8 0.9 %copy-done.1 = f32[1,48,3,128]{3,1,2,0:T(8,128)S(1)} copy-done((f32[1,48,3,128]{3,1,2,0:T(8,128)S(1)}, f32[1,48,3,128]{3,1,2,0:T(8,128)}, u32[]{:S(2)}) %copy-start.1) | copy-done | bytes 73752
  3.6 0.0 copy-start.2
  3.6 0.7 %copy-done.2 = s32[1,27,128]{2,0,1:T(1,128)S(1)} copy-done((s32[1,27,128]{2,0,1:T(1,128)S(1)}, s32[1,27,128]{2,0,1:T(1,128)}, u32[]{:S(2)}) %copy-start.2) | copy-done | bytes 13848
  4.4 0.0 copy-start.3
  4.4 0.7 %copy-done.3 = s32[1,6,32]{2,0,1:T(1,128)S(1)} copy-done((s32[1,6,32]{2,0,1:T(1,128)S(1)}, s32[1,6,32]{2,0,1:T(1,128)}, u32[]{:S(2)}) %copy-start.3) | copy-done | bytes 792
  5.0 0.0 copy-start.4
  5.0 0.7 %copy-done.4 = s32[1,6,32]{2,0,1:T(1,128)S(1)} copy-done((s32[1,6,32]{2,0,1:T(1,128)S(1)}, s32[1,6,32]{2,0,1:T(1,128)}, u32[]{:S(2)}) %copy-start.4) | copy-done | bytes 792
  5.7 0.0 copy-start.5
  5.7 0.7 %copy-done.5 = f32[1,3,128]{2,0,1:T(1,128)S(1)} copy-done((f32[1,3,128]{2,0,1:T(1,128)S(1)}, f32[1,3,128]{2,0,1:T(1,128)}, u32[]{:S(2)}) %copy-start.5) | copy-done | bytes 1560
  6.4 0.0 copy-start.6
  6.4 0.7 %copy-done.6 = s32[1,6,1]{1,2,0:T(1,128)S(1)} copy-done((s32[1,6,1]{1,2,0:T(1,128)S(1)}, s32[1,6,1]{1,2,0:T(1,128)}, u32[]{:S(2)}) %copy-start.6) | copy-done | bytes 48
  7.1 0.0 copy-start.7
  7.1 0.7 %copy-done.7 = s32[1,128]{1,0:T(1,128)S(1)} copy-done((s32[1,128]{1,0:T(1,128)S(1)}, s32[1,128]{1,0:T(1,128)}, u32[]{:S(2)}) %copy-start.7) | copy-done | bytes 536
  7.7 0.6 %shard_map.95.p0 = f32[192,128]{1,0:T(8,128)S(1)} custom-call(s32[1]{0:T(128)} %bitcast.c_ref, s32[6]{0:T(128)S(1)} %bitcast.26, f32[144,128]{1,0:T(8,128)S(1)} %bitcast.21, s32[27,1,128]{2,1,0:T(1,128)S(1)} %bitcast.22, s32[1,128]{1,0:T(1,128)S(1)} %copy-done.7, f32[3,1,128]{2,1,0:T(1,128)S(1)} %bitcast.25, s32[6,1,32]{2,1,0:T(1,128)S(1)} %bitcast.23, ...), custom_call_target="tpu_custom_call" | custom-call | tf_op jit(solution)/shard_map/pallas_call | solution.py:395
  8.4 0.1 collective-permute-start.1
  8.5 0.0 copy-done
  8.5 3.2 %collective-permute-start.3 = (f32[243,1,128]{2,1,0:T(1,128)S(1)}, f32[243,1,128]{2,1,0:T(1,128)S(1)}, u32[]{:S(2)}, u32[]{:S(2)}) collective-permute-start(f32[243,1,128]{2,1,0:T(1,128)S(1)} %bitcast.19), channel_id=1, source_target_pairs={{0,1},{1,0},{2,3},{3,2},{4,5},{5,4},{6,7},{7,6},{8,9},{9,8},{10,11... | collective-permute-start | bytes 373256 | tf_op jit(solution)/shard_map/ppermute | solution.py:392
  11.7 0.0 collective-permute-done.4.v2
  11.7 0.1 collective-permute-start.5
  11.8 0.4 collective-permute-start
  12.2 0.0 collective-permute-done.1.p2
  12.2 2.1 %collective-permute-start.2 = (f32[192,128]{1,0:T(8,128)S(1)}, f32[192,128]{1,0:T(8,128)S(1)}, u32[]{:S(2)}, u32[]{:S(2)}) collective-permute-start(f32[192,128]{1,0:T(8,128)S(1)} %collective-permute-done.1.p2), channel_id=1, source_target_pairs={{0,1},{1,0},{2,3},{3,2},{4,5},{5,4},{6,7},{7,6},{8,9},{9,8},{10,11... | collective-permute-start | bytes 294920 | tf_op jit(solution)/shard_map/ppermute | solution.py:392
  14.3 0.0 collective-permute-done.p1
  14.3 0.0 collective-permute-done.3.v1
  14.3 0.9 %collective-permute-done.2.p3 = f32[192,128]{1,0:T(8,128)S(1)} collective-permute-done((f32[192,128]{1,0:T(8,128)S(1)}, f32[192,128]{1,0:T(8,128)S(1)}, u32[]{:S(2)}, u32[]{:S(2)}) %collective-permute-start.2) | collective-permute-done | bytes 98336 | tf_op jit(solution)/shard_map/ppermute | solution.py:392
  15.2 0.0 collective-permute-done.5.v3
  15.2 16.8 %shard_map.96 = (f32[4,144,128]{2,1,0:T(8,128)S(1)}, f32[4,144,128]{2,1,0:T(8,128)S(1)}, f32[48,48]{1,0:T(8,128)S(1)}, f32[144,128]{1,0:T(8,128)S(1)}, f32[72,128]{1,0:T(8,128)S(1)}, /*index=5*/f32[8,128]{1,0:T(8,128)S(1)}) custom-call(s32[1]{0:T(128)} %bitcast.c_ref, f32[192,128]{1,0:T(8,128)S(1)} %shard_map.95.p0, f32[192,128]{1,0:T(8,128)S(1)} %collective-permute-done.p1, ...), custom_call_target="tpu_custom_call" | custom-call | tf_op jit(solution)/shard_map/pallas_call | solution.py:416
  32.0 1.7 %collective-permute-start.6 = (f32[144,128]{1,0:T(8,128)S(1)}, f32[144,128]{1,0:T(8,128)S(1)}, u32[]{:S(2)}, u32[]{:S(2)}) collective-permute-start(f32[144,128]{1,0:T(8,128)S(1)} %get-tuple-element.24), channel_id=1, source_target_pairs={{0,14},{1,7},{2,244},{3,253},{4,18},{5,11},{6,248},{7,1},{8,22},{9... | collective-permute-start | bytes 221192 | tf_op jit(solution)/shard_map/ppermute | solution.py:450
  33.7 8.0 %collective-permute-start.7 = (f32[72,128]{1,0:T(8,128)S(1)}, f32[72,128]{1,0:T(8,128)S(1)}, u32[]{:S(2)}, u32[]{:S(2)}) collective-permute-start(f32[72,128]{1,0:T(8,128)S(1)} %get-tuple-element.25), channel_id=1, source_target_pairs={{0,8},{1,249},{2,10},{3,251},{4,12},{5,253},{6,14},{7,255},{8,16},... | collective-permute-start | bytes 110600 | tf_op jit(solution)/shard_map/ppermute | solution.py:450
  41.7 1.2 %shard_map.97 = (f32[144,128]{1,0:T(8,128)}, f32[144,128]{1,0:T(8,128)S(1)}, f32[144,128]{1,0:T(8,128)S(1)}, f32[48,48]{1,0:T(8,128)S(1)}) custom-call(s32[1]{0:T(128)} %bitcast.c_ref, f32[8,128]{1,0:T(8,128)S(1)} %get-tuple-element.16.row_ref, f32[4,144,128]{2,1,0:T(8,128)S(1)} %get-tuple-element.17.y2_ref, f32[4,144,128]{2,1,0:T(8,128)S(1)} %get-tuple-element.18.w_ref, ...), custom_call_target="tpu_custom_call" | custom-call | tf_op jit(solution)/shard_map/pallas_call | solution.py:454
  42.9 0.0 collective-permute-done.7.got2_ref
  42.9 0.0 collective-permute-done.6.got1_ref
  42.9 0.3 shard_map.98
  43.2 0.4 collective-permute-start.8
  43.6 6.6 %collective-permute-start.9 = (f32[32,128]{1,0:T(8,128)S(1)}, f32[32,128]{1,0:T(8,128)S(1)}, u32[]{:S(2)}, u32[]{:S(2)}) collective-permute-start(f32[32,128]{1,0:T(8,128)S(1)} %get-tuple-element.28), channel_id=1, source_target_pairs={{0,2},{1,3},{2,0},{3,1},{4,6},{5,7},{6,4},{7,5},{8,10},{9,11},{10,... | collective-permute-start | bytes 49160 | tf_op jit(solution)/shard_map/ppermute | solution.py:392
  50.2 0.1 collective-permute-start.10
  50.3 0.0 collective-permute-done.8.a_ref
  50.3 1.0 %collective-permute-done.9.b_ref = f32[32,128]{1,0:T(8,128)S(1)} collective-permute-done((f32[32,128]{1,0:T(8,128)S(1)}, f32[32,128]{1,0:T(8,128)S(1)}, u32[]{:S(2)}, u32[]{:S(2)}) %collective-permute-start.9) | collective-permute-done | bytes 16416 | tf_op jit(solution)/shard_map/ppermute | solution.py:392
  51.3 2.0 %collective-permute-done.10.d_ref = f32[32,128]{1,0:T(8,128)S(1)} collective-permute-done((f32[32,128]{1,0:T(8,128)S(1)}, f32[32,128]{1,0:T(8,128)S(1)}, u32[]{:S(2)}, u32[]{:S(2)}) %collective-permute-start.10) | collective-permute-done | bytes 16416 | tf_op jit(solution)/shard_map/ppermute | solution.py:392
  53.4 0.7 %shard_map.99 = f32[84,1,48]{2,1,0:T(1,128)} custom-call(s32[1]{0:T(128)} %bitcast.c_ref, f32[48,48]{1,0:T(8,128)S(1)} %get-tuple-element.21.center_ref, f32[32,128]{1,0:T(8,128)S(1)} %get-tuple-element.26.own_ref, f32[32,128]{1,0:T(8,128)S(1)} %collective-permute-done.8.a_ref, f32[32,128]{1,0:T(8,128)S(1)} %collective-permute-done.9.b_ref, ...), custom_call_target="tpu_custom_call" | custom-call | tf_op jit(solution)/shard_map/pallas_call | solution.py:477
Async XLA Ops:
  0.6 7.8 %copy-start = (f32[1,9,27,128]{3,0,2,1:T(1,128)S(1)}, f32[1,9,27,128]{3,0,2,1:T(1,128)}, u32[]{:S(2)}) copy-start(f32[1,9,27,128]{3,0,2,1:T(1,128)} %param.9) | copy-start | bytes 373252
  0.6 11.0 %collective-permute-start.4 = (f32[243,1,128]{2,1,0:T(1,128)}, f32[243,1,128]{2,1,0:T(1,128)S(1)}, u32[]{:S(2)}, u32[]{:S(2)}) collective-permute-start(f32[243,1,128]{2,1,0:T(1,128)} %bitcast.18), channel_id=1, source_target_pairs={{0,2},{1,3},{2,0},{3,1},{4,6},{5,7},{6,4},{7,5},{8,10},{9,11},{10,... | collective-permute-start | bytes 373256 | tf_op jit(solution)/shard_map/ppermute | solution.py:392
  2.8 0.9 %copy-start.1 = (f32[1,48,3,128]{3,1,2,0:T(8,128)S(1)}, f32[1,48,3,128]{3,1,2,0:T(8,128)}, u32[]{:S(2)}) copy-start(f32[1,48,3,128]{3,1,2,0:T(8,128)} %param.8) | copy-start | bytes 221188
  3.6 0.7 %copy-start.2 = (s32[1,27,128]{2,0,1:T(1,128)S(1)}, s32[1,27,128]{2,0,1:T(1,128)}, u32[]{:S(2)}) copy-start(s32[1,27,128]{2,0,1:T(1,128)} %param.10) | copy-start | bytes 41476
  4.4 0.7 %copy-start.3 = (s32[1,6,32]{2,0,1:T(1,128)S(1)}, s32[1,6,32]{2,0,1:T(1,128)}, u32[]{:S(2)}) copy-start(s32[1,6,32]{2,0,1:T(1,128)} %param.13) | copy-start | bytes 2308
  5.0 0.7 %copy-start.4 = (s32[1,6,32]{2,0,1:T(1,128)S(1)}, s32[1,6,32]{2,0,1:T(1,128)}, u32[]{:S(2)}) copy-start(s32[1,6,32]{2,0,1:T(1,128)} %param.14) | copy-start | bytes 2308
  5.7 0.7 %copy-start.5 = (f32[1,3,128]{2,0,1:T(1,128)S(1)}, f32[1,3,128]{2,0,1:T(1,128)}, u32[]{:S(2)}) copy-start(f32[1,3,128]{2,0,1:T(1,128)} %param.12) | copy-start | bytes 4612
  6.4 0.7 %copy-start.6 = (s32[1,6,1]{1,2,0:T(1,128)S(1)}, s32[1,6,1]{1,2,0:T(1,128)}, u32[]{:S(2)}) copy-start(s32[1,6,1]{1,2,0:T(1,128)} %param.15) | copy-start | bytes 76
  7.1 0.7 %copy-start.7 = (s32[1,128]{1,0:T(1,128)S(1)}, s32[1,128]{1,0:T(1,128)}, u32[]{:S(2)}) copy-start(s32[1,128]{1,0:T(1,128)} %cnt_ref.1) | copy-start | bytes 1540
  8.4 3.8 %collective-permute-start.1 = (f32[192,128]{1,0:T(8,128)S(1)}, f32[192,128]{1,0:T(8,128)S(1)}, u32[]{:S(2)}, u32[]{:S(2)}) collective-permute-start(f32[192,128]{1,0:T(8,128)S(1)} %shard_map.95.p0), channel_id=1, source_target_pairs={{0,2},{1,3},{2,0},{3,1},{4,6},{5,7},{6,4},{7,5},{8,10},{9,11},{10,... | collective-permute-start | bytes 294920 | tf_op jit(solution)/shard_map/ppermute | solution.py:392
  8.5 5.8 %collective-permute-start.3 = (f32[243,1,128]{2,1,0:T(1,128)S(1)}, f32[243,1,128]{2,1,0:T(1,128)S(1)}, u32[]{:S(2)}, u32[]{:S(2)}) collective-permute-start(f32[243,1,128]{2,1,0:T(1,128)S(1)} %bitcast.19), channel_id=1, source_target_pairs={{0,1},{1,0},{2,3},{3,2},{4,5},{5,4},{6,7},{7,6},{8,9},{9,8},{10,11... | collective-permute-start | bytes 373256 | tf_op jit(solution)/shard_map/ppermute | solution.py:392
  11.7 3.6 %collective-permute-start.5 = (f32[243,1,128]{2,1,0:T(1,128)S(1)}, f32[243,1,128]{2,1,0:T(1,128)S(1)}, u32[]{:S(2)}, u32[]{:S(2)}) collective-permute-start(f32[243,1,128]{2,1,0:T(1,128)S(1)} %collective-permute-done.4.v2), channel_id=1, source_target_pairs={{0,1},{1,0},{2,3},{3,2},{4,5},{5,4},{6,7},{7,6},{8,9},{9,8},{10,11... | collective-permute-start | bytes 373256 | tf_op jit(solution)/shard_map/ppermute | solution.py:392
  11.8 2.5 %collective-permute-start = (f32[192,128]{1,0:T(8,128)S(1)}, f32[192,128]{1,0:T(8,128)S(1)}, u32[]{:S(2)}, u32[]{:S(2)}) collective-permute-start(f32[192,128]{1,0:T(8,128)S(1)} %shard_map.95.p0), channel_id=1, source_target_pairs={{0,1},{1,0},{2,3},{3,2},{4,5},{5,4},{6,7},{7,6},{8,9},{9,8},{10,11... | collective-permute-start | bytes 294920 | tf_op jit(solution)/shard_map/ppermute | solution.py:392
  12.2 3.0 %collective-permute-start.2 = (f32[192,128]{1,0:T(8,128)S(1)}, f32[192,128]{1,0:T(8,128)S(1)}, u32[]{:S(2)}, u32[]{:S(2)}) collective-permute-start(f32[192,128]{1,0:T(8,128)S(1)} %collective-permute-done.1.p2), channel_id=1, source_target_pairs={{0,1},{1,0},{2,3},{3,2},{4,5},{5,4},{6,7},{7,6},{8,9},{9,8},{10,11... | collective-permute-start | bytes 294920 | tf_op jit(solution)/shard_map/ppermute | solution.py:392
  32.0 10.9 %collective-permute-start.6 = (f32[144,128]{1,0:T(8,128)S(1)}, f32[144,128]{1,0:T(8,128)S(1)}, u32[]{:S(2)}, u32[]{:S(2)}) collective-permute-start(f32[144,128]{1,0:T(8,128)S(1)} %get-tuple-element.24), channel_id=1, source_target_pairs={{0,14},{1,7},{2,244},{3,253},{4,18},{5,11},{6,248},{7,1},{8,22},{9... | collective-permute-start | bytes 221192 | tf_op jit(solution)/shard_map/ppermute | solution.py:450
  33.7 9.2 %collective-permute-start.7 = (f32[72,128]{1,0:T(8,128)S(1)}, f32[72,128]{1,0:T(8,128)S(1)}, u32[]{:S(2)}, u32[]{:S(2)}) collective-permute-start(f32[72,128]{1,0:T(8,128)S(1)} %get-tuple-element.25), channel_id=1, source_target_pairs={{0,8},{1,249},{2,10},{3,251},{4,12},{5,253},{6,14},{7,255},{8,16},... | collective-permute-start | bytes 110600 | tf_op jit(solution)/shard_map/ppermute | solution.py:450
  43.2 7.1 %collective-permute-start.8 = (f32[32,128]{1,0:T(8,128)S(1)}, f32[32,128]{1,0:T(8,128)S(1)}, u32[]{:S(2)}, u32[]{:S(2)}) collective-permute-start(f32[32,128]{1,0:T(8,128)S(1)} %get-tuple-element.27), channel_id=1, source_target_pairs={{0,1},{1,0},{2,3},{3,2},{4,5},{5,4},{6,7},{7,6},{8,9},{9,8},{10,11... | collective-permute-start | bytes 49160 | tf_op jit(solution)/shard_map/ppermute | solution.py:392
  43.6 7.7 %collective-permute-start.9 = (f32[32,128]{1,0:T(8,128)S(1)}, f32[32,128]{1,0:T(8,128)S(1)}, u32[]{:S(2)}, u32[]{:S(2)}) collective-permute-start(f32[32,128]{1,0:T(8,128)S(1)} %get-tuple-element.28), channel_id=1, source_target_pairs={{0,2},{1,3},{2,0},{3,1},{4,6},{5,7},{6,4},{7,5},{8,10},{9,11},{10,... | collective-permute-start | bytes 49160 | tf_op jit(solution)/shard_map/ppermute | solution.py:392
  50.2 3.2 %collective-permute-start.10 = (f32[32,128]{1,0:T(8,128)S(1)}, f32[32,128]{1,0:T(8,128)S(1)}, u32[]{:S(2)}, u32[]{:S(2)}) collective-permute-start(f32[32,128]{1,0:T(8,128)S(1)} %get-tuple-element.29), channel_id=1, source_target_pairs={{0,3},{1,2},{2,1},{3,0},{4,7},{5,6},{6,5},{7,4},{8,11},{9,10},{10,... | collective-permute-start | bytes 49160 | tf_op jit(solution)/shard_map/ppermute | solution.py:392

commit v4 on v3

--- a/solution.py
+++ b/solution.py
@@ -25,7 +25,7 @@
 OFFSETS = [o - RADIUS if o < RADIUS else o - RADIUS + 1 for o in range(SLOTS)]
 SENT = [0, 2, 5, 3]
 GOT = [SENT[c ^ 2] for c in range(NC)]
-SPLIT = [1, 4, 1, 4]
+SPLIT = [1, 1, 4, 4]
 HIGH = lax.Precision.HIGHEST
 F32 = jnp.float32
 
@@ -307,7 +307,7 @@
     linv_ref[...] = linv
     first = wide(index_row(small_ref, SEND0 + entry(SENT, c))).astype(jnp.int32)
     second = wide(index_row(small_ref, SEND0 + entry(SPLIT, c))).astype(jnp.int32)
-    half = (c // 2) * (V // 2)
+    half = (c % 2) * (V // 2)
     for n, slot in enumerate((entry(GOT, c), entry(SPLIT, c))):
         row_ref[2 * n : 2 * n + 1, :] = index_row(small_ref, RECV0 + slot)
         row_ref[2 * n + 1 : 2 * n + 2, :] = index_row(small_ref, LIVE0 + slot)
@@ -340,7 +340,7 @@
     )
 
 
-def coarse_kernel(c_ref, mine1_ref, mine2_ref, got1_ref, got2_ref, own_ref, a_ref, b_ref, d_ref, r_ref):
+def coarse_kernel(c_ref, mine1_ref, mine2_ref, got1_ref, got2_ref, own_ref, a_ref, far_ref, r_ref):
     c = c_ref[0]
 
     def side(ref, count):
@@ -354,15 +354,15 @@
         r_ref[d, 16 : 16 + part, 0 : V // 2] = two[d * part : d * part + part, :]
     own_ref[...] = r_ref[c]
     a_ref[...] = r_ref[c ^ 1]
-    b_ref[...] = r_ref[c ^ 2]
-    d_ref[...] = r_ref[c ^ 3]
-
-
-def join_kernel(c_ref, center_ref, own_ref, a_ref, b_ref, d_ref, out_ref, r_ref):
+    far_ref[0] = r_ref[c ^ 2]
+    far_ref[1] = r_ref[c ^ 3]
+
+
+def join_kernel(c_ref, center_ref, own_ref, a_ref, far_ref, on_ref, out_ref, r_ref):
     c = c_ref[0]
     part = V // NC
-    for m, ref in enumerate((own_ref, a_ref, b_ref, d_ref)):
-        r_ref[m] = ref[...]
+    for m, value in enumerate((own_ref[...], a_ref[...], far_ref[0], on_ref[1])):
+        r_ref[m] = value
 
     def put(place, value):
         for v in range(part):
@@ -371,9 +371,9 @@
     for d in range(NC):
         slot = GOT[d]
         put(slot if slot < RADIUS else slot + 1, r_ref[c ^ d, 0:part, 0:V])
-    for d in range(2):
+    for d in (0, 2):
         slot = SPLIT[d]
-        sides = [r_ref[c ^ (d + 2 * h), 16 : 16 + part, 0 : V // 2] for h in range(2)]
+        sides = [r_ref[c ^ (d + h), 16 : 16 + part, 0 : V // 2] for h in range(2)]
         put(slot if slot < RADIUS else slot + 1, jnp.concatenate(sides, axis=1))
     for d in range(NC):
 
@@ -397,7 +397,6 @@
         out_shape=shape((PACKED, LANES), F32),
         in_specs=[smem(), smem()] + [vmem()] * 6,
         out_specs=vmem(),
-        compiler_params=LIMIT,
     )(
         c,
         ov_count.reshape(SLOTS),
@@ -464,16 +463,16 @@
         scratch_shapes=[pltpu.VMEM(block, F32)],
         compiler_params=LIMIT,
     )(c, *map(near, (row, y2, w, linv)))
-    slab = shape((32, LANES), F32)
-    own, to1, to2, to3 = pl.pallas_call(
+    own, to1, to2 = pl.pallas_call(
         coarse_kernel,
-        out_shape=(slab,) * 4,
+        out_shape=(shape((32, LANES), F32), shape((32, LANES), F32), shape((2, 32, LANES), F32)),
         in_specs=[smem()] + [vmem()] * 4,
-        out_specs=(vmem(),) * 4,
+        out_specs=(vmem(),) * 3,
         scratch_shapes=[pltpu.VMEM((NC, 32, LANES), F32)],
         compiler_params=LIMIT,
     )(c, *map(near, (mine1, mine2, got1, got2)))
-    got = [pass_on(t, m) for m, t in ((1, to1), (2, to2), (3, to3))]
+    far = pass_on(to2, 2)
+    got = (pass_on(to1, 1), far, pass_on(far, 1))
     coarse = pl.pallas_call(
         join_kernel,
         out_shape=jax.ShapeDtypeStruct(((2 * RADIUS + 1) * (V // NC), 1, V), F32),

time: 54.4 us -> 46.9 us (0.86)
  starting transfers between devices: 24.8 us -> 15.5 us
  waiting for transfers between devices: 4.03 us -> 10.7 us
  local copies, waits for them, and re-layouts: 4.96 us -> 0.01 us
    ppermute x2, waiting for transfers between devices: 0.01 us -> 6.89 us  [across(): return lax.ppermute(piece, ('sub', 'crow'), pairs)]
    ppermute x2, starting transfers between devices: 9.7 us -> 3.06 us  [across(): return lax.ppermute(piece, ('sub', 'crow'), pairs)]
    unnamed x16 -> x2, local copies, waits for them, and re-layouts: 4.96 us -> 0.01 us
    ppermute x9, starting transfers between devices: 15.1 us -> 12.4 us  [pass_on(): return lax.ppermute(piece, 'crow', [(n, n ^ m) for n in range(NC)])]
  transfers between devices with their start and end apart: 11 -> 11, of which waited for: 3 -> 5; matrix products, arithmetic and copies ran while one was open for 0% -> 0% of each run, Pallas kernels for 3% -> 5%
where the time goes in v4:
time: 46.9 us; the launch traced here: 46.8 us
  Pallas kernels  19.9 us (42%)
  starting transfers between devices  15.5 us (33%)
  waiting for transfers between devices  10.7 us (23%)
  between operations  0.67 us (1%)
    pallas_call x1, Pallas kernels, shards(): pl.pallas_call(main_kernel, out_shape=(shape(block, F32), shape(block, F3...  16.7 us
    ppermute x9, starting transfers between devices, pass_on(): return lax.ppermute(piece, 'crow', [(n, n ^ m) for n in range(NC)])  12.4 us
    ppermute x2, waiting for transfers between devices, across(): return lax.ppermute(piece, ('sub', 'crow'), pairs)  6.89 us
    ppermute x9, waiting for transfers between devices, pass_on(): return lax.ppermute(piece, 'crow', [(n, n ^ m) for n in range(NC)])  3.78 us
    ppermute x2, starting transfers between devices, across(): return lax.ppermute(piece, ('sub', 'crow'), pairs)  3.06 us
    pallas_call x1, Pallas kernels, shards(): pl.pallas_call(middle_kernel, out_shape=(jax.ShapeDtypeStruct((3 * V, LAN...  1.18 us
    pallas_call x1, Pallas kernels, shards(): pl.pallas_call(pack_kernel, out_shape=shape((PACKED, LANES), F32), in_spe...  1.03 us
  transfers between devices with their start and end apart: 11, of which 5 were waited for; matrix products, arithmetic and copies ran while one was open for 0% of the time, Pallas kernels for 5%

profile of v4, /device:TPU:1, one launch (start us, length us, event | category | flops | bytes accessed | tf_op | source)
XLA Modules:
  0.0 46.8 jit_solution(12363286255476092072)
XLA Ops:
  0.6 0.0 copy-start
  0.6 2.1 %collective-permute-start.4 = (f32[243,1,128]{2,1,0:T(1,128)}, f32[243,1,128]{2,1,0:T(1,128)S(1)}, u32[]{:S(2)}, u32[]{:S(2)}) collective-permute-start(f32[243,1,128]{2,1,0:T(1,128)} %bitcast.18), channel_id=1, source_target_pairs={{0,2},{1,3},{2,0},{3,1},{4,6},{5,7},{6,4},{7,5},{8,10},{9,11},{10,... | collective-permute-start | bytes 373256 | tf_op jit(solution)/shard_map/ppermute | solution.py:392
  2.8 1.0 %shard_map.95.p0 = f32[192,128]{1,0:T(8,128)S(1)} custom-call(s32[1]{0:T(128)} %bitcast.c_ref, s32[6]{0:T(128)} %bitcast.27, f32[144,128]{1,0:T(8,128)} %bitcast.21, s32[27,1,128]{2,1,0:T(1,128)} %bitcast.23, s32[1,128]{1,0:T(1,128)} %cnt_ref.1, f32[3,1,128]{2,1,0:T(1,128)} %bitcast.26, s32[6,1,32]{2,1,0:T(1,128)} %bitcast.24, s32[6,1,32]{2,1,0:T(1,128)} %bitcast.25), custom_call_target="tpu_custom_call" | custom-call | tf_op jit(solution)/shard_map/pallas_call | solution.py:395
  3.8 0.1 collective-permute-start.1
  3.9 0.0 copy-done
  3.9 3.2 %collective-permute-start.3 = (f32[243,1,128]{2,1,0:T(1,128)S(1)}, f32[243,1,128]{2,1,0:T(1,128)S(1)}, u32[]{:S(2)}, u32[]{:S(2)}) collective-permute-start(f32[243,1,128]{2,1,0:T(1,128)S(1)} %bitcast.19), channel_id=1, source_target_pairs={{0,1},{1,0},{2,3},{3,2},{4,5},{5,4},{6,7},{7,6},{8,9},{9,8},{10,11... | collective-permute-start | bytes 373256 | tf_op jit(solution)/shard_map/ppermute | solution.py:392
  7.1 0.0 collective-permute-done.4.v2
  7.1 2.3 %collective-permute-start.5 = (f32[243,1,128]{2,1,0:T(1,128)S(1)}, f32[243,1,128]{2,1,0:T(1,128)S(1)}, u32[]{:S(2)}, u32[]{:S(2)}) collective-permute-start(f32[243,1,128]{2,1,0:T(1,128)S(1)} %collective-permute-done.4.v2), channel_id=1, source_target_pairs={{0,1},{1,0},{2,3},{3,2},{4,5},{5,4},{6,7},{7,6},{8,9},{9,8},{10,11... | collective-permute-start | bytes 373256 | tf_op jit(solution)/shard_map/ppermute | solution.py:392
  9.4 0.0 collective-permute-start
  9.4 0.0 collective-permute-done.1.p2
  9.4 1.0 %collective-permute-start.2 = (f32[192,128]{1,0:T(8,128)S(1)}, f32[192,128]{1,0:T(8,128)S(1)}, u32[]{:S(2)}, u32[]{:S(2)}) collective-permute-start(f32[192,128]{1,0:T(8,128)S(1)} %collective-permute-done.1.p2), channel_id=1, source_target_pairs={{0,1},{1,0},{2,3},{3,2},{4,5},{5,4},{6,7},{7,6},{8,9},{9,8},{10,11... | collective-permute-start | bytes 294920 | tf_op jit(solution)/shard_map/ppermute | solution.py:392
  10.4 0.2 collective-permute-done.p1
  10.7 0.0 collective-permute-done.3.v1
  10.7 0.7 %collective-permute-done.2.p3 = f32[192,128]{1,0:T(8,128)S(1)} collective-permute-done((f32[192,128]{1,0:T(8,128)S(1)}, f32[192,128]{1,0:T(8,128)S(1)}, u32[]{:S(2)}, u32[]{:S(2)}) %collective-permute-start.2) | collective-permute-done | bytes 98336 | tf_op jit(solution)/shard_map/ppermute | solution.py:392
  11.4 0.0 collective-permute-done.5.v3
  11.4 16.7 %shard_map.96 = (f32[4,144,128]{2,1,0:T(8,128)S(1)}, f32[4,144,128]{2,1,0:T(8,128)S(1)}, f32[48,48]{1,0:T(8,128)S(1)}, f32[144,128]{1,0:T(8,128)S(1)}, f32[72,128]{1,0:T(8,128)S(1)}, /*index=5*/f32[8,128]{1,0:T(8,128)S(1)}) custom-call(s32[1]{0:T(128)} %bitcast.c_ref, f32[192,128]{1,0:T(8,128)S(1)} %shard_map.95.p0, f32[192,128]{1,0:T(8,128)S(1)} %collective-permute-done.p1, ...), custom_call_target="tpu_custom_call" | custom-call | tf_op jit(solution)/shard_map/pallas_call | solution.py:415
  28.1 1.8 %collective-permute-start.6 = (f32[144,128]{1,0:T(8,128)S(1)}, f32[144,128]{1,0:T(8,128)S(1)}, u32[]{:S(2)}, u32[]{:S(2)}) collective-permute-start(f32[144,128]{1,0:T(8,128)S(1)} %get-tuple-element.23), channel_id=1, source_target_pairs={{0,14},{1,7},{2,244},{3,253},{4,18},{5,11},{6,248},{7,1},{8,22},{9... | collective-permute-start | bytes 221192 | tf_op jit(solution)/shard_map/ppermute | solution.py:449
  29.9 1.3 %collective-permute-start.7 = (f32[72,128]{1,0:T(8,128)S(1)}, f32[72,128]{1,0:T(8,128)S(1)}, u32[]{:S(2)}, u32[]{:S(2)}) collective-permute-start(f32[72,128]{1,0:T(8,128)S(1)} %get-tuple-element.24), channel_id=1, source_target_pairs={{0,8},{1,9},{2,250},{3,251},{4,12},{5,13},{6,254},{7,255},{8,16},{... | collective-permute-start | bytes 110600 | tf_op jit(solution)/shard_map/ppermute | solution.py:449
  31.2 1.2 %shard_map.97 = (f32[144,128]{1,0:T(8,128)}, f32[144,128]{1,0:T(8,128)S(1)}, f32[144,128]{1,0:T(8,128)S(1)}, f32[48,48]{1,0:T(8,128)S(1)}) custom-call(s32[1]{0:T(128)} %bitcast.c_ref, f32[8,128]{1,0:T(8,128)S(1)} %get-tuple-element.15.row_ref, f32[4,144,128]{2,1,0:T(8,128)S(1)} %get-tuple-element.16.y2_ref, f32[4,144,128]{2,1,0:T(8,128)S(1)} %get-tuple-element.17.w_ref, ...), custom_call_target="tpu_custom_call" | custom-call | tf_op jit(solution)/shard_map/pallas_call | solution.py:453
  32.4 6.9 %collective-permute-done.7.got2_ref = f32[72,128]{1,0:T(8,128)S(1)} collective-permute-done((f32[72,128]{1,0:T(8,128)S(1)}, f32[72,128]{1,0:T(8,128)S(1)}, u32[]{:S(2)}, u32[]{:S(2)}) %collective-permute-start.7) | collective-permute-done | bytes 36896 | tf_op jit(solution)/shard_map/ppermute | solution.py:449
  39.2 0.0 collective-permute-done.6.got1_ref
  39.2 0.3 shard_map.98
  39.5 1.2 %collective-permute-start.9 = (f32[2,32,128]{2,1,0:T(8,128)S(1)}, f32[2,32,128]{2,1,0:T(8,128)S(1)}, u32[]{:S(2)}, u32[]{:S(2)}) collective-permute-start(f32[2,32,128]{2,1,0:T(8,128)S(1)} %get-tuple-element.27), channel_id=1, source_target_pairs={{0,2},{1,3},{2,0},{3,1},{4,6},{5,7},{6,4},{7,5},{8,10},{9,11},{10,... | collective-permute-start | bytes 98312 | tf_op jit(solution)/shard_map/ppermute | solution.py:392
  40.7 1.6 %collective-permute-done.9.far_ref = f32[2,32,128]{2,1,0:T(8,128)S(1)} collective-permute-done((f32[2,32,128]{2,1,0:T(8,128)S(1)}, f32[2,32,128]{2,1,0:T(8,128)S(1)}, u32[]{:S(2)}, u32[]{:S(2)}) %collective-permute-start.9) | collective-permute-done | bytes 32800 | tf_op jit(solution)/shard_map/ppermute | solution.py:392
  42.4 2.5 %collective-permute-start.10 = (f32[2,32,128]{2,1,0:T(8,128)S(1)}, f32[2,32,128]{2,1,0:T(8,128)S(1)}, u32[]{:S(2)}, u32[]{:S(2)}) collective-permute-start(f32[2,32,128]{2,1,0:T(8,128)S(1)} %collective-permute-done.9.far_ref), channel_id=1, source_target_pairs={{0,1},{1,0},{2,3},{3,2},{4,5},{5,4},{6,7},{7,6},{8,9},{9,8},{10,11... | collective-permute-start | bytes 98312 | tf_op jit(solution)/shard_map/ppermute | solution.py:392
  44.9 0.0 collective-permute-start.8
  44.9 1.2 %collective-permute-done.8.a_ref = f32[32,128]{1,0:T(8,128)S(1)} collective-permute-done((f32[32,128]{1,0:T(8,128)S(1)}, f32[32,128]{1,0:T(8,128)S(1)}, u32[]{:S(2)}, u32[]{:S(2)}) %collective-permute-start.8) | collective-permute-done | bytes 16416 | tf_op jit(solution)/shard_map/ppermute | solution.py:392
  46.1 0.0 collective-permute-done.10.on_ref
  46.1 0.7 %shard_map.99 = f32[84,1,48]{2,1,0:T(1,128)} custom-call(s32[1]{0:T(128)} %bitcast.c_ref, f32[48,48]{1,0:T(8,128)S(1)} %get-tuple-element.20.center_ref, f32[32,128]{1,0:T(8,128)S(1)} %get-tuple-element.25.own_ref, f32[32,128]{1,0:T(8,128)S(1)} %collective-permute-done.8.a_ref, f32[2,32,128]{2,1,0:T(8,128)S(1)} %collective-permute-done.9.far_ref, ...), custom_call_target="tpu_custom_call" | custom-call | tf_op jit(solution)/shard_map/pallas_call | solution.py:476
Async XLA Ops:
  0.6 3.3 %copy-start = (f32[1,9,27,128]{3,0,2,1:T(1,128)S(1)}, f32[1,9,27,128]{3,0,2,1:T(1,128)}, u32[]{:S(2)}) copy-start(f32[1,9,27,128]{3,0,2,1:T(1,128)} %param.9) | copy-start | bytes 373252
  0.6 6.4 %collective-permute-start.4 = (f32[243,1,128]{2,1,0:T(1,128)}, f32[243,1,128]{2,1,0:T(1,128)S(1)}, u32[]{:S(2)}, u32[]{:S(2)}) collective-permute-start(f32[243,1,128]{2,1,0:T(1,128)} %bitcast.18), channel_id=1, source_target_pairs={{0,2},{1,3},{2,0},{3,1},{4,6},{5,7},{6,4},{7,5},{8,10},{9,11},{10,... | collective-permute-start | bytes 373256 | tf_op jit(solution)/shard_map/ppermute | solution.py:392
  3.8 5.6 %collective-permute-start.1 = (f32[192,128]{1,0:T(8,128)S(1)}, f32[192,128]{1,0:T(8,128)S(1)}, u32[]{:S(2)}, u32[]{:S(2)}) collective-permute-start(f32[192,128]{1,0:T(8,128)S(1)} %shard_map.95.p0), channel_id=1, source_target_pairs={{0,2},{1,3},{2,0},{3,1},{4,6},{5,7},{6,4},{7,5},{8,10},{9,11},{10,... | collective-permute-start | bytes 294920 | tf_op jit(solution)/shard_map/ppermute | solution.py:392
  3.9 6.8 %collective-permute-start.3 = (f32[243,1,128]{2,1,0:T(1,128)S(1)}, f32[243,1,128]{2,1,0:T(1,128)S(1)}, u32[]{:S(2)}, u32[]{:S(2)}) collective-permute-start(f32[243,1,128]{2,1,0:T(1,128)S(1)} %bitcast.19), channel_id=1, source_target_pairs={{0,1},{1,0},{2,3},{3,2},{4,5},{5,4},{6,7},{7,6},{8,9},{9,8},{10,11... | collective-permute-start | bytes 373256 | tf_op jit(solution)/shard_map/ppermute | solution.py:392
  7.1 4.3 %collective-permute-start.5 = (f32[243,1,128]{2,1,0:T(1,128)S(1)}, f32[243,1,128]{2,1,0:T(1,128)S(1)}, u32[]{:S(2)}, u32[]{:S(2)}) collective-permute-start(f32[243,1,128]{2,1,0:T(1,128)S(1)} %collective-permute-done.4.v2), channel_id=1, source_target_pairs={{0,1},{1,0},{2,3},{3,2},{4,5},{5,4},{6,7},{7,6},{8,9},{9,8},{10,11... | collective-permute-start | bytes 373256 | tf_op jit(solution)/shard_map/ppermute | solution.py:392
  9.4 1.3 %collective-permute-start = (f32[192,128]{1,0:T(8,128)S(1)}, f32[192,128]{1,0:T(8,128)S(1)}, u32[]{:S(2)}, u32[]{:S(2)}) collective-permute-start(f32[192,128]{1,0:T(8,128)S(1)} %shard_map.95.p0), channel_id=1, source_target_pairs={{0,1},{1,0},{2,3},{3,2},{4,5},{5,4},{6,7},{7,6},{8,9},{9,8},{10,11... | collective-permute-start | bytes 294920 | tf_op jit(solution)/shard_map/ppermute | solution.py:392
  9.4 2.0 %collective-permute-start.2 = (f32[192,128]{1,0:T(8,128)S(1)}, f32[192,128]{1,0:T(8,128)S(1)}, u32[]{:S(2)}, u32[]{:S(2)}) collective-permute-start(f32[192,128]{1,0:T(8,128)S(1)} %collective-permute-done.1.p2), channel_id=1, source_target_pairs={{0,1},{1,0},{2,3},{3,2},{4,5},{5,4},{6,7},{7,6},{8,9},{9,8},{10,11... | collective-permute-start | bytes 294920 | tf_op jit(solution)/shard_map/ppermute | solution.py:392
  28.1 11.1 %collective-permute-start.6 = (f32[144,128]{1,0:T(8,128)S(1)}, f32[144,128]{1,0:T(8,128)S(1)}, u32[]{:S(2)}, u32[]{:S(2)}) collective-permute-start(f32[144,128]{1,0:T(8,128)S(1)} %get-tuple-element.23), channel_id=1, source_target_pairs={{0,14},{1,7},{2,244},{3,253},{4,18},{5,11},{6,248},{7,1},{8,22},{9... | collective-permute-start | bytes 221192 | tf_op jit(solution)/shard_map/ppermute | solution.py:449
  29.9 9.4 %collective-permute-start.7 = (f32[72,128]{1,0:T(8,128)S(1)}, f32[72,128]{1,0:T(8,128)S(1)}, u32[]{:S(2)}, u32[]{:S(2)}) collective-permute-start(f32[72,128]{1,0:T(8,128)S(1)} %get-tuple-element.24), channel_id=1, source_target_pairs={{0,8},{1,9},{2,250},{3,251},{4,12},{5,13},{6,254},{7,255},{8,16},{... | collective-permute-start | bytes 110600 | tf_op jit(solution)/shard_map/ppermute | solution.py:449
  39.5 2.9 %collective-permute-start.9 = (f32[2,32,128]{2,1,0:T(8,128)S(1)}, f32[2,32,128]{2,1,0:T(8,128)S(1)}, u32[]{:S(2)}, u32[]{:S(2)}) collective-permute-start(f32[2,32,128]{2,1,0:T(8,128)S(1)} %get-tuple-element.27), channel_id=1, source_target_pairs={{0,2},{1,3},{2,0},{3,1},{4,6},{5,7},{6,4},{7,5},{8,10},{9,11},{10,... | collective-permute-start | bytes 98312 | tf_op jit(solution)/shard_map/ppermute | solution.py:392
  42.4 3.7 %collective-permute-start.10 = (f32[2,32,128]{2,1,0:T(8,128)S(1)}, f32[2,32,128]{2,1,0:T(8,128)S(1)}, u32[]{:S(2)}, u32[]{:S(2)}) collective-permute-start(f32[2,32,128]{2,1,0:T(8,128)S(1)} %collective-permute-done.9.far_ref), channel_id=1, source_target_pairs={{0,1},{1,0},{2,3},{3,2},{4,5},{5,4},{6,7},{7,6},{8,9},{9,8},{10,11... | collective-permute-start | bytes 98312 | tf_op jit(solution)/shard_map/ppermute | solution.py:392
  44.9 1.2 %collective-permute-start.8 = (f32[32,128]{1,0:T(8,128)S(1)}, f32[32,128]{1,0:T(8,128)S(1)}, u32[]{:S(2)}, u32[]{:S(2)}) collective-permute-start(f32[32,128]{1,0:T(8,128)S(1)} %get-tuple-element.26), channel_id=1, source_target_pairs={{0,1},{1,0},{2,3},{3,2},{4,5},{5,4},{6,7},{7,6},{8,9},{9,8},{10,11... | collective-permute-start | bytes 49160 | tf_op jit(solution)/shard_map/ppermute | solution.py:392

commit v5 on v4

--- a/solution.py
+++ b/solution.py
@@ -96,7 +96,8 @@
                 dst_ref[q, rows, :] = piv * src_ref[q, rows, :]
 
 
-ONE = 18
+ONE = 16
+REST = 12
 BF16 = jnp.bfloat16
 
 
@@ -114,18 +115,50 @@
             )
 
 
-def lane_block(val_ref, cols_ref, src_ref, dst_ref, rc, k):
-    col = wide(cols_ref[rc, pl.ds(k, 1), :]).astype(jnp.int32)
-    val = [jnp.where(col >= 0, value_row(val_ref, rc, ab, k), 0.0) for ab in range(9)]
-    index = col & (LANES - 1)
-    odd = (col & LANES) != 0
-    top = col >= 2 * LANES
-
-    def pick_of(b, t):
-        got = [lanes_of(src_ref[q, b * V + 8 * t : b * V + 8 * t + 8, :], index) for q in range(NC)]
-        return jnp.where(top, jnp.where(odd, got[3], got[2]), jnp.where(odd, got[1], got[0]))
-
-    add_block(val, dst_ref, rc, pick_of)
+def pack_pairs(src_ref, scale_ref, pair_ref):
+    inverse = []
+    for t in range(TILES):
+        top = None
+        for q in range(NC):
+            for b in range(3):
+                size = jnp.abs(src_ref[q, b * V + 8 * t : b * V + 8 * t + 8, :])
+                top = size if top is None else jnp.maximum(top, size)
+        top = jnp.broadcast_to(jnp.maximum(jnp.max(top, axis=1, keepdims=True), 1e-30), (8, LANES))
+        scale_ref[8 * t : 8 * t + 8, :] = top * (1.0 / 32767.0)
+        inverse.append(32767.0 / top)
+    for q in range(NC):
+        for b in range(3):
+            for p in range(TILES // 2):
+                whole = [
+                    jnp.round(src_ref[q, b * V + 8 * t : b * V + 8 * t + 8, :] * inverse[t]).astype(jnp.int32)
+                    for t in (2 * p, 2 * p + 1)
+                ]
+                at = 8 * (b * (TILES // 2) + p)
+                pair_ref[q, at : at + 8, :] = (whole[0] << 16) | (whole[1] & 65535)
+
+
+def lane_blocks(val_ref, cols_ref, pair_ref, sum_ref, rc, ks):
+    blocks = []
+    for k in ks:
+        col = wide(cols_ref[rc, pl.ds(k, 1), :]).astype(jnp.int32)
+        real = jnp.minimum(k, NB - 1)
+        val = [jnp.where(col >= 0, value_row(val_ref, rc, ab, real), 0.0) for ab in range(9)]
+        blocks.append((val, col & (LANES - 1), (col & LANES) != 0, col >= 2 * LANES))
+    for p in range(TILES // 2):
+        rows = [[slice(a * V + 8 * t, a * V + 8 * t + 8) for t in (2 * p, 2 * p + 1)] for a in range(3)]
+        total = [[sum_ref[rc, at, :] for at in pair] for pair in rows]
+        for val, index, odd, top in blocks:
+            for b in range(3):
+                at = 8 * (b * (TILES // 2) + p)
+                got = [lanes_of(pair_ref[q, at : at + 8, :], index) for q in range(NC)]
+                both = jnp.where(top, jnp.where(odd, got[3], got[2]), jnp.where(odd, got[1], got[0]))
+                pick = ((both >> 16).astype(F32), ((both << 16) >> 16).astype(F32))
+                for a in range(3):
+                    for n in range(2):
+                        total[a][n] = total[a][n] + val[3 * a + b] * pick[n]
+        for a in range(3):
+            for n in range(2):
+                sum_ref[rc, rows[a][n], :] = total[a][n]
 
 
 def one_hot(cols_ref, oh_ref, k):
@@ -201,7 +234,7 @@
 
 
 CHOL = 3
-UN = 6
+UN = 8
 
 
 def factor_piece(m_ref, col_ref, j):
@@ -263,7 +296,7 @@
 def main_kernel(
     c_ref, p0, p1, p2, p3, v0, v1, v2, v3,
     y2_ref, w_ref, linv_ref, s1_ref, s2_ref, row_ref,
-    y_ref, z_ref, m_ref, col_ref, g_ref, x_ref, oh_ref, t_ref, cols_ref,
+    y_ref, z_ref, m_ref, col_ref, g_ref, x_ref, oh_ref, t_ref, cols_ref, pair_ref, scale_ref, sum_ref,
 ):
     c = c_ref[0]
     small_ref = Blocks((p0, p1, p2, p3))
@@ -271,6 +304,7 @@
     for m in range(NC):
         col = small_ref[m, COL0 : COL0 + NB, :]
         local = (col.astype(jnp.int32) ^ (c * LANES)).astype(F32)
+        cols_ref[m, NB:32, :] = jnp.full((32 - NB, LANES), -1.0, F32)
         cols_ref[m, 0:NB, :] = jnp.where(col < 0.0, -1.0, local)
     m_ref[V:, :] = jnp.zeros((8, LANES), F32)
 
@@ -282,14 +316,16 @@
         else:
             gram_to(m_ref, x_ref)
         start_op(small_ref, src_ref, dst_ref)
+        pack_pairs(src_ref, scale_ref, pair_ref)
+        sum_ref[...] = jnp.zeros((NC, 3 * V, LANES), F32)
         issue(x_ref, oh_ref, t_ref, 0, 0)
 
         def step(it, carry):
             for u in range(UN):
                 k = UN * it + u
                 issue(x_ref, oh_ref, t_ref, jnp.minimum(k + 1, ONE - 1), (u + 1) % 2)
-                for rc in (2 * (u % 2), 2 * (u % 2) + 1):
-                    lane_block(val_ref, cols_ref, src_ref, dst_ref, rc, ONE + (UN // 2) * it + u // 2)
+                ks = [ONE + (REST // 2) * it + 3 * (u % 2) + n for n in range(3)]
+                lane_blocks(val_ref, cols_ref, pair_ref, sum_ref, u // 2, ks)
                 if first:
                     one_hot(cols_ref, oh_ref, jnp.minimum(k + 2, ONE - 1))
                 else:
@@ -298,6 +334,10 @@
             return carry
 
         lax.fori_loop(0, ONE // UN, step, 0)
+        for q in range(NC):
+            for a in range(3):
+                at = slice(a * V, a * V + V)
+                dst_ref[q, at, :] = dst_ref[q, at, :] + sum_ref[q, at, :] * scale_ref[...]
 
     loop(small_ref, y_ref, True)
     loop(y_ref, z_ref, False)
@@ -340,7 +380,7 @@
     )
 
 
-def coarse_kernel(c_ref, mine1_ref, mine2_ref, got1_ref, got2_ref, own_ref, a_ref, far_ref, r_ref):
+def coarse_kernel(c_ref, mine1_ref, mine2_ref, got1_ref, got2_ref, near_ref, far_ref, r_ref):
     c = c_ref[0]
 
     def side(ref, count):
@@ -352,16 +392,21 @@
     for d in range(NC):
         r_ref[d, 0:part, 0:V] = one[d * part : d * part + part, :]
         r_ref[d, 16 : 16 + part, 0 : V // 2] = two[d * part : d * part + part, :]
-    own_ref[...] = r_ref[c]
-    a_ref[...] = r_ref[c ^ 1]
+    near_ref[0] = r_ref[c]
+    near_ref[1] = r_ref[c ^ 1]
     far_ref[0] = r_ref[c ^ 2]
     far_ref[1] = r_ref[c ^ 3]
 
 
-def join_kernel(c_ref, center_ref, own_ref, a_ref, far_ref, on_ref, out_ref, r_ref):
+def pair_kernel(near_ref, far_ref, out_ref):
+    out_ref[0] = near_ref[1]
+    out_ref[1] = far_ref[1]
+
+
+def join_kernel(c_ref, center_ref, near_ref, far_ref, on_ref, out_ref, r_ref):
     c = c_ref[0]
     part = V // NC
-    for m, value in enumerate((own_ref[...], a_ref[...], far_ref[0], on_ref[1])):
+    for m, value in enumerate((near_ref[0], on_ref[0], far_ref[0], on_ref[1])):
         r_ref[m] = value
 
     def put(place, value):
@@ -434,6 +479,9 @@
             pltpu.VMEM((2, ONE, NC * LANES, 2 * LANES), BF16),
             pltpu.VMEM((2, 2, 3 * V, 2 * LANES), F32),
             pltpu.VMEM((NC, 32, LANES), F32),
+            pltpu.VMEM((NC, 3 * V // 2, LANES), jnp.int32),
+            pltpu.VMEM((V, LANES), F32),
+            pltpu.VMEM(block, F32),
         ],
         compiler_params=LIMIT,
     )(c, *map(near, blocks))
@@ -463,24 +511,28 @@
         scratch_shapes=[pltpu.VMEM(block, F32)],
         compiler_params=LIMIT,
     )(c, *map(near, (row, y2, w, linv)))
-    own, to1, to2 = pl.pallas_call(
+    pair = shape((2, 32, LANES), F32)
+    mine, sent = pl.pallas_call(
         coarse_kernel,
-        out_shape=(shape((32, LANES), F32), shape((32, LANES), F32), shape((2, 32, LANES), F32)),
+        out_shape=(pair, pair),
         in_specs=[smem()] + [vmem()] * 4,
-        out_specs=(vmem(),) * 3,
+        out_specs=(vmem(),) * 2,
         scratch_shapes=[pltpu.VMEM((NC, 32, LANES), F32)],
         compiler_params=LIMIT,
     )(c, *map(near, (mine1, mine2, got1, got2)))
-    far = pass_on(to2, 2)
-    got = (pass_on(to1, 1), far, pass_on(far, 1))
+    far = pass_on(sent, 2)
+    both = pl.pallas_call(
+        pair_kernel, out_shape=pair, in_specs=[vmem()] * 2, out_specs=vmem(), compiler_params=LIMIT
+    )(near(mine), near(far))
+    on = pass_on(both, 1)
     coarse = pl.pallas_call(
         join_kernel,
         out_shape=jax.ShapeDtypeStruct(((2 * RADIUS + 1) * (V // NC), 1, V), F32),
-        in_specs=[smem()] + [vmem()] * 5,
+        in_specs=[smem()] + [vmem()] * 4,
         out_specs=vmem(),
         scratch_shapes=[pltpu.VMEM((NC, 32, LANES), F32)],
         compiler_params=LIMIT,
-    )(c, *map(near, (center, own, *got)))
+    )(c, *map(near, (center, mine, far, on)))
     coarse = coarse.reshape(2 * RADIUS + 1, V // NC, V)
     basis = jnp.transpose(basis.reshape(3, V, LANES), (1, 0, 2))
     return basis[None], coarse[None]

time: 46.9 us -> 44.4 us (0.947)
  Pallas kernels: 19.9 us -> 17.7 us
    pallas_call x1, Pallas kernels: 16.7 us -> 14.5 us  [shards(): pl.pallas_call(main_kernel, out_shape=(shape(block, F32), shape(block, F3...]
    ppermute x9 -> x8, waiting for transfers between devices: 3.78 us -> 3.46 us  [pass_on(): return lax.ppermute(piece, 'crow', [(n, n ^ m) for n in range(NC)])]
    ppermute x9 -> x8, starting transfers between devices: 12.4 us -> 12.4 us  [pass_on(): return lax.ppermute(piece, 'crow', [(n, n ^ m) for n in range(NC)])]
  transfers between devices with their start and end apart: 11 -> 10, of which waited for: 5 -> 5; matrix products, arithmetic and copies ran while one was open for 0% -> 0% of each run, Pallas kernels for 5% -> 5%
where the time goes in v5:
time: 44.4 us; the launch traced here: 44.3 us
  Pallas kernels  17.7 us (40%)
  starting transfers between devices  15.5 us (35%)
  waiting for transfers between devices  10.3 us (23%)
  between operations  0.67 us (2%)
    pallas_call x1, Pallas kernels, shards(): pl.pallas_call(main_kernel, out_shape=(shape(block, F32), shape(block, F3...  14.5 us
    ppermute x8, starting transfers between devices, pass_on(): return lax.ppermute(piece, 'crow', [(n, n ^ m) for n in range(NC)])  12.4 us
    ppermute x2, waiting for transfers between devices, across(): return lax.ppermute(piece, ('sub', 'crow'), pairs)  6.89 us
    ppermute x8, waiting for transfers between devices, pass_on(): return lax.ppermute(piece, 'crow', [(n, n ^ m) for n in range(NC)])  3.46 us
    ppermute x2, starting transfers between devices, across(): return lax.ppermute(piece, ('sub', 'crow'), pairs)  3.07 us
    pallas_call x1, Pallas kernels, shards(): pl.pallas_call(middle_kernel, out_shape=(jax.ShapeDtypeStruct((3 * V, LAN...  1.19 us
    pallas_call x1, Pallas kernels, shards(): pl.pallas_call(pack_kernel, out_shape=shape((PACKED, LANES), F32), in_spe...  1.03 us
  transfers between devices with their start and end apart: 10, of which 5 were waited for; matrix products, arithmetic and copies ran while one was open for 0% of the time, Pallas kernels for 5%

profile of v5, /device:TPU:1, one launch (start us, length us, event | category | flops | bytes accessed | tf_op | source)
XLA Modules:
  0.0 44.3 jit_solution(4698144845774242207)
XLA Ops:
  0.6 0.0 copy-start
  0.6 2.1 %collective-permute-start.4 = (f32[243,1,128]{2,1,0:T(1,128)}, f32[243,1,128]{2,1,0:T(1,128)S(1)}, u32[]{:S(2)}, u32[]{:S(2)}) collective-permute-start(f32[243,1,128]{2,1,0:T(1,128)} %bitcast.18), channel_id=1, source_target_pairs={{0,2},{1,3},{2,0},{3,1},{4,6},{5,7},{6,4},{7,5},{8,10},{9,11},{10,... | collective-permute-start | bytes 373256 | tf_op jit(solution)/shard_map/ppermute | solution.py:437
  2.8 1.0 %shard_map.95.p0 = f32[192,128]{1,0:T(8,128)S(1)} custom-call(s32[1]{0:T(128)} %bitcast.c_ref, s32[6]{0:T(128)} %bitcast.27, f32[144,128]{1,0:T(8,128)} %bitcast.21, s32[27,1,128]{2,1,0:T(1,128)} %bitcast.23, s32[1,128]{1,0:T(1,128)} %cnt_ref.1, f32[3,1,128]{2,1,0:T(1,128)} %bitcast.26, s32[6,1,32]{2,1,0:T(1,128)} %bitcast.24, s32[6,1,32]{2,1,0:T(1,128)} %bitcast.25), custom_call_target="tpu_custom_call" | custom-call | tf_op jit(solution)/shard_map/pallas_call | solution.py:440
  3.8 0.1 collective-permute-start.1
  3.9 0.0 copy-done
  3.9 3.2 %collective-permute-start.3 = (f32[243,1,128]{2,1,0:T(1,128)S(1)}, f32[243,1,128]{2,1,0:T(1,128)S(1)}, u32[]{:S(2)}, u32[]{:S(2)}) collective-permute-start(f32[243,1,128]{2,1,0:T(1,128)S(1)} %bitcast.19), channel_id=1, source_target_pairs={{0,1},{1,0},{2,3},{3,2},{4,5},{5,4},{6,7},{7,6},{8,9},{9,8},{10,11... | collective-permute-start | bytes 373256 | tf_op jit(solution)/shard_map/ppermute | solution.py:437
  7.1 0.0 collective-permute-done.4.v2
  7.1 2.3 %collective-permute-start.5 = (f32[243,1,128]{2,1,0:T(1,128)S(1)}, f32[243,1,128]{2,1,0:T(1,128)S(1)}, u32[]{:S(2)}, u32[]{:S(2)}) collective-permute-start(f32[243,1,128]{2,1,0:T(1,128)S(1)} %collective-permute-done.4.v2), channel_id=1, source_target_pairs={{0,1},{1,0},{2,3},{3,2},{4,5},{5,4},{6,7},{7,6},{8,9},{9,8},{10,11... | collective-permute-start | bytes 373256 | tf_op jit(solution)/shard_map/ppermute | solution.py:437
  9.4 0.0 collective-permute-start
  9.4 0.0 collective-permute-done.1.p2
  9.4 1.0 %collective-permute-start.2 = (f32[192,128]{1,0:T(8,128)S(1)}, f32[192,128]{1,0:T(8,128)S(1)}, u32[]{:S(2)}, u32[]{:S(2)}) collective-permute-start(f32[192,128]{1,0:T(8,128)S(1)} %collective-permute-done.1.p2), channel_id=1, source_target_pairs={{0,1},{1,0},{2,3},{3,2},{4,5},{5,4},{6,7},{7,6},{8,9},{9,8},{10,11... | collective-permute-start | bytes 294920 | tf_op jit(solution)/shard_map/ppermute | solution.py:437
  10.4 0.2 collective-permute-done.p1
  10.7 0.0 collective-permute-done.3.v1
  10.7 0.7 %collective-permute-done.2.p3 = f32[192,128]{1,0:T(8,128)S(1)} collective-permute-done((f32[192,128]{1,0:T(8,128)S(1)}, f32[192,128]{1,0:T(8,128)S(1)}, u32[]{:S(2)}, u32[]{:S(2)}) %collective-permute-start.2) | collective-permute-done | bytes 98336 | tf_op jit(solution)/shard_map/ppermute | solution.py:437
  11.4 0.0 collective-permute-done.5.v3
  11.4 14.5 %shard_map.96 = (f32[4,144,128]{2,1,0:T(8,128)S(1)}, f32[4,144,128]{2,1,0:T(8,128)S(1)}, f32[48,48]{1,0:T(8,128)S(1)}, f32[144,128]{1,0:T(8,128)S(1)}, f32[72,128]{1,0:T(8,128)S(1)}, /*index=5*/f32[8,128]{1,0:T(8,128)S(1)}) custom-call(s32[1]{0:T(128)} %bitcast.c_ref, f32[192,128]{1,0:T(8,128)S(1)} %shard_map.95.p0, f32[192,128]{1,0:T(8,128)S(1)} %collective-permute-done.p1, ...), custom_call_target="tpu_custom_call" | custom-call | tf_op jit(solution)/shard_map/pallas_call | solution.py:460
  25.9 1.8 %collective-permute-start.6 = (f32[144,128]{1,0:T(8,128)S(1)}, f32[144,128]{1,0:T(8,128)S(1)}, u32[]{:S(2)}, u32[]{:S(2)}) collective-permute-start(f32[144,128]{1,0:T(8,128)S(1)} %get-tuple-element.22), channel_id=1, source_target_pairs={{0,14},{1,7},{2,244},{3,253},{4,18},{5,11},{6,248},{7,1},{8,22},{9... | collective-permute-start | bytes 221192 | tf_op jit(solution)/shard_map/ppermute | solution.py:497
  27.7 1.3 %collective-permute-start.7 = (f32[72,128]{1,0:T(8,128)S(1)}, f32[72,128]{1,0:T(8,128)S(1)}, u32[]{:S(2)}, u32[]{:S(2)}) collective-permute-start(f32[72,128]{1,0:T(8,128)S(1)} %get-tuple-element.23), channel_id=1, source_target_pairs={{0,8},{1,9},{2,250},{3,251},{4,12},{5,13},{6,254},{7,255},{8,16},{... | collective-permute-start | bytes 110600 | tf_op jit(solution)/shard_map/ppermute | solution.py:497
  29.0 1.2 %shard_map.97 = (f32[144,128]{1,0:T(8,128)}, f32[144,128]{1,0:T(8,128)S(1)}, f32[144,128]{1,0:T(8,128)S(1)}, f32[48,48]{1,0:T(8,128)S(1)}) custom-call(s32[1]{0:T(128)} %bitcast.c_ref, f32[8,128]{1,0:T(8,128)S(1)} %get-tuple-element.14.row_ref, f32[4,144,128]{2,1,0:T(8,128)S(1)} %get-tuple-element.15.y2_ref, f32[4,144,128]{2,1,0:T(8,128)S(1)} %get-tuple-element.16.w_ref, ...), custom_call_target="tpu_custom_call" | custom-call | tf_op jit(solution)/shard_map/pallas_call | solution.py:501
  30.2 6.9 %collective-permute-done.7.got2_ref = f32[72,128]{1,0:T(8,128)S(1)} collective-permute-done((f32[72,128]{1,0:T(8,128)S(1)}, f32[72,128]{1,0:T(8,128)S(1)}, u32[]{:S(2)}, u32[]{:S(2)}) %collective-permute-start.7) | collective-permute-done | bytes 36896 | tf_op jit(solution)/shard_map/ppermute | solution.py:497
  37.1 0.0 collective-permute-done.6.got1_ref
  37.1 0.3 shard_map.98
  37.3 1.2 %collective-permute-start.8 = (f32[2,32,128]{2,1,0:T(8,128)S(1)}, f32[2,32,128]{2,1,0:T(8,128)S(1)}, u32[]{:S(2)}, u32[]{:S(2)}) collective-permute-start(f32[2,32,128]{2,1,0:T(8,128)S(1)} %get-tuple-element.25), channel_id=1, source_target_pairs={{0,2},{1,3},{2,0},{3,1},{4,6},{5,7},{6,4},{7,5},{8,10},{9,11},{10,... | collective-permute-start | bytes 98312 | tf_op jit(solution)/shard_map/ppermute | solution.py:437
  38.5 1.6 %collective-permute-done.8.far_ref = f32[2,32,128]{2,1,0:T(8,128)S(1)} collective-permute-done((f32[2,32,128]{2,1,0:T(8,128)S(1)}, f32[2,32,128]{2,1,0:T(8,128)S(1)}, u32[]{:S(2)}, u32[]{:S(2)}) %collective-permute-start.8) | collective-permute-done | bytes 32800 | tf_op jit(solution)/shard_map/ppermute | solution.py:437
  40.2 2.5 %collective-permute-start.9 = (f32[2,32,128]{2,1,0:T(8,128)S(1)}, f32[2,32,128]{2,1,0:T(8,128)S(1)}, u32[]{:S(2)}, u32[]{:S(2)}) collective-permute-start(f32[2,32,128]{2,1,0:T(8,128)S(1)} %shard_map.99), channel_id=1, source_target_pairs={{0,1},{1,0},{2,3},{3,2},{4,5},{5,4},{6,7},{7,6},{8,9},{9,8},{10,11... | collective-permute-start | bytes 98312 | tf_op jit(solution)/shard_map/ppermute | solution.py:437
  42.7 0.9 %collective-permute-done.9.on_ref = f32[2,32,128]{2,1,0:T(8,128)S(1)} collective-permute-done((f32[2,32,128]{2,1,0:T(8,128)S(1)}, f32[2,32,128]{2,1,0:T(8,128)S(1)}, u32[]{:S(2)}, u32[]{:S(2)}) %collective-permute-start.9) | collective-permute-done | bytes 32800 | tf_op jit(solution)/shard_map/ppermute | solution.py:437
  43.6 0.7 %shard_map.100 = f32[84,1,48]{2,1,0:T(1,128)} custom-call(s32[1]{0:T(128)} %bitcast.c_ref, f32[48,48]{1,0:T(8,128)S(1)} %get-tuple-element.19.center_ref, f32[2,32,128]{2,1,0:T(8,128)S(1)} %get-tuple-element.24.near_ref, f32[2,32,128]{2,1,0:T(8,128)S(1)} %collective-permute-done.8.far_ref, f32[2,32,128]{2,1,0:T(8,128)S(1)} %collective-permute-done.9.on_ref), custom_call_target="tpu_custom_call" | custom-call | tf_op jit(solution)/shard_map/pallas_call | solution.py:528
  (1 shorter events, 0.0 us)
Async XLA Ops:
  0.6 3.3 %copy-start = (f32[1,9,27,128]{3,0,2,1:T(1,128)S(1)}, f32[1,9,27,128]{3,0,2,1:T(1,128)}, u32[]{:S(2)}) copy-start(f32[1,9,27,128]{3,0,2,1:T(1,128)} %param.9) | copy-start | bytes 373252
  0.6 6.4 %collective-permute-start.4 = (f32[243,1,128]{2,1,0:T(1,128)}, f32[243,1,128]{2,1,0:T(1,128)S(1)}, u32[]{:S(2)}, u32[]{:S(2)}) collective-permute-start(f32[243,1,128]{2,1,0:T(1,128)} %bitcast.18), channel_id=1, source_target_pairs={{0,2},{1,3},{2,0},{3,1},{4,6},{5,7},{6,4},{7,5},{8,10},{9,11},{10,... | collective-permute-start | bytes 373256 | tf_op jit(solution)/shard_map/ppermute | solution.py:437
  3.8 5.6 %collective-permute-start.1 = (f32[192,128]{1,0:T(8,128)S(1)}, f32[192,128]{1,0:T(8,128)S(1)}, u32[]{:S(2)}, u32[]{:S(2)}) collective-permute-start(f32[192,128]{1,0:T(8,128)S(1)} %shard_map.95.p0), channel_id=1, source_target_pairs={{0,2},{1,3},{2,0},{3,1},{4,6},{5,7},{6,4},{7,5},{8,10},{9,11},{10,... | collective-permute-start | bytes 294920 | tf_op jit(solution)/shard_map/ppermute | solution.py:437
  3.9 6.8 %collective-permute-start.3 = (f32[243,1,128]{2,1,0:T(1,128)S(1)}, f32[243,1,128]{2,1,0:T(1,128)S(1)}, u32[]{:S(2)}, u32[]{:S(2)}) collective-permute-start(f32[243,1,128]{2,1,0:T(1,128)S(1)} %bitcast.19), channel_id=1, source_target_pairs={{0,1},{1,0},{2,3},{3,2},{4,5},{5,4},{6,7},{7,6},{8,9},{9,8},{10,11... | collective-permute-start | bytes 373256 | tf_op jit(solution)/shard_map/ppermute | solution.py:437
  7.1 4.3 %collective-permute-start.5 = (f32[243,1,128]{2,1,0:T(1,128)S(1)}, f32[243,1,128]{2,1,0:T(1,128)S(1)}, u32[]{:S(2)}, u32[]{:S(2)}) collective-permute-start(f32[243,1,128]{2,1,0:T(1,128)S(1)} %collective-permute-done.4.v2), channel_id=1, source_target_pairs={{0,1},{1,0},{2,3},{3,2},{4,5},{5,4},{6,7},{7,6},{8,9},{9,8},{10,11... | collective-permute-start | bytes 373256 | tf_op jit(solution)/shard_map/ppermute | solution.py:437
  9.4 1.3 %collective-permute-start = (f32[192,128]{1,0:T(8,128)S(1)}, f32[192,128]{1,0:T(8,128)S(1)}, u32[]{:S(2)}, u32[]{:S(2)}) collective-permute-start(f32[192,128]{1,0:T(8,128)S(1)} %shard_map.95.p0), channel_id=1, source_target_pairs={{0,1},{1,0},{2,3},{3,2},{4,5},{5,4},{6,7},{7,6},{8,9},{9,8},{10,11... | collective-permute-start | bytes 294920 | tf_op jit(solution)/shard_map/ppermute | solution.py:437
  9.4 2.0 %collective-permute-start.2 = (f32[192,128]{1,0:T(8,128)S(1)}, f32[192,128]{1,0:T(8,128)S(1)}, u32[]{:S(2)}, u32[]{:S(2)}) collective-permute-start(f32[192,128]{1,0:T(8,128)S(1)} %collective-permute-done.1.p2), channel_id=1, source_target_pairs={{0,1},{1,0},{2,3},{3,2},{4,5},{5,4},{6,7},{7,6},{8,9},{9,8},{10,11... | collective-permute-start | bytes 294920 | tf_op jit(solution)/shard_map/ppermute | solution.py:437
  25.9 11.2 %collective-permute-start.6 = (f32[144,128]{1,0:T(8,128)S(1)}, f32[144,128]{1,0:T(8,128)S(1)}, u32[]{:S(2)}, u32[]{:S(2)}) collective-permute-start(f32[144,128]{1,0:T(8,128)S(1)} %get-tuple-element.22), channel_id=1, source_target_pairs={{0,14},{1,7},{2,244},{3,253},{4,18},{5,11},{6,248},{7,1},{8,22},{9... | collective-permute-start | bytes 221192 | tf_op jit(solution)/shard_map/ppermute | solution.py:497
  27.7 9.4 %collective-permute-start.7 = (f32[72,128]{1,0:T(8,128)S(1)}, f32[72,128]{1,0:T(8,128)S(1)}, u32[]{:S(2)}, u32[]{:S(2)}) collective-permute-start(f32[72,128]{1,0:T(8,128)S(1)} %get-tuple-element.23), channel_id=1, source_target_pairs={{0,8},{1,9},{2,250},{3,251},{4,12},{5,13},{6,254},{7,255},{8,16},{... | collective-permute-start | bytes 110600 | tf_op jit(solution)/shard_map/ppermute | solution.py:497
  37.3 2.9 %collective-permute-start.8 = (f32[2,32,128]{2,1,0:T(8,128)S(1)}, f32[2,32,128]{2,1,0:T(8,128)S(1)}, u32[]{:S(2)}, u32[]{:S(2)}) collective-permute-start(f32[2,32,128]{2,1,0:T(8,128)S(1)} %get-tuple-element.25), channel_id=1, source_target_pairs={{0,2},{1,3},{2,0},{3,1},{4,6},{5,7},{6,4},{7,5},{8,10},{9,11},{10,... | collective-permute-start | bytes 98312 | tf_op jit(solution)/shard_map/ppermute | solution.py:437
  40.2 3.4 %collective-permute-start.9 = (f32[2,32,128]{2,1,0:T(8,128)S(1)}, f32[2,32,128]{2,1,0:T(8,128)S(1)}, u32[]{:S(2)}, u32[]{:S(2)}) collective-permute-start(f32[2,32,128]{2,1,0:T(8,128)S(1)} %shard_map.99), channel_id=1, source_target_pairs={{0,1},{1,0},{2,3},{3,2},{4,5},{5,4},{6,7},{7,6},{8,9},{9,8},{10,11... | collective-permute-start | bytes 98312 | tf_op jit(solution)/shard_map/ppermute | solution.py:437

commit v6 on v5

--- a/solution.py
+++ b/solution.py
@@ -363,21 +363,28 @@
         s2_ref[a * (V // 2) : (a + 1) * (V // 2), :] = g_ref[1, pl.ds(pl.multiple_of(a * V + half, 8), V // 2), :]
 
 
-def middle_kernel(c_ref, row_ref, y2_ref, w_ref, linv_ref, basis_ref, mine1_ref, mine2_ref, center_ref, q_ref):
+def middle_kernel(c_ref, row_ref, y2_ref, linv_ref, mine1_ref, mine2_ref, g_ref):
     c = c_ref[0]
+    tiles = [slice(8 * t, 8 * t + 8) for t in range(3 * TILES)]
+    for n in range(2):
+        index = wide(row_ref[2 * n : 2 * n + 1, :]).astype(jnp.int32)
+        live = wide(row_ref[2 * n + 1 : 2 * n + 2, :])
+        for at, piece in zip(tiles, rows_of(y2_ref, index, tiles, c)):
+            g_ref[n, at, :] = piece * live
+    both = jnp.concatenate([g_ref[n, a * V : a * V + V, :] for n in range(2) for a in range(3)], axis=1)
+    mine = mix(linv_ref[...], both)
+    for n, out_ref in enumerate((mine1_ref, mine2_ref)):
+        for a in range(3):
+            at = (3 * n + a) * LANES
+            out_ref[a * V : a * V + V, :] = mine[:, at : at + LANES]
+
+
+def basis_kernel(after_ref, y2_ref, w_ref, linv_ref, basis_ref, center_ref, q_ref):
     linv = linv_ref[...]
     solve_to(q_ref, linv, y2_ref)
     basis_ref[...] = q_ref[0]
-    tiles = [slice(8 * t, 8 * t + 8) for t in range(3 * TILES)]
-    for n, out_ref in enumerate((mine1_ref, mine2_ref)):
-        index = wide(row_ref[2 * n : 2 * n + 1, :]).astype(jnp.int32)
-        live = wide(row_ref[2 * n + 1 : 2 * n + 2, :])
-        for at, piece in zip(tiles, rows_of(q_ref, index, tiles, c)):
-            out_ref[at, :] = piece * live
     image = mix(linv, flat(w_ref))
-    center_ref[...] = lax.dot_general(
-        flat(q_ref), image, NT, precision=HIGH, preferred_element_type=F32
-    )
+    center_ref[...] = lax.dot_general(flat(q_ref), image, NT, precision=HIGH, preferred_element_type=F32)
 
 
 def coarse_kernel(c_ref, mine1_ref, mine2_ref, got1_ref, got2_ref, near_ref, far_ref, r_ref):
@@ -398,7 +405,7 @@
     far_ref[1] = r_ref[c ^ 3]
 
 
-def pair_kernel(near_ref, far_ref, out_ref):
+def pair_kernel(near_ref, far_ref, after_ref, out_ref):
     out_ref[0] = near_ref[1]
     out_ref[1] = far_ref[1]
 
@@ -498,19 +505,14 @@
 
     got1 = across(s1, SENT, 2)
     got2 = across(s2, SPLIT, 0)
-    basis, mine1, mine2, center = pl.pallas_call(
+    mine1, mine2 = pl.pallas_call(
         middle_kernel,
-        out_shape=(
-            jax.ShapeDtypeStruct((3 * V, LANES), F32),
-            shape((3 * V, LANES), F32),
-            shape((3 * V, LANES), F32),
-            shape((V, V), F32),
-        ),
-        in_specs=[smem()] + [vmem()] * 4,
-        out_specs=(vmem(),) * 4,
-        scratch_shapes=[pltpu.VMEM(block, F32)],
+        out_shape=(shape((3 * V, LANES), F32), shape((3 * V, LANES), F32)),
+        in_specs=[smem()] + [vmem()] * 3,
+        out_specs=(vmem(),) * 2,
+        scratch_shapes=[pltpu.VMEM((2, 3 * V, LANES), F32)],
         compiler_params=LIMIT,
-    )(c, *map(near, (row, y2, w, linv)))
+    )(c, *map(near, (row, y2, linv)))
     pair = shape((2, 32, LANES), F32)
     mine, sent = pl.pallas_call(
         coarse_kernel,
@@ -521,9 +523,17 @@
         compiler_params=LIMIT,
     )(c, *map(near, (mine1, mine2, got1, got2)))
     far = pass_on(sent, 2)
+    basis, center = pl.pallas_call(
+        basis_kernel,
+        out_shape=(jax.ShapeDtypeStruct((3 * V, LANES), F32), shape((V, V), F32)),
+        in_specs=[vmem()] * 4,
+        out_specs=(vmem(),) * 2,
+        scratch_shapes=[pltpu.VMEM(block, F32)],
+        compiler_params=LIMIT,
+    )(*map(near, (mine, y2, w, linv)))
     both = pl.pallas_call(
-        pair_kernel, out_shape=pair, in_specs=[vmem()] * 2, out_specs=vmem(), compiler_params=LIMIT
-    )(near(mine), near(far))
+        pair_kernel, out_shape=pair, in_specs=[vmem()] * 3, out_specs=vmem(), compiler_params=LIMIT
+    )(near(mine), near(far), near(center))
     on = pass_on(both, 1)
     coarse = pl.pallas_call(
         join_kernel,

time: 44.4 us -> 44.4 us (level)
    ppermute x8, waiting for transfers between devices: 3.46 us -> 2.55 us  [pass_on(): return lax.ppermute(piece, 'crow', [(n, n ^ m) for n in range(NC)])]
    ppermute x2, waiting for transfers between devices: 6.89 us -> 7.69 us  [across(): return lax.ppermute(piece, ('sub', 'crow'), pairs)]
    pallas_call x2 -> x3, Pallas kernels: 1.19 us -> 1.29 us  [the longest x1 0.9 us: shards(): pl.pallas_call(basis_kernel, out_shape=(jax.ShapeDtypeStruct((3 * V, LANE...]
where the time goes in v6:
time: 44.4 us; the launch traced here: 44.3 us
  Pallas kernels  17.8 us (40%)
  starting transfers between devices  15.5 us (35%)
  waiting for transfers between devices  10.2 us (23%)
  between operations  0.68 us (2%)
    pallas_call x1, Pallas kernels, shards(): pl.pallas_call(main_kernel, out_shape=(shape(block, F32), shape(block, F3...  14.5 us
    ppermute x8, starting transfers between devices, pass_on(): return lax.ppermute(piece, 'crow', [(n, n ^ m) for n in range(NC)])  12.4 us
    ppermute x2, waiting for transfers between devices, across(): return lax.ppermute(piece, ('sub', 'crow'), pairs)  7.69 us
    ppermute x2, starting transfers between devices, across(): return lax.ppermute(piece, ('sub', 'crow'), pairs)  3.07 us
    ppermute x8, waiting for transfers between devices, pass_on(): return lax.ppermute(piece, 'crow', [(n, n ^ m) for n in range(NC)])  2.55 us
    pallas_call x1, Pallas kernels, shards(): pl.pallas_call(pack_kernel, out_shape=shape((PACKED, LANES), F32), in_spe...  1.03 us
    pallas_call x1, Pallas kernels, shards(): pl.pallas_call(basis_kernel, out_shape=(jax.ShapeDtypeStruct((3 * V, LANE...  0.9 us
  transfers between devices with their start and end apart: 10, of which 5 were waited for; matrix products, arithmetic and copies ran while one was open for 0% of the time, Pallas kernels for 5%

profile of v6, /device:TPU:1, one launch (start us, length us, event | category | flops | bytes accessed | tf_op | source)
XLA Modules:
  0.0 44.3 jit_solution(10781858385452224963)
XLA Ops:
  0.6 0.0 copy-start
  0.6 2.1 %collective-permute-start.4 = (f32[243,1,128]{2,1,0:T(1,128)}, f32[243,1,128]{2,1,0:T(1,128)S(1)}, u32[]{:S(2)}, u32[]{:S(2)}) collective-permute-start(f32[243,1,128]{2,1,0:T(1,128)} %bitcast.18), channel_id=1, source_target_pairs={{0,2},{1,3},{2,0},{3,1},{4,6},{5,7},{6,4},{7,5},{8,10},{9,11},{10,... | collective-permute-start | bytes 373256 | tf_op jit(solution)/shard_map/ppermute | solution.py:444
  2.8 1.0 %shard_map.95.p0 = f32[192,128]{1,0:T(8,128)S(1)} custom-call(s32[1]{0:T(128)} %bitcast.c_ref, s32[6]{0:T(128)} %bitcast.27, f32[144,128]{1,0:T(8,128)} %bitcast.21, s32[27,1,128]{2,1,0:T(1,128)} %bitcast.23, s32[1,128]{1,0:T(1,128)} %cnt_ref.1, f32[3,1,128]{2,1,0:T(1,128)} %bitcast.26, s32[6,1,32]{2,1,0:T(1,128)} %bitcast.24, s32[6,1,32]{2,1,0:T(1,128)} %bitcast.25), custom_call_target="tpu_custom_call" | custom-call | tf_op jit(solution)/shard_map/pallas_call | solution.py:447
  3.8 0.1 collective-permute-start.1
  3.9 0.0 copy-done
  3.9 3.2 %collective-permute-start.3 = (f32[243,1,128]{2,1,0:T(1,128)S(1)}, f32[243,1,128]{2,1,0:T(1,128)S(1)}, u32[]{:S(2)}, u32[]{:S(2)}) collective-permute-start(f32[243,1,128]{2,1,0:T(1,128)S(1)} %bitcast.19), channel_id=1, source_target_pairs={{0,1},{1,0},{2,3},{3,2},{4,5},{5,4},{6,7},{7,6},{8,9},{9,8},{10,11... | collective-permute-start | bytes 373256 | tf_op jit(solution)/shard_map/ppermute | solution.py:444
  7.1 0.0 collective-permute-done.4.v2
  7.1 2.3 %collective-permute-start.5 = (f32[243,1,128]{2,1,0:T(1,128)S(1)}, f32[243,1,128]{2,1,0:T(1,128)S(1)}, u32[]{:S(2)}, u32[]{:S(2)}) collective-permute-start(f32[243,1,128]{2,1,0:T(1,128)S(1)} %collective-permute-done.4.v2), channel_id=1, source_target_pairs={{0,1},{1,0},{2,3},{3,2},{4,5},{5,4},{6,7},{7,6},{8,9},{9,8},{10,11... | collective-permute-start | bytes 373256 | tf_op jit(solution)/shard_map/ppermute | solution.py:444
  9.4 0.0 collective-permute-start
  9.4 0.0 collective-permute-done.1.p2
  9.4 1.0 %collective-permute-start.2 = (f32[192,128]{1,0:T(8,128)S(1)}, f32[192,128]{1,0:T(8,128)S(1)}, u32[]{:S(2)}, u32[]{:S(2)}) collective-permute-start(f32[192,128]{1,0:T(8,128)S(1)} %collective-permute-done.1.p2), channel_id=1, source_target_pairs={{0,1},{1,0},{2,3},{3,2},{4,5},{5,4},{6,7},{7,6},{8,9},{9,8},{10,11... | collective-permute-start | bytes 294920 | tf_op jit(solution)/shard_map/ppermute | solution.py:444
  10.4 0.2 collective-permute-done.p1
  10.7 0.0 collective-permute-done.3.v1
  10.7 0.7 %collective-permute-done.2.p3 = f32[192,128]{1,0:T(8,128)S(1)} collective-permute-done((f32[192,128]{1,0:T(8,128)S(1)}, f32[192,128]{1,0:T(8,128)S(1)}, u32[]{:S(2)}, u32[]{:S(2)}) %collective-permute-start.2) | collective-permute-done | bytes 98336 | tf_op jit(solution)/shard_map/ppermute | solution.py:444
  11.4 0.0 collective-permute-done.5.v3
  11.4 14.5 %shard_map.96 = (f32[4,144,128]{2,1,0:T(8,128)S(1)}, f32[4,144,128]{2,1,0:T(8,128)S(1)}, f32[48,48]{1,0:T(8,128)S(1)}, f32[144,128]{1,0:T(8,128)S(1)}, f32[72,128]{1,0:T(8,128)S(1)}, /*index=5*/f32[8,128]{1,0:T(8,128)S(1)}) custom-call(s32[1]{0:T(128)} %bitcast.c_ref, f32[192,128]{1,0:T(8,128)S(1)} %shard_map.95.p0, f32[192,128]{1,0:T(8,128)S(1)} %collective-permute-done.p1, ...), custom_call_target="tpu_custom_call" | custom-call | tf_op jit(solution)/shard_map/pallas_call | solution.py:467
  25.9 1.8 %collective-permute-start.6 = (f32[144,128]{1,0:T(8,128)S(1)}, f32[144,128]{1,0:T(8,128)S(1)}, u32[]{:S(2)}, u32[]{:S(2)}) collective-permute-start(f32[144,128]{1,0:T(8,128)S(1)} %get-tuple-element.19), channel_id=1, source_target_pairs={{0,14},{1,7},{2,244},{3,253},{4,18},{5,11},{6,248},{7,1},{8,22},{9... | collective-permute-start | bytes 221192 | tf_op jit(solution)/shard_map/ppermute | solution.py:504
  27.7 1.3 %collective-permute-start.7 = (f32[72,128]{1,0:T(8,128)S(1)}, f32[72,128]{1,0:T(8,128)S(1)}, u32[]{:S(2)}, u32[]{:S(2)}) collective-permute-start(f32[72,128]{1,0:T(8,128)S(1)} %get-tuple-element.20), channel_id=1, source_target_pairs={{0,8},{1,9},{2,250},{3,251},{4,12},{5,13},{6,254},{7,255},{8,16},{... | collective-permute-start | bytes 110600 | tf_op jit(solution)/shard_map/ppermute | solution.py:504
  29.0 0.4 shard_map.97
  29.4 7.7 %collective-permute-done.7.got2_ref = f32[72,128]{1,0:T(8,128)S(1)} collective-permute-done((f32[72,128]{1,0:T(8,128)S(1)}, f32[72,128]{1,0:T(8,128)S(1)}, u32[]{:S(2)}, u32[]{:S(2)}) %collective-permute-start.7) | collective-permute-done | bytes 36896 | tf_op jit(solution)/shard_map/ppermute | solution.py:504
  37.1 0.0 collective-permute-done.6.got1_ref
  37.1 0.3 shard_map.98
  37.3 1.2 %collective-permute-start.8 = (f32[2,32,128]{2,1,0:T(8,128)S(1)}, f32[2,32,128]{2,1,0:T(8,128)S(1)}, u32[]{:S(2)}, u32[]{:S(2)}) collective-permute-start(f32[2,32,128]{2,1,0:T(8,128)S(1)} %get-tuple-element.25), channel_id=1, source_target_pairs={{0,2},{1,3},{2,0},{3,1},{4,6},{5,7},{6,4},{7,5},{8,10},{9,11},{10,... | collective-permute-start | bytes 98312 | tf_op jit(solution)/shard_map/ppermute | solution.py:444
  38.5 0.9 %shard_map.99 = (f32[144,128]{1,0:T(8,128)}, f32[48,48]{1,0:T(8,128)S(1)}) custom-call(f32[2,32,128]{2,1,0:T(8,128)S(1)} %get-tuple-element.21.after_ref.near_ref, f32[4,144,128]{2,1,0:T(8,128)S(1)} %get-tuple-element.15.y2_ref, f32[4,144,128]{2,1,0:T(8,128)S(1)} %get-tuple-element.22.w_ref, f32[48,48]{1,0:T(8,128)S(1)} %get-tuple-element.16.linv_ref), custom_call_target="tpu_custom_call" | custom-call | tf_op jit(solution)/shard_map/pallas_call | solution.py:526
  39.5 0.7 %collective-permute-done.8.far_ref = f32[2,32,128]{2,1,0:T(8,128)S(1)} collective-permute-done((f32[2,32,128]{2,1,0:T(8,128)S(1)}, f32[2,32,128]{2,1,0:T(8,128)S(1)}, u32[]{:S(2)}, u32[]{:S(2)}) %collective-permute-start.8) | collective-permute-done | bytes 32800 | tf_op jit(solution)/shard_map/ppermute | solution.py:444
  40.2 2.5 %collective-permute-start.9 = (f32[2,32,128]{2,1,0:T(8,128)S(1)}, f32[2,32,128]{2,1,0:T(8,128)S(1)}, u32[]{:S(2)}, u32[]{:S(2)}) collective-permute-start(f32[2,32,128]{2,1,0:T(8,128)S(1)} %shard_map.100), channel_id=1, source_target_pairs={{0,1},{1,0},{2,3},{3,2},{4,5},{5,4},{6,7},{7,6},{8,9},{9,8},{10,11... | collective-permute-start | bytes 98312 | tf_op jit(solution)/shard_map/ppermute | solution.py:444
  42.7 0.9 %collective-permute-done.9.on_ref = f32[2,32,128]{2,1,0:T(8,128)S(1)} collective-permute-done((f32[2,32,128]{2,1,0:T(8,128)S(1)}, f32[2,32,128]{2,1,0:T(8,128)S(1)}, u32[]{:S(2)}, u32[]{:S(2)}) %collective-permute-start.9) | collective-permute-done | bytes 32800 | tf_op jit(solution)/shard_map/ppermute | solution.py:444
  43.6 0.7 %shard_map.101 = f32[84,1,48]{2,1,0:T(1,128)} custom-call(s32[1]{0:T(128)} %bitcast.c_ref, f32[48,48]{1,0:T(8,128)S(1)} %get-tuple-element.24.after_ref.center_ref, f32[2,32,128]{2,1,0:T(8,128)S(1)} %get-tuple-element.21.after_ref.near_ref, f32[2,32,128]{2,1,0:T(8,128)S(1)} %collective-permute-done.8.far_ref, f32[2,32,128]{2,1,0:T(8,128)S(1)} %collective-permute-done.9.on_ref), custom_call_target="tpu_custom_call" | custom-call | tf_op jit(solution)/shard_map/pallas_call | solution.py:538
  (1 shorter events, 0.0 us)
Async XLA Ops:
  0.6 3.3 %copy-start = (f32[1,9,27,128]{3,0,2,1:T(1,128)S(1)}, f32[1,9,27,128]{3,0,2,1:T(1,128)}, u32[]{:S(2)}) copy-start(f32[1,9,27,128]{3,0,2,1:T(1,128)} %param.9) | copy-start | bytes 373252
  0.6 6.4 %collective-permute-start.4 = (f32[243,1,128]{2,1,0:T(1,128)}, f32[243,1,128]{2,1,0:T(1,128)S(1)}, u32[]{:S(2)}, u32[]{:S(2)}) collective-permute-start(f32[243,1,128]{2,1,0:T(1,128)} %bitcast.18), channel_id=1, source_target_pairs={{0,2},{1,3},{2,0},{3,1},{4,6},{5,7},{6,4},{7,5},{8,10},{9,11},{10,... | collective-permute-start | bytes 373256 | tf_op jit(solution)/shard_map/ppermute | solution.py:444
  3.8 5.6 %collective-permute-start.1 = (f32[192,128]{1,0:T(8,128)S(1)}, f32[192,128]{1,0:T(8,128)S(1)}, u32[]{:S(2)}, u32[]{:S(2)}) collective-permute-start(f32[192,128]{1,0:T(8,128)S(1)} %shard_map.95.p0), channel_id=1, source_target_pairs={{0,2},{1,3},{2,0},{3,1},{4,6},{5,7},{6,4},{7,5},{8,10},{9,11},{10,... | collective-permute-start | bytes 294920 | tf_op jit(solution)/shard_map/ppermute | solution.py:444
  3.9 6.8 %collective-permute-start.3 = (f32[243,1,128]{2,1,0:T(1,128)S(1)}, f32[243,1,128]{2,1,0:T(1,128)S(1)}, u32[]{:S(2)}, u32[]{:S(2)}) collective-permute-start(f32[243,1,128]{2,1,0:T(1,128)S(1)} %bitcast.19), channel_id=1, source_target_pairs={{0,1},{1,0},{2,3},{3,2},{4,5},{5,4},{6,7},{7,6},{8,9},{9,8},{10,11... | collective-permute-start | bytes 373256 | tf_op jit(solution)/shard_map/ppermute | solution.py:444
  7.1 4.3 %collective-permute-start.5 = (f32[243,1,128]{2,1,0:T(1,128)S(1)}, f32[243,1,128]{2,1,0:T(1,128)S(1)}, u32[]{:S(2)}, u32[]{:S(2)}) collective-permute-start(f32[243,1,128]{2,1,0:T(1,128)S(1)} %collective-permute-done.4.v2), channel_id=1, source_target_pairs={{0,1},{1,0},{2,3},{3,2},{4,5},{5,4},{6,7},{7,6},{8,9},{9,8},{10,11... | collective-permute-start | bytes 373256 | tf_op jit(solution)/shard_map/ppermute | solution.py:444
  9.4 1.3 %collective-permute-start = (f32[192,128]{1,0:T(8,128)S(1)}, f32[192,128]{1,0:T(8,128)S(1)}, u32[]{:S(2)}, u32[]{:S(2)}) collective-permute-start(f32[192,128]{1,0:T(8,128)S(1)} %shard_map.95.p0), channel_id=1, source_target_pairs={{0,1},{1,0},{2,3},{3,2},{4,5},{5,4},{6,7},{7,6},{8,9},{9,8},{10,11... | collective-permute-start | bytes 294920 | tf_op jit(solution)/shard_map/ppermute | solution.py:444
  9.4 2.0 %collective-permute-start.2 = (f32[192,128]{1,0:T(8,128)S(1)}, f32[192,128]{1,0:T(8,128)S(1)}, u32[]{:S(2)}, u32[]{:S(2)}) collective-permute-start(f32[192,128]{1,0:T(8,128)S(1)} %collective-permute-done.1.p2), channel_id=1, source_target_pairs={{0,1},{1,0},{2,3},{3,2},{4,5},{5,4},{6,7},{7,6},{8,9},{9,8},{10,11... | collective-permute-start | bytes 294920 | tf_op jit(solution)/shard_map/ppermute | solution.py:444
  25.9 11.2 %collective-permute-start.6 = (f32[144,128]{1,0:T(8,128)S(1)}, f32[144,128]{1,0:T(8,128)S(1)}, u32[]{:S(2)}, u32[]{:S(2)}) collective-permute-start(f32[144,128]{1,0:T(8,128)S(1)} %get-tuple-element.19), channel_id=1, source_target_pairs={{0,14},{1,7},{2,244},{3,253},{4,18},{5,11},{6,248},{7,1},{8,22},{9... | collective-permute-start | bytes 221192 | tf_op jit(solution)/shard_map/ppermute | solution.py:504
  27.7 9.4 %collective-permute-start.7 = (f32[72,128]{1,0:T(8,128)S(1)}, f32[72,128]{1,0:T(8,128)S(1)}, u32[]{:S(2)}, u32[]{:S(2)}) collective-permute-start(f32[72,128]{1,0:T(8,128)S(1)} %get-tuple-element.20), channel_id=1, source_target_pairs={{0,8},{1,9},{2,250},{3,251},{4,12},{5,13},{6,254},{7,255},{8,16},{... | collective-permute-start | bytes 110600 | tf_op jit(solution)/shard_map/ppermute | solution.py:504
  37.3 2.9 %collective-permute-start.8 = (f32[2,32,128]{2,1,0:T(8,128)S(1)}, f32[2,32,128]{2,1,0:T(8,128)S(1)}, u32[]{:S(2)}, u32[]{:S(2)}) collective-permute-start(f32[2,32,128]{2,1,0:T(8,128)S(1)} %get-tuple-element.25), channel_id=1, source_target_pairs={{0,2},{1,3},{2,0},{3,1},{4,6},{5,7},{6,4},{7,5},{8,10},{9,11},{10,... | collective-permute-start | bytes 98312 | tf_op jit(solution)/shard_map/ppermute | solution.py:444
  40.2 3.4 %collective-permute-start.9 = (f32[2,32,128]{2,1,0:T(8,128)S(1)}, f32[2,32,128]{2,1,0:T(8,128)S(1)}, u32[]{:S(2)}, u32[]{:S(2)}) collective-permute-start(f32[2,32,128]{2,1,0:T(8,128)S(1)} %shard_map.100), channel_id=1, source_target_pairs={{0,1},{1,0},{2,3},{3,2},{4,5},{5,4},{6,7},{7,6},{8,9},{9,8},{10,11... | collective-permute-start | bytes 98312 | tf_op jit(solution)/shard_map/ppermute | solution.py:444

commit v7 on v6

--- a/solution.py
+++ b/solution.py
@@ -97,7 +97,6 @@
 
 
 ONE = 16
-REST = 12
 BF16 = jnp.bfloat16
 
 
@@ -140,9 +139,8 @@
 def lane_blocks(val_ref, cols_ref, pair_ref, sum_ref, rc, ks):
     blocks = []
     for k in ks:
-        col = wide(cols_ref[rc, pl.ds(k, 1), :]).astype(jnp.int32)
-        real = jnp.minimum(k, NB - 1)
-        val = [jnp.where(col >= 0, value_row(val_ref, rc, ab, real), 0.0) for ab in range(9)]
+        col = wide(cols_ref[rc, k : k + 1, :]).astype(jnp.int32)
+        val = [jnp.where(col >= 0, value_row(val_ref, rc, ab, k), 0.0) for ab in range(9)]
         blocks.append((val, col & (LANES - 1), (col & LANES) != 0, col >= 2 * LANES))
     for p in range(TILES // 2):
         rows = [[slice(a * V + 8 * t, a * V + 8 * t + 8) for t in (2 * p, 2 * p + 1)] for a in range(3)]
@@ -165,7 +163,7 @@
     half = 2 * LANES
     place = lax.broadcasted_iota(jnp.int32, (half, half), 0).astype(F32).astype(BF16)
     for m in range(2):
-        col = jnp.concatenate([cols_ref[2 * m + n, pl.ds(k, 1), :] for n in range(2)], axis=1)
+        col = jnp.concatenate([cols_ref[2 * m + n, k : k + 1, :] for n in range(2)], axis=1)
         for h in range(2):
             local = col - float(h * half)
             local = jnp.where((local >= 0.0) & (local < float(half)), local, -1.0)
@@ -234,24 +232,28 @@
 
 
 CHOL = 3
-UN = 8
 
 
 def factor_piece(m_ref, col_ref, j):
     sub = lax.broadcasted_iota(jnp.int32, (8, LANES), 0)
-    m = [m_ref[8 * t : 8 * t + 8, :] for t in range(TILES)]
+    tiles = range(j // 8, TILES)
+    m = {t: m_ref[8 * t : 8 * t + 8, :] for t in tiles}
     cols = []
     for s in range(CHOL):
-        index = jnp.full((8, LANES), 64 + s, jnp.int32) + j
-        cols.append([lanes_of(m[t], index) for t in range(TILES)])
-        for t in range(TILES):
+        index = jnp.full((8, LANES), 64 + s + j, jnp.int32)
+        cols.append({t: lanes_of(m[t], index) for t in tiles})
+        for t in tiles:
             col_ref[s, 8 * t : 8 * t + 8, :] = cols[s][t]
     for s in range(CHOL):
-        row = wide(m_ref[pl.ds(j + s, 1), :])
-        head = {n: wide(col_ref[n, pl.ds(j + s, 1), :]) for n in range(s, CHOL)}
+        row = wide(m_ref[j + s : j + s + 1, :])
+        head = {n: wide(col_ref[n, j + s : j + s + 1, :]) for n in range(s, CHOL)}
         inverse = 1.0 / head[s]
-        for t in range(TILES):
-            factor = jnp.where(sub + 8 * t > j + s, cols[s][t] * inverse, 0.0)
+        for t in tiles:
+            if 8 * t + 7 <= j + s:
+                continue
+            factor = cols[s][t] * inverse
+            if 8 * t <= j + s:
+                factor = jnp.where(sub + 8 * t > j + s, factor, 0.0)
             m[t] = m[t] - factor * row
             m_ref[8 * t : 8 * t + 8, :] = m[t]
             for n in range(s + 1, CHOL):
@@ -308,7 +310,7 @@
         cols_ref[m, 0:NB, :] = jnp.where(col < 0.0, -1.0, local)
     m_ref[V:, :] = jnp.zeros((8, LANES), F32)
 
-    def loop(src_ref, dst_ref, first):
+    def apply(src_ref, dst_ref, first):
         split_to(x_ref, src_ref)
         if first:
             one_hot(cols_ref, oh_ref, 0)
@@ -320,29 +322,26 @@
         sum_ref[...] = jnp.zeros((NC, 3 * V, LANES), F32)
         issue(x_ref, oh_ref, t_ref, 0, 0)
 
-        def step(it, carry):
-            for u in range(UN):
-                k = UN * it + u
-                issue(x_ref, oh_ref, t_ref, jnp.minimum(k + 1, ONE - 1), (u + 1) % 2)
-                ks = [ONE + (REST // 2) * it + 3 * (u % 2) + n for n in range(3)]
-                lane_blocks(val_ref, cols_ref, pair_ref, sum_ref, u // 2, ks)
-                if first:
-                    one_hot(cols_ref, oh_ref, jnp.minimum(k + 2, ONE - 1))
-                else:
-                    factor_piece(m_ref, col_ref, k * CHOL)
-                take(val_ref, dst_ref, t_ref, k, u % 2)
-            return carry
-
-        lax.fori_loop(0, ONE // UN, step, 0)
+        for k in range(ONE):
+            if k + 1 < ONE:
+                issue(x_ref, oh_ref, t_ref, k + 1, (k + 1) % 2)
+            ks = [n for n in range(ONE + 3 * (k % 4), ONE + 3 * (k % 4) + 3) if n < NB]
+            lane_blocks(val_ref, cols_ref, pair_ref, sum_ref, k // 4, ks)
+            if first:
+                if k + 2 < ONE:
+                    one_hot(cols_ref, oh_ref, k + 2)
+            else:
+                factor_piece(m_ref, col_ref, k * CHOL)
+            take(val_ref, dst_ref, t_ref, k, k % 2)
         for q in range(NC):
             for a in range(3):
                 at = slice(a * V, a * V + V)
                 dst_ref[q, at, :] = dst_ref[q, at, :] + sum_ref[q, at, :] * scale_ref[...]
 
-    loop(small_ref, y_ref, True)
-    loop(y_ref, z_ref, False)
+    apply(small_ref, y_ref, True)
+    apply(y_ref, z_ref, False)
     solve_to(y2_ref, inverse_of(m_ref), z_ref)
-    loop(y2_ref, w_ref, False)
+    apply(y2_ref, w_ref, False)
     linv = inverse_of(m_ref)
     linv_ref[...] = linv
     first = wide(index_row(small_ref, SEND0 + entry(SENT, c))).astype(jnp.int32)

time: 44.4 us -> 42.1 us (0.948)
  Pallas kernels: 17.8 us -> 15.6 us
    pallas_call x1, Pallas kernels: 14.5 us -> 12.3 us  [shards(): pl.pallas_call(main_kernel, out_shape=(shape(block, F32), shape(block, F3...]
  transfers between devices with their start and end apart: 10 -> 10, of which waited for: 5 -> 5; matrix products, arithmetic and copies ran while one was open for 0% -> 0% of each run, Pallas kernels for 5% -> 6%
where the time goes in v7:
time: 42.1 us; the launch traced here: 42 us
  Pallas kernels  15.6 us (37%)
  starting transfers between devices  15.5 us (37%)
  waiting for transfers between devices  10.2 us (24%)
  between operations  0.68 us (2%)
    ppermute x8, starting transfers between devices, pass_on(): return lax.ppermute(piece, 'crow', [(n, n ^ m) for n in range(NC)])  12.4 us
    pallas_call x1, Pallas kernels, shards(): pl.pallas_call(main_kernel, out_shape=(shape(block, F32), shape(block, F3...  12.3 us
    ppermute x2, waiting for transfers between devices, across(): return lax.ppermute(piece, ('sub', 'crow'), pairs)  7.69 us
    ppermute x2, starting transfers between devices, across(): return lax.ppermute(piece, ('sub', 'crow'), pairs)  3.06 us
    ppermute x8, waiting for transfers between devices, pass_on(): return lax.ppermute(piece, 'crow', [(n, n ^ m) for n in range(NC)])  2.54 us
    pallas_call x1, Pallas kernels, shards(): pl.pallas_call(pack_kernel, out_shape=shape((PACKED, LANES), F32), in_spe...  1.03 us
    pallas_call x1, Pallas kernels, shards(): pl.pallas_call(basis_kernel, out_shape=(jax.ShapeDtypeStruct((3 * V, LANE...  0.9 us
  transfers between devices with their start and end apart: 10, of which 5 were waited for; matrix products, arithmetic and copies ran while one was open for 0% of the time, Pallas kernels for 6%

profile of v7, /device:TPU:1, one launch (start us, length us, event | category | flops | bytes accessed | tf_op | source)
XLA Modules:
  0.0 42.0 jit_solution(6568850382084267083)
XLA Ops:
  0.6 0.0 copy-start
  0.6 2.1 %collective-permute-start.4 = (f32[243,1,128]{2,1,0:T(1,128)}, f32[243,1,128]{2,1,0:T(1,128)S(1)}, u32[]{:S(2)}, u32[]{:S(2)}) collective-permute-start(f32[243,1,128]{2,1,0:T(1,128)} %bitcast.18), channel_id=1, source_target_pairs={{0,2},{1,3},{2,0},{3,1},{4,6},{5,7},{6,4},{7,5},{8,10},{9,11},{10,... | collective-permute-start | bytes 373256 | tf_op jit(solution)/shard_map/ppermute | solution.py:443
  2.8 1.0 %shard_map.95.p0 = f32[192,128]{1,0:T(8,128)S(1)} custom-call(s32[1]{0:T(128)} %bitcast.c_ref, s32[6]{0:T(128)} %bitcast.27, f32[144,128]{1,0:T(8,128)} %bitcast.21, s32[27,1,128]{2,1,0:T(1,128)} %bitcast.23, s32[1,128]{1,0:T(1,128)} %cnt_ref.1, f32[3,1,128]{2,1,0:T(1,128)} %bitcast.26, s32[6,1,32]{2,1,0:T(1,128)} %bitcast.24, s32[6,1,32]{2,1,0:T(1,128)} %bitcast.25), custom_call_target="tpu_custom_call" | custom-call | tf_op jit(solution)/shard_map/pallas_call | solution.py:446
  3.8 0.1 collective-permute-start.1
  3.9 0.0 copy-done
  3.9 3.2 %collective-permute-start.3 = (f32[243,1,128]{2,1,0:T(1,128)S(1)}, f32[243,1,128]{2,1,0:T(1,128)S(1)}, u32[]{:S(2)}, u32[]{:S(2)}) collective-permute-start(f32[243,1,128]{2,1,0:T(1,128)S(1)} %bitcast.19), channel_id=1, source_target_pairs={{0,1},{1,0},{2,3},{3,2},{4,5},{5,4},{6,7},{7,6},{8,9},{9,8},{10,11... | collective-permute-start | bytes 373256 | tf_op jit(solution)/shard_map/ppermute | solution.py:443
  7.1 0.0 collective-permute-done.4.v2
  7.1 2.3 %collective-permute-start.5 = (f32[243,1,128]{2,1,0:T(1,128)S(1)}, f32[243,1,128]{2,1,0:T(1,128)S(1)}, u32[]{:S(2)}, u32[]{:S(2)}) collective-permute-start(f32[243,1,128]{2,1,0:T(1,128)S(1)} %collective-permute-done.4.v2), channel_id=1, source_target_pairs={{0,1},{1,0},{2,3},{3,2},{4,5},{5,4},{6,7},{7,6},{8,9},{9,8},{10,11... | collective-permute-start | bytes 373256 | tf_op jit(solution)/shard_map/ppermute | solution.py:443
  9.4 0.0 collective-permute-start
  9.4 0.0 collective-permute-done.1.p2
  9.4 1.0 %collective-permute-start.2 = (f32[192,128]{1,0:T(8,128)S(1)}, f32[192,128]{1,0:T(8,128)S(1)}, u32[]{:S(2)}, u32[]{:S(2)}) collective-permute-start(f32[192,128]{1,0:T(8,128)S(1)} %collective-permute-done.1.p2), channel_id=1, source_target_pairs={{0,1},{1,0},{2,3},{3,2},{4,5},{5,4},{6,7},{7,6},{8,9},{9,8},{10,11... | collective-permute-start | bytes 294920 | tf_op jit(solution)/shard_map/ppermute | solution.py:443
  10.4 0.2 collective-permute-done.p1
  10.7 0.0 collective-permute-done.3.v1
  10.7 0.7 %collective-permute-done.2.p3 = f32[192,128]{1,0:T(8,128)S(1)} collective-permute-done((f32[192,128]{1,0:T(8,128)S(1)}, f32[192,128]{1,0:T(8,128)S(1)}, u32[]{:S(2)}, u32[]{:S(2)}) %collective-permute-start.2) | collective-permute-done | bytes 98336 | tf_op jit(solution)/shard_map/ppermute | solution.py:443
  11.4 0.0 collective-permute-done.5.v3
  11.4 12.3 %shard_map.96 = (f32[4,144,128]{2,1,0:T(8,128)S(1)}, f32[4,144,128]{2,1,0:T(8,128)S(1)}, f32[48,48]{1,0:T(8,128)S(1)}, f32[144,128]{1,0:T(8,128)S(1)}, f32[72,128]{1,0:T(8,128)S(1)}, /*index=5*/f32[8,128]{1,0:T(8,128)S(1)}) custom-call(s32[1]{0:T(128)} %bitcast.c_ref, f32[192,128]{1,0:T(8,128)S(1)} %shard_map.95.p0, f32[192,128]{1,0:T(8,128)S(1)} %collective-permute-done.p1, ...), custom_call_target="tpu_custom_call" | custom-call | tf_op jit(solution)/shard_map/pallas_call | solution.py:466
  23.7 1.8 %collective-permute-start.6 = (f32[144,128]{1,0:T(8,128)S(1)}, f32[144,128]{1,0:T(8,128)S(1)}, u32[]{:S(2)}, u32[]{:S(2)}) collective-permute-start(f32[144,128]{1,0:T(8,128)S(1)} %get-tuple-element.19), channel_id=1, source_target_pairs={{0,14},{1,7},{2,244},{3,253},{4,18},{5,11},{6,248},{7,1},{8,22},{9... | collective-permute-start | bytes 221192 | tf_op jit(solution)/shard_map/ppermute | solution.py:503
  25.4 1.3 %collective-permute-start.7 = (f32[72,128]{1,0:T(8,128)S(1)}, f32[72,128]{1,0:T(8,128)S(1)}, u32[]{:S(2)}, u32[]{:S(2)}) collective-permute-start(f32[72,128]{1,0:T(8,128)S(1)} %get-tuple-element.20), channel_id=1, source_target_pairs={{0,8},{1,9},{2,250},{3,251},{4,12},{5,13},{6,254},{7,255},{8,16},{... | collective-permute-start | bytes 110600 | tf_op jit(solution)/shard_map/ppermute | solution.py:503
  26.7 0.4 shard_map.97
  27.1 7.7 %collective-permute-done.7.got2_ref = f32[72,128]{1,0:T(8,128)S(1)} collective-permute-done((f32[72,128]{1,0:T(8,128)S(1)}, f32[72,128]{1,0:T(8,128)S(1)}, u32[]{:S(2)}, u32[]{:S(2)}) %collective-permute-start.7) | collective-permute-done | bytes 36896 | tf_op jit(solution)/shard_map/ppermute | solution.py:503
  34.8 0.0 collective-permute-done.6.got1_ref
  34.8 0.3 shard_map.98
  35.1 1.2 %collective-permute-start.8 = (f32[2,32,128]{2,1,0:T(8,128)S(1)}, f32[2,32,128]{2,1,0:T(8,128)S(1)}, u32[]{:S(2)}, u32[]{:S(2)}) collective-permute-start(f32[2,32,128]{2,1,0:T(8,128)S(1)} %get-tuple-element.25), channel_id=1, source_target_pairs={{0,2},{1,3},{2,0},{3,1},{4,6},{5,7},{6,4},{7,5},{8,10},{9,11},{10,... | collective-permute-start | bytes 98312 | tf_op jit(solution)/shard_map/ppermute | solution.py:443
  36.3 0.9 %shard_map.99 = (f32[144,128]{1,0:T(8,128)}, f32[48,48]{1,0:T(8,128)S(1)}) custom-call(f32[2,32,128]{2,1,0:T(8,128)S(1)} %get-tuple-element.21.after_ref.near_ref, f32[4,144,128]{2,1,0:T(8,128)S(1)} %get-tuple-element.15.y2_ref, f32[4,144,128]{2,1,0:T(8,128)S(1)} %get-tuple-element.22.w_ref, f32[48,48]{1,0:T(8,128)S(1)} %get-tuple-element.16.linv_ref), custom_call_target="tpu_custom_call" | custom-call | tf_op jit(solution)/shard_map/pallas_call | solution.py:525
  37.2 0.7 %collective-permute-done.8.far_ref = f32[2,32,128]{2,1,0:T(8,128)S(1)} collective-permute-done((f32[2,32,128]{2,1,0:T(8,128)S(1)}, f32[2,32,128]{2,1,0:T(8,128)S(1)}, u32[]{:S(2)}, u32[]{:S(2)}) %collective-permute-start.8) | collective-permute-done | bytes 32800 | tf_op jit(solution)/shard_map/ppermute | solution.py:443
  38.0 2.5 %collective-permute-start.9 = (f32[2,32,128]{2,1,0:T(8,128)S(1)}, f32[2,32,128]{2,1,0:T(8,128)S(1)}, u32[]{:S(2)}, u32[]{:S(2)}) collective-permute-start(f32[2,32,128]{2,1,0:T(8,128)S(1)} %shard_map.100), channel_id=1, source_target_pairs={{0,1},{1,0},{2,3},{3,2},{4,5},{5,4},{6,7},{7,6},{8,9},{9,8},{10,11... | collective-permute-start | bytes 98312 | tf_op jit(solution)/shard_map/ppermute | solution.py:443
  40.5 0.9 %collective-permute-done.9.on_ref = f32[2,32,128]{2,1,0:T(8,128)S(1)} collective-permute-done((f32[2,32,128]{2,1,0:T(8,128)S(1)}, f32[2,32,128]{2,1,0:T(8,128)S(1)}, u32[]{:S(2)}, u32[]{:S(2)}) %collective-permute-start.9) | collective-permute-done | bytes 32800 | tf_op jit(solution)/shard_map/ppermute | solution.py:443
  41.3 0.7 %shard_map.101 = f32[84,1,48]{2,1,0:T(1,128)} custom-call(s32[1]{0:T(128)} %bitcast.c_ref, f32[48,48]{1,0:T(8,128)S(1)} %get-tuple-element.24.after_ref.center_ref, f32[2,32,128]{2,1,0:T(8,128)S(1)} %get-tuple-element.21.after_ref.near_ref, f32[2,32,128]{2,1,0:T(8,128)S(1)} %collective-permute-done.8.far_ref, f32[2,32,128]{2,1,0:T(8,128)S(1)} %collective-permute-done.9.on_ref), custom_call_target="tpu_custom_call" | custom-call | tf_op jit(solution)/shard_map/pallas_call | solution.py:537
  (1 shorter events, 0.0 us)
Async XLA Ops:
  0.6 3.3 %copy-start = (f32[1,9,27,128]{3,0,2,1:T(1,128)S(1)}, f32[1,9,27,128]{3,0,2,1:T(1,128)}, u32[]{:S(2)}) copy-start(f32[1,9,27,128]{3,0,2,1:T(1,128)} %param.9) | copy-start | bytes 373252
  0.6 6.4 %collective-permute-start.4 = (f32[243,1,128]{2,1,0:T(1,128)}, f32[243,1,128]{2,1,0:T(1,128)S(1)}, u32[]{:S(2)}, u32[]{:S(2)}) collective-permute-start(f32[243,1,128]{2,1,0:T(1,128)} %bitcast.18), channel_id=1, source_target_pairs={{0,2},{1,3},{2,0},{3,1},{4,6},{5,7},{6,4},{7,5},{8,10},{9,11},{10,... | collective-permute-start | bytes 373256 | tf_op jit(solution)/shard_map/ppermute | solution.py:443
  3.8 5.6 %collective-permute-start.1 = (f32[192,128]{1,0:T(8,128)S(1)}, f32[192,128]{1,0:T(8,128)S(1)}, u32[]{:S(2)}, u32[]{:S(2)}) collective-permute-start(f32[192,128]{1,0:T(8,128)S(1)} %shard_map.95.p0), channel_id=1, source_target_pairs={{0,2},{1,3},{2,0},{3,1},{4,6},{5,7},{6,4},{7,5},{8,10},{9,11},{10,... | collective-permute-start | bytes 294920 | tf_op jit(solution)/shard_map/ppermute | solution.py:443
  3.9 6.8 %collective-permute-start.3 = (f32[243,1,128]{2,1,0:T(1,128)S(1)}, f32[243,1,128]{2,1,0:T(1,128)S(1)}, u32[]{:S(2)}, u32[]{:S(2)}) collective-permute-start(f32[243,1,128]{2,1,0:T(1,128)S(1)} %bitcast.19), channel_id=1, source_target_pairs={{0,1},{1,0},{2,3},{3,2},{4,5},{5,4},{6,7},{7,6},{8,9},{9,8},{10,11... | collective-permute-start | bytes 373256 | tf_op jit(solution)/shard_map/ppermute | solution.py:443
  7.1 4.3 %collective-permute-start.5 = (f32[243,1,128]{2,1,0:T(1,128)S(1)}, f32[243,1,128]{2,1,0:T(1,128)S(1)}, u32[]{:S(2)}, u32[]{:S(2)}) collective-permute-start(f32[243,1,128]{2,1,0:T(1,128)S(1)} %collective-permute-done.4.v2), channel_id=1, source_target_pairs={{0,1},{1,0},{2,3},{3,2},{4,5},{5,4},{6,7},{7,6},{8,9},{9,8},{10,11... | collective-permute-start | bytes 373256 | tf_op jit(solution)/shard_map/ppermute | solution.py:443
  9.4 1.3 %collective-permute-start = (f32[192,128]{1,0:T(8,128)S(1)}, f32[192,128]{1,0:T(8,128)S(1)}, u32[]{:S(2)}, u32[]{:S(2)}) collective-permute-start(f32[192,128]{1,0:T(8,128)S(1)} %shard_map.95.p0), channel_id=1, source_target_pairs={{0,1},{1,0},{2,3},{3,2},{4,5},{5,4},{6,7},{7,6},{8,9},{9,8},{10,11... | collective-permute-start | bytes 294920 | tf_op jit(solution)/shard_map/ppermute | solution.py:443
  9.4 2.0 %collective-permute-start.2 = (f32[192,128]{1,0:T(8,128)S(1)}, f32[192,128]{1,0:T(8,128)S(1)}, u32[]{:S(2)}, u32[]{:S(2)}) collective-permute-start(f32[192,128]{1,0:T(8,128)S(1)} %collective-permute-done.1.p2), channel_id=1, source_target_pairs={{0,1},{1,0},{2,3},{3,2},{4,5},{5,4},{6,7},{7,6},{8,9},{9,8},{10,11... | collective-permute-start | bytes 294920 | tf_op jit(solution)/shard_map/ppermute | solution.py:443
  23.7 11.1 %collective-permute-start.6 = (f32[144,128]{1,0:T(8,128)S(1)}, f32[144,128]{1,0:T(8,128)S(1)}, u32[]{:S(2)}, u32[]{:S(2)}) collective-permute-start(f32[144,128]{1,0:T(8,128)S(1)} %get-tuple-element.19), channel_id=1, source_target_pairs={{0,14},{1,7},{2,244},{3,253},{4,18},{5,11},{6,248},{7,1},{8,22},{9... | collective-permute-start | bytes 221192 | tf_op jit(solution)/shard_map/ppermute | solution.py:503
  25.4 9.4 %collective-permute-start.7 = (f32[72,128]{1,0:T(8,128)S(1)}, f32[72,128]{1,0:T(8,128)S(1)}, u32[]{:S(2)}, u32[]{:S(2)}) collective-permute-start(f32[72,128]{1,0:T(8,128)S(1)} %get-tuple-element.20), channel_id=1, source_target_pairs={{0,8},{1,9},{2,250},{3,251},{4,12},{5,13},{6,254},{7,255},{8,16},{... | collective-permute-start | bytes 110600 | tf_op jit(solution)/shard_map/ppermute | solution.py:503
  35.1 2.9 %collective-permute-start.8 = (f32[2,32,128]{2,1,0:T(8,128)S(1)}, f32[2,32,128]{2,1,0:T(8,128)S(1)}, u32[]{:S(2)}, u32[]{:S(2)}) collective-permute-start(f32[2,32,128]{2,1,0:T(8,128)S(1)} %get-tuple-element.25), channel_id=1, source_target_pairs={{0,2},{1,3},{2,0},{3,1},{4,6},{5,7},{6,4},{7,5},{8,10},{9,11},{10,... | collective-permute-start | bytes 98312 | tf_op jit(solution)/shard_map/ppermute | solution.py:443
  38.0 3.4 %collective-permute-start.9 = (f32[2,32,128]{2,1,0:T(8,128)S(1)}, f32[2,32,128]{2,1,0:T(8,128)S(1)}, u32[]{:S(2)}, u32[]{:S(2)}) collective-permute-start(f32[2,32,128]{2,1,0:T(8,128)S(1)} %shard_map.100), channel_id=1, source_target_pairs={{0,1},{1,0},{2,3},{3,2},{4,5},{5,4},{6,7},{7,6},{8,9},{9,8},{10,11... | collective-permute-start | bytes 98312 | tf_op jit(solution)/shard_map/ppermute | solution.py:443

commit v8 on v7

--- a/solution.py
+++ b/solution.py
@@ -96,7 +96,7 @@
                 dst_ref[q, rows, :] = piv * src_ref[q, rows, :]
 
 
-ONE = 16
+ONE = 14
 BF16 = jnp.bfloat16
 
 
@@ -231,7 +231,7 @@
     )
 
 
-CHOL = 3
+CHOL = 4
 
 
 def factor_piece(m_ref, col_ref, j):
@@ -322,15 +322,16 @@
         sum_ref[...] = jnp.zeros((NC, 3 * V, LANES), F32)
         issue(x_ref, oh_ref, t_ref, 0, 0)
 
+        groups = [(rc, range(n, min(n + 4, NB))) for rc in range(NC) for n in range(ONE, NB, 4)]
         for k in range(ONE):
             if k + 1 < ONE:
                 issue(x_ref, oh_ref, t_ref, k + 1, (k + 1) % 2)
-            ks = [n for n in range(ONE + 3 * (k % 4), ONE + 3 * (k % 4) + 3) if n < NB]
-            lane_blocks(val_ref, cols_ref, pair_ref, sum_ref, k // 4, ks)
+            for rc, ks in groups[k * len(groups) // ONE : (k + 1) * len(groups) // ONE]:
+                lane_blocks(val_ref, cols_ref, pair_ref, sum_ref, rc, ks)
             if first:
                 if k + 2 < ONE:
                     one_hot(cols_ref, oh_ref, k + 2)
-            else:
+            elif k * CHOL < V:
                 factor_piece(m_ref, col_ref, k * CHOL)
             take(val_ref, dst_ref, t_ref, k, k % 2)
         for q in range(NC):
@@ -459,9 +460,10 @@
         recv_rows.reshape(SLOTS, 1, OVD),
     )
     far_p = pass_on(packed, 2)
-    blocks = []
-    for own, far in ((packed, far_p), (values, far_v)):
-        blocks += [own, pass_on(own, 1), far, pass_on(far, 1)]
+    near_v = pass_on(values, 1)
+    near_p = pass_on(packed, 1)
+    far_v, near_p = lax.optimization_barrier((far_v, near_p))
+    blocks = [packed, near_p, far_p, pass_on(far_p, 1), values, near_v, far_v, pass_on(far_v, 1)]
     block = (NC, 3 * V, LANES)
     y2, w, linv, s1, s2, row = pl.pallas_call(
         main_kernel,

time: 42.1 us -> 42 us (level)
  waiting for transfers between devices: 10.2 us -> 10.7 us
    ppermute x2, starting transfers between devices: 3.06 us -> 2.35 us  [across(): return lax.ppermute(piece, ('sub', 'crow'), pairs)]
    ppermute x8, starting transfers between devices: 12.4 us -> 12.9 us  [pass_on(): return lax.ppermute(piece, 'crow', [(n, n ^ m) for n in range(NC)])]
where the time goes in v8:
time: 42 us; the launch traced here: 41.9 us
  Pallas kernels  15.4 us (37%)
  starting transfers between devices  15.2 us (36%)
  waiting for transfers between devices  10.7 us (25%)
  between operations  0.67 us (2%)
    ppermute x8, starting transfers between devices, pass_on(): return lax.ppermute(piece, 'crow', [(n, n ^ m) for n in range(NC)])  12.9 us
    pallas_call x1, Pallas kernels, shards(): pl.pallas_call(main_kernel, out_shape=(shape(block, F32), shape(block, F3...  12 us
    ppermute x2, waiting for transfers between devices, across(): return lax.ppermute(piece, ('sub', 'crow'), pairs)  7.69 us
    ppermute x8, waiting for transfers between devices, pass_on(): return lax.ppermute(piece, 'crow', [(n, n ^ m) for n in range(NC)])  2.96 us
    ppermute x2, starting transfers between devices, across(): return lax.ppermute(piece, ('sub', 'crow'), pairs)  2.35 us
    pallas_call x1, Pallas kernels, shards(): pl.pallas_call(pack_kernel, out_shape=shape((PACKED, LANES), F32), in_spe...  1.03 us
    pallas_call x1, Pallas kernels, shards(): pl.pallas_call(basis_kernel, out_shape=(jax.ShapeDtypeStruct((3 * V, LANE...  0.9 us
  transfers between devices with their start and end apart: 10, of which 5 were waited for; matrix products, arithmetic and copies ran while one was open for 0% of the time, Pallas kernels for 6%

profile of v8, /device:TPU:1, one launch (start us, length us, event | category | flops | bytes accessed | tf_op | source)
XLA Modules:
  0.0 41.9 jit_solution(6875226913862263075)
XLA Ops:
  0.6 0.0 copy-start
  0.6 2.1 %collective-permute-start = (f32[243,1,128]{2,1,0:T(1,128)}, f32[243,1,128]{2,1,0:T(1,128)S(1)}, u32[]{:S(2)}, u32[]{:S(2)}) collective-permute-start(f32[243,1,128]{2,1,0:T(1,128)} %bitcast.18), channel_id=1, source_target_pairs={{0,2},{1,3},{2,0},{3,1},{4,6},{5,7},{6,4},{7,5},{8,10},{9,11},{10,... | collective-permute-start | bytes 373256 | tf_op jit(solution)/shard_map/ppermute | solution.py:444
  2.8 1.0 %shard_map.95.p0 = f32[192,128]{1,0:T(8,128)S(1)} custom-call(s32[1]{0:T(128)} %bitcast.c_ref, s32[6]{0:T(128)} %bitcast.27, f32[144,128]{1,0:T(8,128)} %bitcast.21, s32[27,1,128]{2,1,0:T(1,128)} %bitcast.23, s32[1,128]{1,0:T(1,128)} %cnt_ref.1, f32[3,1,128]{2,1,0:T(1,128)} %bitcast.26, s32[6,1,32]{2,1,0:T(1,128)} %bitcast.24, s32[6,1,32]{2,1,0:T(1,128)} %bitcast.25), custom_call_target="tpu_custom_call" | custom-call | tf_op jit(solution)/shard_map/pallas_call | solution.py:447
  3.8 1.3 %collective-permute-start.1 = (f32[192,128]{1,0:T(8,128)S(1)}, f32[192,128]{1,0:T(8,128)S(1)}, u32[]{:S(2)}, u32[]{:S(2)}) collective-permute-start(f32[192,128]{1,0:T(8,128)S(1)} %shard_map.95.p0), channel_id=1, source_target_pairs={{0,1},{1,0},{2,3},{3,2},{4,5},{5,4},{6,7},{7,6},{8,9},{9,8},{10,11... | collective-permute-start | bytes 294920 | tf_op jit(solution)/shard_map/ppermute | solution.py:444
  5.1 1.7 %collective-permute-start.2 = (f32[192,128]{1,0:T(8,128)S(1)}, f32[192,128]{1,0:T(8,128)S(1)}, u32[]{:S(2)}, u32[]{:S(2)}) collective-permute-start(f32[192,128]{1,0:T(8,128)S(1)} %shard_map.95.p0), channel_id=1, source_target_pairs={{0,2},{1,3},{2,0},{3,1},{4,6},{5,7},{6,4},{7,5},{8,10},{9,11},{10,... | collective-permute-start | bytes 294920 | tf_op jit(solution)/shard_map/ppermute | solution.py:444
  6.8 0.0 copy-done
  6.8 0.4 collective-permute-start.4
  7.2 0.0 collective-permute-done.1.p1
  7.2 0.0 collective-permute-done.v2
  7.2 2.4 %collective-permute-start.5 = (f32[243,1,128]{2,1,0:T(1,128)S(1)}, f32[243,1,128]{2,1,0:T(1,128)S(1)}, u32[]{:S(2)}, u32[]{:S(2)}) collective-permute-start(f32[243,1,128]{2,1,0:T(1,128)S(1)} %collective-permute-done.v2), channel_id=1, source_target_pairs={{0,1},{1,0},{2,3},{3,2},{4,5},{5,4},{6,7},{7,6},{8,9},{9,8},{10,11... | collective-permute-start | bytes 373256 | tf_op jit(solution)/shard_map/ppermute | solution.py:444
  9.6 0.5 %collective-permute-done.2.p2 = f32[192,128]{1,0:T(8,128)S(1)} collective-permute-done((f32[192,128]{1,0:T(8,128)S(1)}, f32[192,128]{1,0:T(8,128)S(1)}, u32[]{:S(2)}, u32[]{:S(2)}) %collective-permute-start.2) | collective-permute-done | bytes 98336 | tf_op jit(solution)/shard_map/ppermute | solution.py:444
  10.2 1.0 %collective-permute-start.3 = (f32[192,128]{1,0:T(8,128)S(1)}, f32[192,128]{1,0:T(8,128)S(1)}, u32[]{:S(2)}, u32[]{:S(2)}) collective-permute-start(f32[192,128]{1,0:T(8,128)S(1)} %collective-permute-done.2.p2), channel_id=1, source_target_pairs={{0,1},{1,0},{2,3},{3,2},{4,5},{5,4},{6,7},{7,6},{8,9},{9,8},{10,11... | collective-permute-start | bytes 294920 | tf_op jit(solution)/shard_map/ppermute | solution.py:444
  11.1 0.0 collective-permute-done.4.v1
  11.1 0.9 %collective-permute-done.3.p3 = f32[192,128]{1,0:T(8,128)S(1)} collective-permute-done((f32[192,128]{1,0:T(8,128)S(1)}, f32[192,128]{1,0:T(8,128)S(1)}, u32[]{:S(2)}, u32[]{:S(2)}) %collective-permute-start.3) | collective-permute-done | bytes 98336 | tf_op jit(solution)/shard_map/ppermute | solution.py:444
  12.1 0.0 collective-permute-done.5.v3
  12.1 12.0 %shard_map.96 = (f32[4,144,128]{2,1,0:T(8,128)S(1)}, f32[4,144,128]{2,1,0:T(8,128)S(1)}, f32[48,48]{1,0:T(8,128)S(1)}, f32[144,128]{1,0:T(8,128)S(1)}, f32[72,128]{1,0:T(8,128)S(1)}, /*index=5*/f32[8,128]{1,0:T(8,128)S(1)}) custom-call(s32[1]{0:T(128)} %bitcast.c_ref, f32[192,128]{1,0:T(8,128)S(1)} %shard_map.95.p0, ...), custom_call_target="tpu_custom_call" | custom-call | tf_op jit(solution)/shard_map/pallas_call | solution.py:468
  24.1 1.1 %collective-permute-start.6 = (f32[144,128]{1,0:T(8,128)S(1)}, f32[144,128]{1,0:T(8,128)S(1)}, u32[]{:S(2)}, u32[]{:S(2)}) collective-permute-start(f32[144,128]{1,0:T(8,128)S(1)} %get-tuple-element.23), channel_id=1, source_target_pairs={{0,14},{1,7},{2,244},{3,253},{4,18},{5,11},{6,248},{7,1},{8,22},{9... | collective-permute-start | bytes 221192 | tf_op jit(solution)/shard_map/ppermute | solution.py:505
  25.2 1.3 %collective-permute-start.7 = (f32[72,128]{1,0:T(8,128)S(1)}, f32[72,128]{1,0:T(8,128)S(1)}, u32[]{:S(2)}, u32[]{:S(2)}) collective-permute-start(f32[72,128]{1,0:T(8,128)S(1)} %get-tuple-element.24), channel_id=1, source_target_pairs={{0,8},{1,9},{2,250},{3,251},{4,12},{5,13},{6,254},{7,255},{8,16},{... | collective-permute-start | bytes 110600 | tf_op jit(solution)/shard_map/ppermute | solution.py:505
  26.5 0.4 shard_map.97
  26.9 7.7 %collective-permute-done.7.got2_ref = f32[72,128]{1,0:T(8,128)S(1)} collective-permute-done((f32[72,128]{1,0:T(8,128)S(1)}, f32[72,128]{1,0:T(8,128)S(1)}, u32[]{:S(2)}, u32[]{:S(2)}) %collective-permute-start.7) | collective-permute-done | bytes 36896 | tf_op jit(solution)/shard_map/ppermute | solution.py:505
  34.6 0.0 collective-permute-done.6.got1_ref
  34.6 0.3 shard_map.98
  34.9 1.3 %collective-permute-start.8 = (f32[2,32,128]{2,1,0:T(8,128)S(1)}, f32[2,32,128]{2,1,0:T(8,128)S(1)}, u32[]{:S(2)}, u32[]{:S(2)}) collective-permute-start(f32[2,32,128]{2,1,0:T(8,128)S(1)} %get-tuple-element.29), channel_id=1, source_target_pairs={{0,2},{1,3},{2,0},{3,1},{4,6},{5,7},{6,4},{7,5},{8,10},{9,11},{10,... | collective-permute-start | bytes 98312 | tf_op jit(solution)/shard_map/ppermute | solution.py:444
  36.2 0.9 %shard_map.99 = (f32[144,128]{1,0:T(8,128)}, f32[48,48]{1,0:T(8,128)S(1)}) custom-call(f32[2,32,128]{2,1,0:T(8,128)S(1)} %get-tuple-element.25.after_ref.near_ref, f32[4,144,128]{2,1,0:T(8,128)S(1)} %get-tuple-element.19.y2_ref, f32[4,144,128]{2,1,0:T(8,128)S(1)} %get-tuple-element.26.w_ref, f32[48,48]{1,0:T(8,128)S(1)} %get-tuple-element.20.linv_ref), custom_call_target="tpu_custom_call" | custom-call | tf_op jit(solution)/shard_map/pallas_call | solution.py:527
  37.1 0.6 %collective-permute-done.8.far_ref = f32[2,32,128]{2,1,0:T(8,128)S(1)} collective-permute-done((f32[2,32,128]{2,1,0:T(8,128)S(1)}, f32[2,32,128]{2,1,0:T(8,128)S(1)}, u32[]{:S(2)}, u32[]{:S(2)}) %collective-permute-start.8) | collective-permute-done | bytes 32800 | tf_op jit(solution)/shard_map/ppermute | solution.py:444
  37.7 2.6 %collective-permute-start.9 = (f32[2,32,128]{2,1,0:T(8,128)S(1)}, f32[2,32,128]{2,1,0:T(8,128)S(1)}, u32[]{:S(2)}, u32[]{:S(2)}) collective-permute-start(f32[2,32,128]{2,1,0:T(8,128)S(1)} %shard_map.100), channel_id=1, source_target_pairs={{0,1},{1,0},{2,3},{3,2},{4,5},{5,4},{6,7},{7,6},{8,9},{9,8},{10,11... | collective-permute-start | bytes 98312 | tf_op jit(solution)/shard_map/ppermute | solution.py:444
  40.3 0.9 %collective-permute-done.9.on_ref = f32[2,32,128]{2,1,0:T(8,128)S(1)} collective-permute-done((f32[2,32,128]{2,1,0:T(8,128)S(1)}, f32[2,32,128]{2,1,0:T(8,128)S(1)}, u32[]{:S(2)}, u32[]{:S(2)}) %collective-permute-start.9) | collective-permute-done | bytes 32800 | tf_op jit(solution)/shard_map/ppermute | solution.py:444
  41.2 0.7 %shard_map.101 = f32[84,1,48]{2,1,0:T(1,128)} custom-call(s32[1]{0:T(128)} %bitcast.c_ref, f32[48,48]{1,0:T(8,128)S(1)} %get-tuple-element.28.after_ref.center_ref, f32[2,32,128]{2,1,0:T(8,128)S(1)} %get-tuple-element.25.after_ref.near_ref, f32[2,32,128]{2,1,0:T(8,128)S(1)} %collective-permute-done.8.far_ref, f32[2,32,128]{2,1,0:T(8,128)S(1)} %collective-permute-done.9.on_ref), custom_call_target="tpu_custom_call" | custom-call | tf_op jit(solution)/shard_map/pallas_call | solution.py:539
  (1 shorter events, 0.0 us)
Async XLA Ops:
  0.6 6.2 %copy-start = (f32[1,9,27,128]{3,0,2,1:T(1,128)S(1)}, f32[1,9,27,128]{3,0,2,1:T(1,128)}, u32[]{:S(2)}) copy-start(f32[1,9,27,128]{3,0,2,1:T(1,128)} %param.9) | copy-start | bytes 373252
  0.6 6.6 %collective-permute-start = (f32[243,1,128]{2,1,0:T(1,128)}, f32[243,1,128]{2,1,0:T(1,128)S(1)}, u32[]{:S(2)}, u32[]{:S(2)}) collective-permute-start(f32[243,1,128]{2,1,0:T(1,128)} %bitcast.18), channel_id=1, source_target_pairs={{0,2},{1,3},{2,0},{3,1},{4,6},{5,7},{6,4},{7,5},{8,10},{9,11},{10,... | collective-permute-start | bytes 373256 | tf_op jit(solution)/shard_map/ppermute | solution.py:444
  3.8 3.4 %collective-permute-start.1 = (f32[192,128]{1,0:T(8,128)S(1)}, f32[192,128]{1,0:T(8,128)S(1)}, u32[]{:S(2)}, u32[]{:S(2)}) collective-permute-start(f32[192,128]{1,0:T(8,128)S(1)} %shard_map.95.p0), channel_id=1, source_target_pairs={{0,1},{1,0},{2,3},{3,2},{4,5},{5,4},{6,7},{7,6},{8,9},{9,8},{10,11... | collective-permute-start | bytes 294920 | tf_op jit(solution)/shard_map/ppermute | solution.py:444
  5.1 5.1 %collective-permute-start.2 = (f32[192,128]{1,0:T(8,128)S(1)}, f32[192,128]{1,0:T(8,128)S(1)}, u32[]{:S(2)}, u32[]{:S(2)}) collective-permute-start(f32[192,128]{1,0:T(8,128)S(1)} %shard_map.95.p0), channel_id=1, source_target_pairs={{0,2},{1,3},{2,0},{3,1},{4,6},{5,7},{6,4},{7,5},{8,10},{9,11},{10,... | collective-permute-start | bytes 294920 | tf_op jit(solution)/shard_map/ppermute | solution.py:444
  6.8 4.3 %collective-permute-start.4 = (f32[243,1,128]{2,1,0:T(1,128)S(1)}, f32[243,1,128]{2,1,0:T(1,128)S(1)}, u32[]{:S(2)}, u32[]{:S(2)}) collective-permute-start(f32[243,1,128]{2,1,0:T(1,128)S(1)} %bitcast.19), channel_id=1, source_target_pairs={{0,1},{1,0},{2,3},{3,2},{4,5},{5,4},{6,7},{7,6},{8,9},{9,8},{10,11... | collective-permute-start | bytes 373256 | tf_op jit(solution)/shard_map/ppermute | solution.py:444
  7.2 4.9 %collective-permute-start.5 = (f32[243,1,128]{2,1,0:T(1,128)S(1)}, f32[243,1,128]{2,1,0:T(1,128)S(1)}, u32[]{:S(2)}, u32[]{:S(2)}) collective-permute-start(f32[243,1,128]{2,1,0:T(1,128)S(1)} %collective-permute-done.v2), channel_id=1, source_target_pairs={{0,1},{1,0},{2,3},{3,2},{4,5},{5,4},{6,7},{7,6},{8,9},{9,8},{10,11... | collective-permute-start | bytes 373256 | tf_op jit(solution)/shard_map/ppermute | solution.py:444
  10.2 1.9 %collective-permute-start.3 = (f32[192,128]{1,0:T(8,128)S(1)}, f32[192,128]{1,0:T(8,128)S(1)}, u32[]{:S(2)}, u32[]{:S(2)}) collective-permute-start(f32[192,128]{1,0:T(8,128)S(1)} %collective-permute-done.2.p2), channel_id=1, source_target_pairs={{0,1},{1,0},{2,3},{3,2},{4,5},{5,4},{6,7},{7,6},{8,9},{9,8},{10,11... | collective-permute-start | bytes 294920 | tf_op jit(solution)/shard_map/ppermute | solution.py:444
  24.1 10.4 %collective-permute-start.6 = (f32[144,128]{1,0:T(8,128)S(1)}, f32[144,128]{1,0:T(8,128)S(1)}, u32[]{:S(2)}, u32[]{:S(2)}) collective-permute-start(f32[144,128]{1,0:T(8,128)S(1)} %get-tuple-element.23), channel_id=1, source_target_pairs={{0,14},{1,7},{2,244},{3,253},{4,18},{5,11},{6,248},{7,1},{8,22},{9... | collective-permute-start | bytes 221192 | tf_op jit(solution)/shard_map/ppermute | solution.py:505
  25.2 9.4 %collective-permute-start.7 = (f32[72,128]{1,0:T(8,128)S(1)}, f32[72,128]{1,0:T(8,128)S(1)}, u32[]{:S(2)}, u32[]{:S(2)}) collective-permute-start(f32[72,128]{1,0:T(8,128)S(1)} %get-tuple-element.24), channel_id=1, source_target_pairs={{0,8},{1,9},{2,250},{3,251},{4,12},{5,13},{6,254},{7,255},{8,16},{... | collective-permute-start | bytes 110600 | tf_op jit(solution)/shard_map/ppermute | solution.py:505
  34.9 2.9 %collective-permute-start.8 = (f32[2,32,128]{2,1,0:T(8,128)S(1)}, f32[2,32,128]{2,1,0:T(8,128)S(1)}, u32[]{:S(2)}, u32[]{:S(2)}) collective-permute-start(f32[2,32,128]{2,1,0:T(8,128)S(1)} %get-tuple-element.29), channel_id=1, source_target_pairs={{0,2},{1,3},{2,0},{3,1},{4,6},{5,7},{6,4},{7,5},{8,10},{9,11},{10,... | collective-permute-start | bytes 98312 | tf_op jit(solution)/shard_map/ppermute | solution.py:444
  37.7 3.5 %collective-permute-start.9 = (f32[2,32,128]{2,1,0:T(8,128)S(1)}, f32[2,32,128]{2,1,0:T(8,128)S(1)}, u32[]{:S(2)}, u32[]{:S(2)}) collective-permute-start(f32[2,32,128]{2,1,0:T(8,128)S(1)} %shard_map.100), channel_id=1, source_target_pairs={{0,1},{1,0},{2,3},{3,2},{4,5},{5,4},{6,7},{7,6},{8,9},{9,8},{10,11... | collective-permute-start | bytes 98312 | tf_op jit(solution)/shard_map/ppermute | solution.py:444
